TPU v7x, 32 devices: a whole 2x2x4 slice. The times are simulated.
32 devices in a mesh: depth: 8 (over z, y), lat: 4 (over x, core).
Axes of the slice: x: 2, y: 2, z: 4, core: 2. Of those that a mesh axis runs over, the one named last changes fastest.
Arguments:
- sources: float32 [8, 2, 64, 4096], P('depth', None, None, 'lat'), may hold values from -6 to 6
- down_expand: float32 [8, 2, 64, 4096], P('depth', None, None, 'lat'), may hold values from -0.75 to 0.75
- down_project: float32 [8, 2, 64, 4096], P('depth', None, None, 'lat'), may hold values from -0.09375 to 0.09375
- up_expand: float32 [8, 2, 64, 4096], P('depth', None, None, 'lat'), may hold values from -0.75 to 0.75
- up_project: float32 [8, 2, 64, 4096], P('depth', None, None, 'lat'), may hold values from -0.09375 to 0.09375
- down_decay: float32 [8, 64], P('depth'), may hold values from 0.3 to 0.8
- up_decay: float32 [8, 64], P('depth'), may hold values from 0.3 to 0.8
- active_list: int32 [8, 64], P('depth'), may hold values from 0 to 63, each once within a row
- active_count: int32 [8], P('depth'), may hold values from 1 to 64
- incident_down: float32 [2, 64, 4096], P(None, None, 'lat'), may hold values from -6 to 6
- incident_up: float32 [2, 64, 4096], P(None, None, 'lat'), may hold values from -6 to 6
Outputs:
- field: float32 [8, 2, 64, 4096], P('depth', None, None, 'lat')
Inputs may be any that keep to these rules, and one draw needn't show every extreme that they name: Each row of active_list holds every source number once.
All inputs are finite; a program needn't handle non-finite values.
Results may differ from a plain program's by a relative error of at most 0.0003.
Values sent between devices are 32-bit elements; how exact they have to be, the bound alone decides.
No kernel may reach another device: no remote copies, remote signals or barrier semaphores. Data moves between devices by JAX's collectives and lax.ppermute only.
A program may use at most 64 MiB of HBM per device.

v0:
```python
import jax
import jax.numpy as jnp
from jax import lax
from jax.sharding import PartitionSpec as P


def passed_along(value, axis, steps):
    count = lax.axis_size(axis)
    first, last = (max(0, -steps), min(count, count - steps))
    return lax.ppermute(value, axis, [(source, source + steps) for source in range(first, last)])


def contract(left, right):
    hp = lax.Precision.HIGHEST
    dims = (((1,), (1,)), ((), ()))

    def prod(a, b):
        return lax.dot_general(a, b, dims, precision=hp, preferred_element_type=jnp.float32)

    real = prod(left[0], right[0]) - prod(left[1], right[1])
    imag = prod(left[0], right[1]) + prod(left[1], right[0])
    return jnp.stack([real, imag])


def expand(coef, basis):
    hp = lax.Precision.HIGHEST
    dims = (((0,), (0,)), ((), ()))

    def prod(a, b):
        return lax.dot_general(a, b, dims, precision=hp, preferred_element_type=jnp.float32)

    real = prod(coef[0], basis[0]) - prod(coef[1], basis[1])
    imag = prod(coef[0], basis[1]) + prod(coef[1], basis[0])
    return jnp.stack([real, imag])


def cmatmul(first, second):
    hp = lax.Precision.HIGHEST

    def prod(a, b):
        return jnp.dot(a, b, precision=hp, preferred_element_type=jnp.float32)

    real = prod(first[0], second[0]) - prod(first[1], second[1])
    imag = prod(first[0], second[1]) + prod(first[1], second[0])
    return jnp.stack([real, imag])


def body(
    sources,
    down_expand,
    down_project,
    up_expand,
    up_project,
    down_decay,
    up_decay,
    active_list,
    active_count,
    incident_down,
    incident_up,
):
    nsrc = sources.shape[2]
    nrank = down_expand.shape[2]
    places = jnp.arange(nsrc, dtype=jnp.int32)
    valid = (places < active_count[0]).astype(jnp.float32)
    hits = (active_list[0][:, None] == places[None, :]).astype(jnp.float32)
    mask = jnp.sum(valid[:, None] * hits, axis=0)
    local = sources[0] * mask[None, :, None]
    own_group = lax.axis_index("depth")
    at_top = own_group == 0
    at_bottom = own_group == lax.axis_size("depth") - 1
    ahead_proj = passed_along(down_project[0], "depth", -1)
    behind_proj = passed_along(up_project[0], "depth", 1)
    parts = (
        contract(ahead_proj, local),
        contract(ahead_proj, down_expand[0]),
        contract(behind_proj, local),
        contract(behind_proj, up_expand[0]),
        contract(down_project[0], incident_down),
        contract(up_project[0], incident_up),
    )
    summed = lax.psum((parts[0], parts[1], parts[2], parts[3], parts[4], parts[5]), "lat")
    down_offset, down_map = passed_along((summed[0], summed[1]), "depth", 1)
    up_offset, up_map = passed_along((summed[2], summed[3]), "depth", -1)
    down_offset = jnp.where(at_top, summed[4], down_offset)
    up_offset = jnp.where(at_bottom, summed[5], up_offset)
    down_scale = down_decay[0][None, :, None]
    up_scale = up_decay[0][None, :, None]
    down_offset = down_scale * down_offset
    down_map = down_scale * down_map
    up_offset = up_scale * up_offset
    up_map = up_scale * up_map

    def advance(step, carry):
        down_coef, up_coef = carry
        above = passed_along(down_coef, "depth", 1)
        below = passed_along(up_coef, "depth", -1)
        return (down_offset + cmatmul(down_map, above), up_offset + cmatmul(up_map, below))

    empty = jnp.zeros((2, nrank, nsrc), jnp.float32)
    down_coef, up_coef = lax.fori_loop(0, lax.axis_size("depth"), advance, (empty, empty))
    field = local + expand(down_coef, down_expand[0]) + expand(up_coef, up_expand[0])
    return field[None]


def solution(mesh):
    in_specs = (
        P("depth", None, None, "lat"),
        P("depth", None, None, "lat"),
        P("depth", None, None, "lat"),
        P("depth", None, None, "lat"),
        P("depth", None, None, "lat"),
        P("depth", None),
        P("depth", None),
        P("depth", None),
        P("depth"),
        P(None, None, "lat"),
        P(None, None, "lat"),
    )
    out_specs = P("depth", None, None, "lat")
    return jax.shard_map(body, mesh=mesh, in_specs=in_specs, out_specs=out_specs, check_vma=False)
```

profile of v0, /device:TPU:0, one launch (start us, length us, event | category | flops | bytes accessed | tf_op | source)
XLA Modules:
  0.0 189.7 jit_solution(10425299569381927790)
XLA Ops:
  6.5 5.1 %collective-permute-start.5 = (f32[2,64,1024]{2,1,0:T(8,128)}, f32[2,64,1024]{2,1,0:T(8,128)S(1)}, u32[]{:S(2)}, u32[]{:S(2)}) collective-permute-start(f32[2,64,1024]{2,1,0:T(8,128)} %bitcast.265), channel_id=1, source_target_pairs={{0,4},{4,8},{8,12},{12,16},{16,20},{20,24},{24,28},{1,5},{5,9},{9,... | collective-permute-start | bytes 1572872 | tf_op jit(solution)/shard_map/ppermute | solution.py:10
  11.6 1.4 collective-permute-start.2
  13.0 1.4 fusion.63
  14.5 1.4 fusion.69
  15.9 1.4 fusion.41
  20.9 13.4 %collective-permute-done.5 = f32[2,64,1024]{2,1,0:T(8,128)S(1)} collective-permute-done((f32[2,64,1024]{2,1,0:T(8,128)}, f32[2,64,1024]{2,1,0:T(8,128)S(1)}, u32[]{:S(2)}, u32[]{:S(2)}) %collective-permute-start.5) | collective-permute-done | bytes 524320 | tf_op jit(solution)/shard_map/ppermute | solution.py:10
  41.8 34.7 %all-reduce.3.cloned.1.call-done = (f32[2,64,64]{2,1,0:T(8,128)}, f32[2,64,64]{2,1,0:T(8,128)}, f32[2,64,64]{2,1,0:T(8,128)}, f32[2,64,64]{2,1,0:T(8,128)}, f32[2,64,64]{2,1,0:T(8,128)}, /*index=5*/f32[2,64,64]{2,1,0:T(8,128)}) async-done(((f32[2,64,64]{2,1,0:T(8,128)}, f32[2,64,64]{2,1,0:T(8,128)}, f32[2,64,64]{2,1,0:T(8,128)}, f32[2,64,64]{2,1,0:T(8,128)}, f32[2,64,64]{2,1,0:T(8,128)}, ...) | async-done | bytes 196624 | tf_op jit(solution)/shard_map/psum | solution.py:81
  76.5 3.4 %collective-permute-start.3 = (f32[2,64,64]{2,1,0:T(8,128)}, f32[2,64,64]{2,1,0:T(8,128)S(1)}, u32[]{:S(2)}, u32[]{:S(2)}) collective-permute-start(f32[2,64,64]{2,1,0:T(8,128)} %get-tuple-element.83), channel_id=1, source_target_pairs={{0,4},{4,8},{8,12},{12,16},{16,20},{20,24},{24,28},{1,5},{5,9},{9,... | collective-permute-start | bytes 98312 | tf_op jit(solution)/shard_map/ppermute | solution.py:10
  79.9 3.4 %collective-permute-start.4 = (f32[2,64,64]{2,1,0:T(8,128)}, f32[2,64,64]{2,1,0:T(8,128)S(1)}, u32[]{:S(2)}, u32[]{:S(2)}) collective-permute-start(f32[2,64,64]{2,1,0:T(8,128)} %get-tuple-element.85), channel_id=1, source_target_pairs={{0,4},{4,8},{8,12},{12,16},{16,20},{20,24},{24,28},{1,5},{5,9},{9,... | collective-permute-start | bytes 98312 | tf_op jit(solution)/shard_map/ppermute | solution.py:10
  83.3 1.3 collective-permute-start.6
  84.6 1.3 collective-permute-start.7
  87.5 2.1 %collective-permute-done.6 = f32[2,64,64]{2,1,0:T(8,128)S(1)} collective-permute-done((f32[2,64,64]{2,1,0:T(8,128)}, f32[2,64,64]{2,1,0:T(8,128)S(1)}, u32[]{:S(2)}, u32[]{:S(2)}) %collective-permute-start.6) | collective-permute-done | bytes 32800 | tf_op jit(solution)/shard_map/ppermute | solution.py:10
  89.7 1.9 %collective-permute-done.7 = f32[2,64,64]{2,1,0:T(8,128)S(1)} collective-permute-done((f32[2,64,64]{2,1,0:T(8,128)}, f32[2,64,64]{2,1,0:T(8,128)S(1)}, u32[]{:S(2)}, u32[]{:S(2)}) %collective-permute-start.7) | collective-permute-done | bytes 32800 | tf_op jit(solution)/shard_map/ppermute | solution.py:10
  92.3 86.2 %while.13 = (s32[]{:T(128)}, f32[2,64,64]{2,1,0:T(8,128)S(1)}, f32[2,64,64]{2,1,0:T(8,128)S(1)}, f32[2,64,64]{2,1,0:T(8,128)S(1)}, f32[2,64,64]{2,1,0:T(8,128)S(...) while((s32[]{:T(128)}, f32[2,64,64]{2,1,0:T(8,128)S(1)}, ...), condition=%wide.region_8.9_spmd.clone, body=%wide.region_7.8_spmd.clone.sunk | while | flops 25231364 | bytes 1376440 | solution.py:100
  92.4 4.8 %collective-permute-start = (f32[2,64,64]{2,1,0:T(8,128)S(1)}, f32[2,64,64]{2,1,0:T(8,128)S(1)}, u32[]{:S(2)}, u32[]{:S(2)}) collective-permute-start(f32[2,64,64]{2,1,0:T(8,128)S(1)} %broadcast_select_fusion.4), channel_id=1, source_target_pairs={{0,4},{4,8},{8,12},{12,16},{16,20},{20,24},{24,28},{1,5},{5,9},{9,... | collective-permute-start | bytes 98312 | tf_op jit(solution)/shard_map/while/body/eval_jaxpr/ppermute | solution.py:10
  100.4 3.0 %collective-permute-done.1 = f32[2,64,64]{2,1,0:T(8,128)S(1)} collective-permute-done((f32[2,64,64]{2,1,0:T(8,128)S(1)}, f32[2,64,64]{2,1,0:T(8,128)S(1)}, u32[]{:S(2)}, u32[]{:S(2)}) %collective-permute-start.1) | collective-permute-done | bytes 32800 | tf_op jit(solution)/shard_map/while/body/eval_jaxpr/ppermute | solution.py:10
  104.1 4.3 %collective-permute-start = (f32[2,64,64]{2,1,0:T(8,128)S(1)}, f32[2,64,64]{2,1,0:T(8,128)S(1)}, u32[]{:S(2)}, u32[]{:S(2)}) collective-permute-start(f32[2,64,64]{2,1,0:T(8,128)S(1)} %broadcast_select_fusion.4), channel_id=1, source_target_pairs={{0,4},{4,8},{8,12},{12,16},{16,20},{20,24},{24,28},{1,5},{5,9},{9,... | collective-permute-start | bytes 98312 | tf_op jit(solution)/shard_map/while/body/eval_jaxpr/ppermute | solution.py:10
  111.0 3.6 %collective-permute-done.1 = f32[2,64,64]{2,1,0:T(8,128)S(1)} collective-permute-done((f32[2,64,64]{2,1,0:T(8,128)S(1)}, f32[2,64,64]{2,1,0:T(8,128)S(1)}, u32[]{:S(2)}, u32[]{:S(2)}) %collective-permute-start.1) | collective-permute-done | bytes 32800 | tf_op jit(solution)/shard_map/while/body/eval_jaxpr/ppermute | solution.py:10
  115.3 3.4 %collective-permute-start = (f32[2,64,64]{2,1,0:T(8,128)S(1)}, f32[2,64,64]{2,1,0:T(8,128)S(1)}, u32[]{:S(2)}, u32[]{:S(2)}) collective-permute-start(f32[2,64,64]{2,1,0:T(8,128)S(1)} %broadcast_select_fusion.4), channel_id=1, source_target_pairs={{0,4},{4,8},{8,12},{12,16},{16,20},{20,24},{24,28},{1,5},{5,9},{9,... | collective-permute-start | bytes 98312 | tf_op jit(solution)/shard_map/while/body/eval_jaxpr/ppermute | solution.py:10
  121.3 3.6 %collective-permute-done.1 = f32[2,64,64]{2,1,0:T(8,128)S(1)} collective-permute-done((f32[2,64,64]{2,1,0:T(8,128)S(1)}, f32[2,64,64]{2,1,0:T(8,128)S(1)}, u32[]{:S(2)}, u32[]{:S(2)}) %collective-permute-start.1) | collective-permute-done | bytes 32800 | tf_op jit(solution)/shard_map/while/body/eval_jaxpr/ppermute | solution.py:10
  125.6 4.2 %collective-permute-start = (f32[2,64,64]{2,1,0:T(8,128)S(1)}, f32[2,64,64]{2,1,0:T(8,128)S(1)}, u32[]{:S(2)}, u32[]{:S(2)}) collective-permute-start(f32[2,64,64]{2,1,0:T(8,128)S(1)} %broadcast_select_fusion.4), channel_id=1, source_target_pairs={{0,4},{4,8},{8,12},{12,16},{16,20},{20,24},{24,28},{1,5},{5,9},{9,... | collective-permute-start | bytes 98312 | tf_op jit(solution)/shard_map/while/body/eval_jaxpr/ppermute | solution.py:10
  132.5 3.9 %collective-permute-done.1 = f32[2,64,64]{2,1,0:T(8,128)S(1)} collective-permute-done((f32[2,64,64]{2,1,0:T(8,128)S(1)}, f32[2,64,64]{2,1,0:T(8,128)S(1)}, u32[]{:S(2)}, u32[]{:S(2)}) %collective-permute-start.1) | collective-permute-done | bytes 32800 | tf_op jit(solution)/shard_map/while/body/eval_jaxpr/ppermute | solution.py:10
  137.1 3.5 %collective-permute-start = (f32[2,64,64]{2,1,0:T(8,128)S(1)}, f32[2,64,64]{2,1,0:T(8,128)S(1)}, u32[]{:S(2)}, u32[]{:S(2)}) collective-permute-start(f32[2,64,64]{2,1,0:T(8,128)S(1)} %broadcast_select_fusion.4), channel_id=1, source_target_pairs={{0,4},{4,8},{8,12},{12,16},{16,20},{20,24},{24,28},{1,5},{5,9},{9,... | collective-permute-start | bytes 98312 | tf_op jit(solution)/shard_map/while/body/eval_jaxpr/ppermute | solution.py:10
  143.2 3.5 %collective-permute-done.1 = f32[2,64,64]{2,1,0:T(8,128)S(1)} collective-permute-done((f32[2,64,64]{2,1,0:T(8,128)S(1)}, f32[2,64,64]{2,1,0:T(8,128)S(1)}, u32[]{:S(2)}, u32[]{:S(2)}) %collective-permute-start.1) | collective-permute-done | bytes 32800 | tf_op jit(solution)/shard_map/while/body/eval_jaxpr/ppermute | solution.py:10
  147.4 4.5 %collective-permute-start = (f32[2,64,64]{2,1,0:T(8,128)S(1)}, f32[2,64,64]{2,1,0:T(8,128)S(1)}, u32[]{:S(2)}, u32[]{:S(2)}) collective-permute-start(f32[2,64,64]{2,1,0:T(8,128)S(1)} %broadcast_select_fusion.4), channel_id=1, source_target_pairs={{0,4},{4,8},{8,12},{12,16},{16,20},{20,24},{24,28},{1,5},{5,9},{9,... | collective-permute-start | bytes 98312 | tf_op jit(solution)/shard_map/while/body/eval_jaxpr/ppermute | solution.py:10
  151.9 1.3 collective-permute-start.1
  155.1 3.0 %collective-permute-done.1 = f32[2,64,64]{2,1,0:T(8,128)S(1)} collective-permute-done((f32[2,64,64]{2,1,0:T(8,128)S(1)}, f32[2,64,64]{2,1,0:T(8,128)S(1)}, u32[]{:S(2)}, u32[]{:S(2)}) %collective-permute-start.1) | collective-permute-done | bytes 32800 | tf_op jit(solution)/shard_map/while/body/eval_jaxpr/ppermute | solution.py:10
  158.8 3.1 %collective-permute-start = (f32[2,64,64]{2,1,0:T(8,128)S(1)}, f32[2,64,64]{2,1,0:T(8,128)S(1)}, u32[]{:S(2)}, u32[]{:S(2)}) collective-permute-start(f32[2,64,64]{2,1,0:T(8,128)S(1)} %broadcast_select_fusion.4), channel_id=1, source_target_pairs={{0,4},{4,8},{8,12},{12,16},{16,20},{20,24},{24,28},{1,5},{5,9},{9,... | collective-permute-start | bytes 98312 | tf_op jit(solution)/shard_map/while/body/eval_jaxpr/ppermute | solution.py:10
  161.9 1.3 collective-permute-start.1
  164.8 3.2 %collective-permute-done.1 = f32[2,64,64]{2,1,0:T(8,128)S(1)} collective-permute-done((f32[2,64,64]{2,1,0:T(8,128)S(1)}, f32[2,64,64]{2,1,0:T(8,128)S(1)}, u32[]{:S(2)}, u32[]{:S(2)}) %collective-permute-start.1) | collective-permute-done | bytes 32800 | tf_op jit(solution)/shard_map/while/body/eval_jaxpr/ppermute | solution.py:10
  168.8 2.8 %collective-permute-start = (f32[2,64,64]{2,1,0:T(8,128)S(1)}, f32[2,64,64]{2,1,0:T(8,128)S(1)}, u32[]{:S(2)}, u32[]{:S(2)}) collective-permute-start(f32[2,64,64]{2,1,0:T(8,128)S(1)} %broadcast_select_fusion.4), channel_id=1, source_target_pairs={{0,4},{4,8},{8,12},{12,16},{16,20},{20,24},{24,28},{1,5},{5,9},{9,... | collective-permute-start | bytes 98312 | tf_op jit(solution)/shard_map/while/body/eval_jaxpr/ppermute | solution.py:10
  174.2 3.6 %collective-permute-done.1 = f32[2,64,64]{2,1,0:T(8,128)S(1)} collective-permute-done((f32[2,64,64]{2,1,0:T(8,128)S(1)}, f32[2,64,64]{2,1,0:T(8,128)S(1)}, u32[]{:S(2)}, u32[]{:S(2)}) %collective-permute-start.1) | collective-permute-done | bytes 32800 | tf_op jit(solution)/shard_map/while/body/eval_jaxpr/ppermute | solution.py:10
  (177 shorter events, 41.6 us)
Async XLA Ops:
  6.5 7.9 %copy-start.3 = (f32[2,64,1024]{2,1,0:T(8,128)S(1)}, f32[2,64,1024]{2,1,0:T(8,128)}, u32[]{:S(2)}) copy-start(f32[2,64,1024]{2,1,0:T(8,128)} %param.22) | copy-start | bytes 1572868
  6.5 70.0 %all-reduce.3.cloned.1.call-start = ((), (), s32[]{:S(2)}) async-start(), calls=%async_computation | async-start | bytes 786432 | tf_op jit(solution)/shard_map/psum | solution.py:81
  6.5 27.7 %collective-permute-start.5 = (f32[2,64,1024]{2,1,0:T(8,128)}, f32[2,64,1024]{2,1,0:T(8,128)S(1)}, u32[]{:S(2)}, u32[]{:S(2)}) collective-permute-start(f32[2,64,1024]{2,1,0:T(8,128)} %bitcast.265), channel_id=1, source_target_pairs={{0,4},{4,8},{8,12},{12,16},{16,20},{20,24},{24,28},{1,5},{5,9},{9,... | collective-permute-start | bytes 1572872 | tf_op jit(solution)/shard_map/ppermute | solution.py:10
  11.6 4.2 %copy-start.4 = (f32[2,64,1024]{2,1,0:T(8,128)S(1)}, f32[2,64,1024]{2,1,0:T(8,128)}, u32[]{:S(2)}) copy-start(f32[2,64,1024]{2,1,0:T(8,128)} %param.23) | copy-start | bytes 1572868
  11.6 26.3 %collective-permute-start.2 = (f32[2,64,1024]{2,1,0:T(8,128)}, f32[2,64,1024]{2,1,0:T(8,128)S(1)}, u32[]{:S(2)}, u32[]{:S(2)}) collective-permute-start(f32[2,64,1024]{2,1,0:T(8,128)} %bitcast.266), channel_id=1, source_target_pairs={{4,0},{8,4},{12,8},{16,12},{20,16},{24,20},{28,24},{5,1},{9,5},{13... | collective-permute-start | bytes 1572872 | tf_op jit(solution)/shard_map/ppermute | solution.py:10
  14.4 2.8 %copy-start.5 = (f32[1,2,64,1024]{3,2,1,0:T(8,128)S(1)}, f32[1,2,64,1024]{3,2,1,0:T(8,128)}, u32[]{:S(2)}) copy-start(f32[1,2,64,1024]{3,2,1,0:T(8,128)} %param.17) | copy-start | bytes 1572868
  15.8 2.4 %copy-start.6 = (f32[1,2,64,1024]{3,2,1,0:T(8,128)S(1)}, f32[1,2,64,1024]{3,2,1,0:T(8,128)}, u32[]{:S(2)}) copy-start(f32[1,2,64,1024]{3,2,1,0:T(8,128)} %param.15) | copy-start | bytes 1572868
  19.0 0.7 copy-start.10
  19.4 1.4 copy-start.2
  20.9 14.1 %copy-start = (f32[1,2,64,1024]{3,2,1,0:T(8,128)S(1)}, f32[1,2,64,1024]{3,2,1,0:T(8,128)}, u32[]{:S(2)}) copy-start(f32[1,2,64,1024]{3,2,1,0:T(8,128)} %param.16) | copy-start | bytes 1572868
  37.9 1.0 copy-start.1
  76.5 9.4 %collective-permute-start.3 = (f32[2,64,64]{2,1,0:T(8,128)}, f32[2,64,64]{2,1,0:T(8,128)S(1)}, u32[]{:S(2)}, u32[]{:S(2)}) collective-permute-start(f32[2,64,64]{2,1,0:T(8,128)} %get-tuple-element.83), channel_id=1, source_target_pairs={{0,4},{4,8},{8,12},{12,16},{16,20},{20,24},{24,28},{1,5},{5,9},{9,... | collective-permute-start | bytes 98312 | tf_op jit(solution)/shard_map/ppermute | solution.py:10
  79.9 6.0 %collective-permute-start.4 = (f32[2,64,64]{2,1,0:T(8,128)}, f32[2,64,64]{2,1,0:T(8,128)S(1)}, u32[]{:S(2)}, u32[]{:S(2)}) collective-permute-start(f32[2,64,64]{2,1,0:T(8,128)} %get-tuple-element.85), channel_id=1, source_target_pairs={{0,4},{4,8},{8,12},{12,16},{16,20},{20,24},{24,28},{1,5},{5,9},{9,... | collective-permute-start | bytes 98312 | tf_op jit(solution)/shard_map/ppermute | solution.py:10
  83.3 6.4 %collective-permute-start.6 = (f32[2,64,64]{2,1,0:T(8,128)}, f32[2,64,64]{2,1,0:T(8,128)S(1)}, u32[]{:S(2)}, u32[]{:S(2)}) collective-permute-start(f32[2,64,64]{2,1,0:T(8,128)} %get-tuple-element.86), channel_id=1, source_target_pairs={{4,0},{8,4},{12,8},{16,12},{20,16},{24,20},{28,24},{5,1},{9,5},{13... | collective-permute-start | bytes 98312 | tf_op jit(solution)/shard_map/ppermute | solution.py:10
  84.6 7.0 %collective-permute-start.7 = (f32[2,64,64]{2,1,0:T(8,128)}, f32[2,64,64]{2,1,0:T(8,128)S(1)}, u32[]{:S(2)}, u32[]{:S(2)}) collective-permute-start(f32[2,64,64]{2,1,0:T(8,128)} %get-tuple-element.88), channel_id=1, source_target_pairs={{4,0},{8,4},{12,8},{16,12},{20,16},{24,20},{28,24},{5,1},{9,5},{13... | collective-permute-start | bytes 98312 | tf_op jit(solution)/shard_map/ppermute | solution.py:10
  86.6 5.0 %copy-start.7 = (f32[2,64,64]{2,1,0:T(8,128)S(1)}, f32[2,64,64]{2,1,0:T(8,128)}, u32[]{:S(2)}) copy-start(f32[2,64,64]{2,1,0:T(8,128)} %get-tuple-element.87) | copy-start | bytes 98308
  92.4 7.3 %collective-permute-start = (f32[2,64,64]{2,1,0:T(8,128)S(1)}, f32[2,64,64]{2,1,0:T(8,128)S(1)}, u32[]{:S(2)}, u32[]{:S(2)}) collective-permute-start(f32[2,64,64]{2,1,0:T(8,128)S(1)} %broadcast_select_fusion.4), channel_id=1, source_target_pairs={{0,4},{4,8},{8,12},{12,16},{16,20},{20,24},{24,28},{1,5},{5,9},{9,... | collective-permute-start | bytes 98312 | tf_op jit(solution)/shard_map/while/body/eval_jaxpr/ppermute | solution.py:10
  97.2 6.2 %collective-permute-start.1 = (f32[2,64,64]{2,1,0:T(8,128)S(1)}, f32[2,64,64]{2,1,0:T(8,128)S(1)}, u32[]{:S(2)}, u32[]{:S(2)}) collective-permute-start(f32[2,64,64]{2,1,0:T(8,128)S(1)} %broadcast_select_fusion.5), channel_id=1, source_target_pairs={{4,0},{8,4},{12,8},{16,12},{20,16},{24,20},{28,24},{5,1},{9,5},{13... | collective-permute-start | bytes 98312 | tf_op jit(solution)/shard_map/while/body/eval_jaxpr/ppermute | solution.py:10
  104.1 6.2 %collective-permute-start = (f32[2,64,64]{2,1,0:T(8,128)S(1)}, f32[2,64,64]{2,1,0:T(8,128)S(1)}, u32[]{:S(2)}, u32[]{:S(2)}) collective-permute-start(f32[2,64,64]{2,1,0:T(8,128)S(1)} %broadcast_select_fusion.4), channel_id=1, source_target_pairs={{0,4},{4,8},{8,12},{12,16},{16,20},{20,24},{24,28},{1,5},{5,9},{9,... | collective-permute-start | bytes 98312 | tf_op jit(solution)/shard_map/while/body/eval_jaxpr/ppermute | solution.py:10
  108.4 6.2 %collective-permute-start.1 = (f32[2,64,64]{2,1,0:T(8,128)S(1)}, f32[2,64,64]{2,1,0:T(8,128)S(1)}, u32[]{:S(2)}, u32[]{:S(2)}) collective-permute-start(f32[2,64,64]{2,1,0:T(8,128)S(1)} %broadcast_select_fusion.5), channel_id=1, source_target_pairs={{4,0},{8,4},{12,8},{16,12},{20,16},{24,20},{28,24},{5,1},{9,5},{13... | collective-permute-start | bytes 98312 | tf_op jit(solution)/shard_map/while/body/eval_jaxpr/ppermute | solution.py:10
  115.3 5.3 %collective-permute-start = (f32[2,64,64]{2,1,0:T(8,128)S(1)}, f32[2,64,64]{2,1,0:T(8,128)S(1)}, u32[]{:S(2)}, u32[]{:S(2)}) collective-permute-start(f32[2,64,64]{2,1,0:T(8,128)S(1)} %broadcast_select_fusion.4), channel_id=1, source_target_pairs={{0,4},{4,8},{8,12},{12,16},{16,20},{20,24},{24,28},{1,5},{5,9},{9,... | collective-permute-start | bytes 98312 | tf_op jit(solution)/shard_map/while/body/eval_jaxpr/ppermute | solution.py:10
  118.8 6.2 %collective-permute-start.1 = (f32[2,64,64]{2,1,0:T(8,128)S(1)}, f32[2,64,64]{2,1,0:T(8,128)S(1)}, u32[]{:S(2)}, u32[]{:S(2)}) collective-permute-start(f32[2,64,64]{2,1,0:T(8,128)S(1)} %broadcast_select_fusion.5), channel_id=1, source_target_pairs={{4,0},{8,4},{12,8},{16,12},{20,16},{24,20},{28,24},{5,1},{9,5},{13... | collective-permute-start | bytes 98312 | tf_op jit(solution)/shard_map/while/body/eval_jaxpr/ppermute | solution.py:10
  125.6 6.1 %collective-permute-start = (f32[2,64,64]{2,1,0:T(8,128)S(1)}, f32[2,64,64]{2,1,0:T(8,128)S(1)}, u32[]{:S(2)}, u32[]{:S(2)}) collective-permute-start(f32[2,64,64]{2,1,0:T(8,128)S(1)} %broadcast_select_fusion.4), channel_id=1, source_target_pairs={{0,4},{4,8},{8,12},{12,16},{16,20},{20,24},{24,28},{1,5},{5,9},{9,... | collective-permute-start | bytes 98312 | tf_op jit(solution)/shard_map/while/body/eval_jaxpr/ppermute | solution.py:10
  129.9 6.4 %collective-permute-start.1 = (f32[2,64,64]{2,1,0:T(8,128)S(1)}, f32[2,64,64]{2,1,0:T(8,128)S(1)}, u32[]{:S(2)}, u32[]{:S(2)}) collective-permute-start(f32[2,64,64]{2,1,0:T(8,128)S(1)} %broadcast_select_fusion.5), channel_id=1, source_target_pairs={{4,0},{8,4},{12,8},{16,12},{20,16},{24,20},{28,24},{5,1},{9,5},{13... | collective-permute-start | bytes 98312 | tf_op jit(solution)/shard_map/while/body/eval_jaxpr/ppermute | solution.py:10
  137.1 5.5 %collective-permute-start = (f32[2,64,64]{2,1,0:T(8,128)S(1)}, f32[2,64,64]{2,1,0:T(8,128)S(1)}, u32[]{:S(2)}, u32[]{:S(2)}) collective-permute-start(f32[2,64,64]{2,1,0:T(8,128)S(1)} %broadcast_select_fusion.4), channel_id=1, source_target_pairs={{0,4},{4,8},{8,12},{12,16},{16,20},{20,24},{24,28},{1,5},{5,9},{9,... | collective-permute-start | bytes 98312 | tf_op jit(solution)/shard_map/while/body/eval_jaxpr/ppermute | solution.py:10
  140.5 6.2 %collective-permute-start.1 = (f32[2,64,64]{2,1,0:T(8,128)S(1)}, f32[2,64,64]{2,1,0:T(8,128)S(1)}, u32[]{:S(2)}, u32[]{:S(2)}) collective-permute-start(f32[2,64,64]{2,1,0:T(8,128)S(1)} %broadcast_select_fusion.5), channel_id=1, source_target_pairs={{4,0},{8,4},{12,8},{16,12},{20,16},{24,20},{28,24},{5,1},{9,5},{13... | collective-permute-start | bytes 98312 | tf_op jit(solution)/shard_map/while/body/eval_jaxpr/ppermute | solution.py:10
  147.4 7.0 %collective-permute-start = (f32[2,64,64]{2,1,0:T(8,128)S(1)}, f32[2,64,64]{2,1,0:T(8,128)S(1)}, u32[]{:S(2)}, u32[]{:S(2)}) collective-permute-start(f32[2,64,64]{2,1,0:T(8,128)S(1)} %broadcast_select_fusion.4), channel_id=1, source_target_pairs={{0,4},{4,8},{8,12},{12,16},{16,20},{20,24},{24,28},{1,5},{5,9},{9,... | collective-permute-start | bytes 98312 | tf_op jit(solution)/shard_map/while/body/eval_jaxpr/ppermute | solution.py:10
  151.9 6.2 %collective-permute-start.1 = (f32[2,64,64]{2,1,0:T(8,128)S(1)}, f32[2,64,64]{2,1,0:T(8,128)S(1)}, u32[]{:S(2)}, u32[]{:S(2)}) collective-permute-start(f32[2,64,64]{2,1,0:T(8,128)S(1)} %broadcast_select_fusion.5), channel_id=1, source_target_pairs={{4,0},{8,4},{12,8},{16,12},{20,16},{24,20},{28,24},{5,1},{9,5},{13... | collective-permute-start | bytes 98312 | tf_op jit(solution)/shard_map/while/body/eval_jaxpr/ppermute | solution.py:10
  158.8 5.3 %collective-permute-start = (f32[2,64,64]{2,1,0:T(8,128)S(1)}, f32[2,64,64]{2,1,0:T(8,128)S(1)}, u32[]{:S(2)}, u32[]{:S(2)}) collective-permute-start(f32[2,64,64]{2,1,0:T(8,128)S(1)} %broadcast_select_fusion.4), channel_id=1, source_target_pairs={{0,4},{4,8},{8,12},{12,16},{16,20},{20,24},{24,28},{1,5},{5,9},{9,... | collective-permute-start | bytes 98312 | tf_op jit(solution)/shard_map/while/body/eval_jaxpr/ppermute | solution.py:10
  161.9 6.2 %collective-permute-start.1 = (f32[2,64,64]{2,1,0:T(8,128)S(1)}, f32[2,64,64]{2,1,0:T(8,128)S(1)}, u32[]{:S(2)}, u32[]{:S(2)}) collective-permute-start(f32[2,64,64]{2,1,0:T(8,128)S(1)} %broadcast_select_fusion.5), channel_id=1, source_target_pairs={{4,0},{8,4},{12,8},{16,12},{20,16},{24,20},{28,24},{5,1},{9,5},{13... | collective-permute-start | bytes 98312 | tf_op jit(solution)/shard_map/while/body/eval_jaxpr/ppermute | solution.py:10
  168.8 4.7 %collective-permute-start = (f32[2,64,64]{2,1,0:T(8,128)S(1)}, f32[2,64,64]{2,1,0:T(8,128)S(1)}, u32[]{:S(2)}, u32[]{:S(2)}) collective-permute-start(f32[2,64,64]{2,1,0:T(8,128)S(1)} %broadcast_select_fusion.4), channel_id=1, source_target_pairs={{0,4},{4,8},{8,12},{12,16},{16,20},{20,24},{24,28},{1,5},{5,9},{9,... | collective-permute-start | bytes 98312 | tf_op jit(solution)/shard_map/while/body/eval_jaxpr/ppermute | solution.py:10
  171.7 6.2 %collective-permute-start.1 = (f32[2,64,64]{2,1,0:T(8,128)S(1)}, f32[2,64,64]{2,1,0:T(8,128)S(1)}, u32[]{:S(2)}, u32[]{:S(2)}) collective-permute-start(f32[2,64,64]{2,1,0:T(8,128)S(1)} %broadcast_select_fusion.5), channel_id=1, source_target_pairs={{4,0},{8,4},{12,8},{16,12},{20,16},{24,20},{28,24},{5,1},{9,5},{13... | collective-permute-start | bytes 98312 | tf_op jit(solution)/shard_map/while/body/eval_jaxpr/ppermute | solution.py:10
  (2 other events, 1.3 us)
Sparse Core Ops, SparseCore 0:
  41.9 34.4 all-reduce.2
where the time goes:
time: 190 us
  waiting for transfers between devices  85.7 us (45%)
  starting transfers between devices  56.7 us (30%)
  matrix products  25.3 us (13%)
  between operations  14.5 us (8%)
  other arithmetic  4.48 us (2%)
  local copies, waits for them, and re-layouts  1.91 us (1%)
    ppermute x22, starting transfers between devices, passed_along(): lax.ppermute(value, axis, [(source, source + steps) for source in range(f...  56.7 us
    ppermute x22, waiting for transfers between devices, passed_along(): lax.ppermute(value, axis, [(source, source + steps) for source in range(f...  51 us
    psum x1, waiting for transfers between devices, body(): lax.psum((parts[0], parts[1], parts[2], parts[3], parts[4], parts[5]), 'l...  34.7 us
    dot_general x32, matrix products, prod(): lax.dot_general(a, b, dims, precision=hp, preferred_element_type=jnp.floa...  15 us
    dot_general x64, matrix products, prod(): return jnp.dot(a, b, precision=hp, preferred_element_type=jnp.float32)  10.3 us
  transfers between devices with their start and end apart: 23, of which 20 were waited for; matrix products, arithmetic and copies ran while one was open for 9% of the time, Pallas kernels for 0%

commit v1 on v0

v1 whole, which is shorter than its diff:
```python
import jax
import jax.numpy as jnp
from jax import lax
from jax.experimental import pallas as pl
from jax.experimental.pallas import tpu as pltpu
from jax.sharding import PartitionSpec as P

F32 = jnp.float32
BF16 = jnp.bfloat16
VMEM = pl.BlockSpec(memory_space=pltpu.VMEM)
SMEM = pl.BlockSpec(memory_space=pltpu.SMEM)


def split(value):
    high = value.astype(BF16)
    return high, (value - high.astype(F32)).astype(BF16)


def dot3(left, right, dims):
    def prod(a, b):
        return lax.dot_general(a, b, (dims, ((), ())), preferred_element_type=F32)

    return prod(left[0], right[0]) + (prod(left[0], right[1]) + prod(left[1], right[0]))


ROWS_COLS = ((1,), (0,))
ROWS_ROWS = ((1,), (1,))


def turned(value):
    half = value.shape[1] // 2
    lanes = lax.broadcasted_iota(jnp.int32, value.shape, 1)
    swapped = pltpu.roll(value, half, 1)
    return jnp.where(lanes < half, -swapped, swapped)


def joined(product):
    half = product.shape[0] // 2
    return product[:half] + turned(product[half:])


def spread(rows):
    half = rows.shape[1] // 2
    lanes = lax.broadcasted_iota(jnp.int32, rows.shape, 1)
    return jnp.concatenate([jnp.where(lanes < half, rows, -rows), pltpu.roll(rows, half, 1)], axis=0)


def apply_map(rows, step):
    rank = step.shape[1] // 2
    matrix = step[:rank]
    full = jnp.concatenate([matrix, turned(matrix)], axis=0)
    return dot3(split(rows), split(full), ROWS_COLS)


def compose(later, earlier):
    rank = later.shape[1] // 2
    out = apply_map(earlier, later)
    return jnp.concatenate([out[:rank], out[rank:] + later[rank:]], axis=0)


def advance(step, rows):
    rank = step.shape[1] // 2
    return apply_map(rows, step) + step[rank:]


def entry_kernel(dp_ref, up_ref, di_ref, ui_ref, out_ref):
    for k, (proj, wave) in enumerate(((dp_ref, di_ref), (up_ref, ui_ref))):
        half = wave.shape[0] // 2
        out = dot3(split(wave[...]), split(proj[...]), ROWS_ROWS)
        out_ref[k * half : (k + 1) * half] = joined(out)


def prepare_kernel(edge_ref, count_ref, list_ref, src_ref, de_ref, ue_ref, dd_ref, ud_ref, entry_ref, loc_ref, left_ref):
    nsrc = src_ref.shape[0] // 2
    rank = de_ref.shape[0] // 2
    rows = lax.broadcasted_iota(jnp.int32, (nsrc, list_ref.shape[1]), 0)
    cols = lax.broadcasted_iota(jnp.int32, (nsrc, list_ref.shape[1]), 1)
    hit = (rows == list_ref[...]) & (cols < count_ref[0])
    mask = jnp.sum(jnp.where(hit, 1.0, 0.0), axis=1, keepdims=True)
    local = src_ref[...] * jnp.concatenate([mask, mask], axis=0)
    loc_ref[...] = local
    eye = lax.broadcasted_iota(jnp.int32, (rank, rank), 0) == lax.broadcasted_iota(jnp.int32, (rank, rank), 1)
    for k, (basis_ref, decay_ref) in enumerate(((de_ref, dd_ref), (ue_ref, ud_ref))):
        decay = jnp.sum(jnp.where(eye, decay_ref[...], 0.0), axis=1, keepdims=True)
        basis = split(basis_ref[...] * jnp.concatenate([decay, decay], axis=0))
        first = jnp.where(edge_ref[k] == 1, entry_ref[k * nsrc : (k + 1) * nsrc], 0.0)
        trace = split(local + dot3(split(spread(first)), basis, ROWS_COLS))
        for part in (0, 1):
            left_ref[k, part, : 2 * rank] = basis[part]
            left_ref[k, part, 2 * rank :] = trace[part]


def gram_kernel(which, proj_ref, left_ref, out_ref):
    rank = proj_ref.shape[0] // 2
    out = dot3((left_ref[which, 0], left_ref[which, 1]), split(proj_ref[...]), ROWS_ROWS)
    half = out.shape[0] // 2
    out_ref[:rank] = joined(out[: 2 * rank])
    out_ref[rank:] = joined(out[2 * rank :])


def pair_kernel(flag_ref, own_ref, other_ref, near_ref, out_ref):
    own, other = own_ref[...], other_ref[...]
    first = flag_ref[0] == 0
    near = jnp.where(first, own, other)
    far = jnp.where(first, other, own)
    near_ref[...] = near
    out_ref[...] = compose(far, near)


def total_kernel(flag_ref, own_ref, other_ref, out_ref):
    own, other = own_ref[...], other_ref[...]
    lower = flag_ref[0] == 0
    out_ref[...] = compose(jnp.where(lower, other, own), jnp.where(lower, own, other))


def total_offset_kernel(flag_ref, own_ref, other_ref, out_ref):
    own, other = own_ref[...], other_ref[...]
    rank = own.shape[1] // 2
    lower = flag_ref[0] == 0
    out_ref[...] = advance(jnp.where(lower, other, own), jnp.where(lower, own, other)[rank:])


def final_kernel(flags_ref, carry_ref, gap_ref, near_ref, entry_ref, out_ref):
    nsrc = carry_ref.shape[0]
    carry = carry_ref[...]
    carry = jnp.where(flags_ref[0] == 1, advance(gap_ref[...], carry), carry)
    carry = jnp.where(flags_ref[1] == 1, advance(near_ref[...], carry), carry)
    entry = jnp.where(flags_ref[3] == 0, entry_ref[:nsrc], entry_ref[nsrc:])
    out_ref[...] = jnp.where(flags_ref[2] == 1, entry, carry)


def expand_kernel(role_ref, own_ref, other_ref, left_ref, loc_ref, out_ref):
    rank2 = own_ref.shape[1]
    total = loc_ref[...]
    for role, rows_ref in ((role_ref[0], own_ref), (1 - role_ref[0], other_ref)):
        basis = (left_ref[role, 0, :rank2], left_ref[role, 1, :rank2])
        total = total + dot3(split(spread(rows_ref[...])), basis, ROWS_COLS)
    out_ref[...] = total


def call(kernel, outs, *args, scalars=0):
    return pl.pallas_call(
        kernel,
        out_shape=outs,
        in_specs=[SMEM] * scalars + [VMEM] * (len(args) - scalars),
        out_specs=jax.tree.map(lambda _: VMEM, outs),
    )(*args)


def shape(*dims, dtype=F32):
    return jax.ShapeDtypeStruct(dims, dtype)


def body(
    sources,
    down_expand,
    down_project,
    up_expand,
    up_project,
    down_decay,
    up_decay,
    active_list,
    active_count,
    incident_down,
    incident_up,
):
    nsrc, width = sources.shape[2:]
    rank = down_expand.shape[2]
    depth, lat = lax.axis_size("depth"), lax.axis_size("lat")
    group = lax.axis_index("depth")
    role = lax.rem(lax.axis_index("lat"), 2)
    place = jnp.where(role == 0, group, depth - 1 - group)
    pair = place // 2

    def flat(value):
        return value.reshape(value.shape[-3] * value.shape[-2], value.shape[-1])

    def flags(*values):
        return jnp.stack([jnp.asarray(value).astype(jnp.int32) for value in values])

    def shifted(value, step):
        pairs = [(k, k + step) for k in range(depth) if 0 <= k + step < depth]
        return lax.ppermute(value, "depth", pairs)

    def swapped(value, axis, bit):
        return lax.ppermute(value, axis, [(k, k ^ bit) for k in range(lax.axis_size(axis))])

    ahead = shifted(flat(down_project), -1)
    behind = shifted(flat(up_project), 1)

    entry = call(entry_kernel, shape(2 * nsrc, 2 * rank), flat(down_project), flat(up_project), flat(incident_down), flat(incident_up))
    bit = 1
    while bit < lat:
        entry = entry + swapped(entry, "lat", bit)
        bit *= 2
    local, left = call(
        prepare_kernel,
        (shape(2 * nsrc, width), shape(2, 2, 2 * rank + 2 * nsrc, width, dtype=BF16)),
        flags(group == 0, group == depth - 1),
        active_count,
        active_list,
        flat(sources),
        flat(down_expand),
        flat(up_expand),
        down_decay,
        up_decay,
        entry,
        scalars=2,
    )
    element = shape(rank + nsrc, 2 * rank)

    def gram(which, proj):
        return call(lambda *refs: gram_kernel(which, *refs), element, proj, left)

    down, up = gram(0, ahead), gram(1, behind)
    own = jnp.where(role == 0, down, up) + swapped(jnp.where(role == 0, up, down), "lat", 1)
    bit = 2
    while bit < lat:
        own = own + swapped(own, "lat", bit)
        bit *= 2

    near, total = call(pair_kernel, (element, element), flags(lax.rem(place, 2)), own, swapped(own, "depth", 1), scalars=1)

    gap, has_gap = near, jnp.int32(0)
    reach = 2
    while reach < depth // 2:
        upper = (place // reach) % 2
        other = swapped(total, "depth", reach)
        if reach == 2:
            gap, has_gap = other, upper
        else:
            joint = call(lambda _, a, b, o: total_kernel(_, a, b, o), element, flags(1), gap, other, scalars=1)
            gap = jnp.where(upper == 1, jnp.where(has_gap == 1, joint, other), gap)
            has_gap = jnp.maximum(has_gap, upper)
        last = reach * 2 >= depth // 2
        kernel = total_offset_kernel if last else total_kernel
        total = call(kernel, shape(nsrc, 2 * rank) if last else element, flags(upper), total, other, scalars=1)
        reach *= 2
    half = depth // 2
    moves = []
    for k in range(half):
        for j in range(lat):
            low, high = (k, k + half) if j % 2 == 0 else (depth - 1 - k, half - 1 - k)
            moves.append((low * lat + j, high * lat + j))
    carry = lax.ppermute(total, ("depth", "lat"), moves)
    coef = call(
        final_kernel,
        shape(nsrc, 2 * rank),
        flags(has_gap, lax.rem(place, 2), place == 0, role),
        carry,
        gap,
        near,
        entry,
        scalars=1,
    )
    field = call(expand_kernel, shape(2 * nsrc, width), flags(role), coef, swapped(coef, "lat", 1), left, local, scalars=1)
    return field.reshape(sources.shape)


def solution(mesh):
    in_specs = (
        P("depth", None, None, "lat"),
        P("depth", None, None, "lat"),
        P("depth", None, None, "lat"),
        P("depth", None, None, "lat"),
        P("depth", None, None, "lat"),
        P("depth", None),
        P("depth", None),
        P("depth", None),
        P("depth"),
        P(None, None, "lat"),
        P(None, None, "lat"),
    )
    out_specs = P("depth", None, None, "lat")
    return jax.shard_map(body, mesh=mesh, in_specs=in_specs, out_specs=out_specs, check_vma=False)
```

time: 190 us -> 71.5 us (0.38)
  waiting for transfers between devices: 85.7 us -> 18.8 us
  starting transfers between devices: 56.7 us -> 22.8 us
  matrix products: 25.3 us -> 0 us
  Pallas kernels: 0 us -> 20.9 us
  between operations: 14.5 us -> 0.72 us
  local copies, waits for them, and re-layouts: 1.91 us -> 4.05 us
    psum x1 -> x0, waiting for transfers between devices: 34.7 us -> none  [body(): lax.psum((parts[0], parts[1], parts[2], parts[3], parts[4], parts[5]), 'l...]
    ppermute x22 -> x10, starting transfers between devices: 56.7 us -> 22.8 us  [the longest x7 11 us: swapped(): lax.ppermute(value, axis, [(k, k ^ bit) for k in range(lax.axis_size(axis...]
    ppermute x22 -> x10, waiting for transfers between devices: 51 us -> 18.8 us  [the longest x7 13.6 us: swapped(): lax.ppermute(value, axis, [(k, k ^ bit) for k in range(lax.axis_size(axis...]
    dot_general x96 -> x0, matrix products: 25.3 us -> none  [the longest x32 15 us: prod(): lax.dot_general(a, b, dims, precision=hp, preferred_element_type=jnp.floa...]
    pallas_call x0 -> x8, Pallas kernels: none -> 20.9 us  [call(): pl.pallas_call(kernel, out_shape=outs, in_specs=[SMEM] * scalars + [VMEM]...]
    unnamed x22 -> x16, local copies, waits for them, and re-layouts: 1.91 us -> 4.05 us
  transfers between devices with their start and end apart: 23 -> 10, of which waited for: 20 -> 9; matrix products, arithmetic and copies ran while one was open for 9% -> 4% of each run, Pallas kernels for 0% -> 13%
where the time goes in v1:
time: 71.5 us; the launch traced here: 70.9 us
  starting transfers between devices  22.8 us (32%)
  Pallas kernels  20.9 us (29%)
  waiting for transfers between devices  18.8 us (26%)
  local copies, waits for them, and re-layouts  4.05 us (6%)
  other arithmetic  3.6 us (5%)
  between operations  0.72 us (1%)
    pallas_call x8, Pallas kernels, call(): pl.pallas_call(kernel, out_shape=outs, in_specs=[SMEM] * scalars + [VMEM]...  20.9 us
    ppermute x7, waiting for transfers between devices, swapped(): lax.ppermute(value, axis, [(k, k ^ bit) for k in range(lax.axis_size(axis...  13.6 us
    ppermute x7, starting transfers between devices, swapped(): lax.ppermute(value, axis, [(k, k ^ bit) for k in range(lax.axis_size(axis...  11 us
    ppermute x2, starting transfers between devices, shifted(): return lax.ppermute(value, 'depth', pairs)  6.84 us
    ppermute x1, starting transfers between devices, body(): carry = lax.ppermute(total, ('depth', 'lat'), moves)  4.93 us
    unnamed x16, local copies, waits for them, and re-layouts  4.05 us
    ppermute x2, waiting for transfers between devices, shifted(): return lax.ppermute(value, 'depth', pairs)  4.03 us
    add x2, other arithmetic, body(): entry = entry + swapped(entry, 'lat', bit)  1.47 us
  transfers between devices with their start and end apart: 10, of which 9 were waited for; matrix products, arithmetic and copies ran while one was open for 4% of the time, Pallas kernels for 13%

profile of v1, /device:TPU:0, one launch (start us, length us, event | category | flops | bytes accessed | tf_op | source)
XLA Modules:
  0.0 70.9 jit_solution(8839920204997399666)
XLA Ops:
  0.0 1.3 %collective-permute-start = (f32[128,1024]{1,0:T(8,128)}, f32[128,1024]{1,0:T(8,128)S(1)}, u32[]{:S(2)}, u32[]{:S(2)}) collective-permute-start(f32[128,1024]{1,0:T(8,128)} %bitcast.19), channel_id=1, source_target_pairs={{4,0},{8,4},{12,8},{16,12},{20,16},{24,20},{28,24},{5,1},{9,5},{13... | collective-permute-start | bytes 1572872 | tf_op jit(solution)/shard_map/ppermute | solution.py:183
  1.3 5.6 %collective-permute-start.3 = (f32[128,1024]{1,0:T(8,128)}, f32[128,1024]{1,0:T(8,128)S(1)}, u32[]{:S(2)}, u32[]{:S(2)}) collective-permute-start(f32[128,1024]{1,0:T(8,128)} %bitcast.21), channel_id=1, source_target_pairs={{0,4},{4,8},{8,12},{12,16},{16,20},{20,24},{24,28},{1,5},{5,9},{9,... | collective-permute-start | bytes 1572872 | tf_op jit(solution)/shard_map/ppermute | solution.py:183
  6.9 2.8 %shard_map.109 = f32[128,128]{1,0:T(8,128)} custom-call(f32[128,1024]{1,0:T(8,128)} %bitcast.20, f32[128,1024]{1,0:T(8,128)} %bitcast.22, f32[128,1024]{1,0:T(8,128)} %bitcast.17, f32[128,1024]{1,0:T(8,128)} %bitcast.18), custom_call_target="tpu_custom_call" | custom-call | tf_op jit(solution)/shard_map/pallas_call | solution.py:142
  10.3 0.8 %collective-permute-done.1 = f32[128,128]{1,0:T(8,128)S(1)} collective-permute-done((f32[128,128]{1,0:T(8,128)}, f32[128,128]{1,0:T(8,128)S(1)}, u32[]{:S(2)}, u32[]{:S(2)}) %collective-permute-start.1) | collective-permute-done | bytes 65568 | tf_op jit(solution)/shard_map/ppermute | solution.py:186
  11.1 0.8 %add.18 = f32[128,128]{1,0:T(8,128)S(1)} add(f32[128,128]{1,0:T(8,128)} %shard_map.109, f32[128,128]{1,0:T(8,128)S(1)} %collective-permute-done.1) | non-fusion elementwise | flops 16384 | bytes 196608 | tf_op jit(solution)/shard_map/add | solution.py:194
  12.0 2.0 %collective-permute-start.2 = (f32[128,128]{1,0:T(8,128)S(1)}, f32[128,128]{1,0:T(8,128)S(1)}, u32[]{:S(2)}, u32[]{:S(2)}) collective-permute-start(f32[128,128]{1,0:T(8,128)S(1)} %add.18), channel_id=1, source_target_pairs={{0,2},{1,3},{2,0},{3,1},{4,6},{5,7},{6,4},{7,5},{8,10},{9,11},{10,... | collective-permute-start | bytes 196616 | tf_op jit(solution)/shard_map/ppermute | solution.py:186
  14.6 1.8 %collective-permute-done.2 = f32[128,128]{1,0:T(8,128)S(1)} collective-permute-done((f32[128,128]{1,0:T(8,128)S(1)}, f32[128,128]{1,0:T(8,128)S(1)}, u32[]{:S(2)}, u32[]{:S(2)}) %collective-permute-start.2) | collective-permute-done | bytes 65568 | tf_op jit(solution)/shard_map/ppermute | solution.py:186
  16.4 0.6 add.19.entry_ref
  17.1 3.6 %shard_map.110 = (f32[128,1024]{1,0:T(8,128)}, bf16[2,2,256,1024]{3,2,1,0:T(8,128)(2,1)}) custom-call(s32[2]{0:T(128)} %add_convert_fusion.edge_ref, s32[1]{0:T(128)S(6)} %copy.12.count_ref, s32[1,64]{1,0:T(1,128)} %list_ref.1, f32[128,1024]{1,0:T(8,128)} %bitcast.14, f32[128,1024]{1,0:T(8,128)} %bitcast.15, f32[128,1024]{1,0:T(8,128)} %bitcast.16, ...), custom_call_target="tpu_custom_call" | custom-call | tf_op jit(solution)/shard_map/pallas_call | solution.py:142
  20.6 0.8 %copy-done.2 = f32[128,1024]{1,0:T(8,128)} copy-done((f32[128,1024]{1,0:T(8,128)}, f32[128,1024]{1,0:T(8,128)S(1)}, u32[]{:S(2)}) %copy-start.2) | copy-done | bytes 524312
  21.4 3.1 %shard_map.111 = f32[128,128]{1,0:T(8,128)} custom-call(f32[128,1024]{1,0:T(8,128)} %copy-done.2, bf16[2,2,256,1024]{3,2,1,0:T(8,128)(2,1)} %get-tuple-element.9.refs_1_.left_ref), custom_call_target="tpu_custom_call" | custom-call | tf_op jit(solution)/shard_map/pallas_call | solution.py:142
  24.5 4.0 %collective-permute-done.3.refs_0_ = f32[128,1024]{1,0:T(8,128)S(1)} collective-permute-done((f32[128,1024]{1,0:T(8,128)}, f32[128,1024]{1,0:T(8,128)S(1)}, u32[]{:S(2)}, u32[]{:S(2)}) %collective-permute-start.3) | collective-permute-done | bytes 524320 | tf_op jit(solution)/shard_map/ppermute | solution.py:183
  28.5 0.8 %copy-done.1 = f32[128,1024]{1,0:T(8,128)} copy-done((f32[128,1024]{1,0:T(8,128)}, f32[128,1024]{1,0:T(8,128)S(1)}, u32[]{:S(2)}) %copy-start.1) | copy-done | bytes 524312
  29.3 3.0 %shard_map.112 = f32[128,128]{1,0:T(8,128)} custom-call(f32[128,1024]{1,0:T(8,128)} %copy-done.1, bf16[2,2,256,1024]{3,2,1,0:T(8,128)(2,1)} %get-tuple-element.9.refs_1_.left_ref), custom_call_target="tpu_custom_call" | custom-call | tf_op jit(solution)/shard_map/pallas_call | solution.py:142
  32.4 0.8 %broadcast_select_fusion = f32[128,128]{1,0:T(8,128)S(1)} fusion(f32[128,128]{1,0:T(8,128)} %shard_map.112, f32[128,128]{1,0:T(8,128)S(1)} %copy-done, pred[]{:T(512)S(6)} %eq.16), kind=kLoop, calls=%fused_computation.1 | loop fusion | flops 16384 | bytes 196609 | tf_op jit(solution)/shard_map/jit(_where)/select_n | solution.py:216
  33.3 1.2 %collective-permute-done.4 = f32[128,128]{1,0:T(8,128)S(1)} collective-permute-done((f32[128,128]{1,0:T(8,128)S(1)}, f32[128,128]{1,0:T(8,128)S(1)}, u32[]{:S(2)}, u32[]{:S(2)}) %collective-permute-start.4) | collective-permute-done | bytes 65568 | tf_op jit(solution)/shard_map/ppermute | solution.py:186
  34.5 1.6 %collective-permute-start.5 = (f32[128,128]{1,0:T(8,128)S(1)}, f32[128,128]{1,0:T(8,128)S(1)}, u32[]{:S(2)}, u32[]{:S(2)}) collective-permute-start(f32[128,128]{1,0:T(8,128)S(1)} %select_add_fusion), channel_id=1, source_target_pairs={{0,2},{1,3},{2,0},{3,1},{4,6},{5,7},{6,4},{7,5},{8,10},{9,11},{10,... | collective-permute-start | bytes 196616 | tf_op jit(solution)/shard_map/ppermute | solution.py:186
  36.1 3.4 %collective-permute-done.5 = f32[128,128]{1,0:T(8,128)S(1)} collective-permute-done((f32[128,128]{1,0:T(8,128)S(1)}, f32[128,128]{1,0:T(8,128)S(1)}, u32[]{:S(2)}, u32[]{:S(2)}) %collective-permute-start.5) | collective-permute-done | bytes 65568 | tf_op jit(solution)/shard_map/ppermute | solution.py:186
  39.6 2.4 %collective-permute-start.6 = (f32[128,128]{1,0:T(8,128)S(1)}, f32[128,128]{1,0:T(8,128)S(1)}, u32[]{:S(2)}, u32[]{:S(2)}) collective-permute-start(f32[128,128]{1,0:T(8,128)S(1)} %add.21.own_ref), channel_id=1, source_target_pairs={{0,4},{4,0},{8,12},{12,8},{16,20},{20,16},{24,28},{28,24},{1,5},{5... | collective-permute-start | bytes 196616 | tf_op jit(solution)/shard_map/ppermute | solution.py:186
  42.0 2.4 %collective-permute-done.6.other_ref = f32[128,128]{1,0:T(8,128)S(1)} collective-permute-done((f32[128,128]{1,0:T(8,128)S(1)}, f32[128,128]{1,0:T(8,128)S(1)}, u32[]{:S(2)}, u32[]{:S(2)}) %collective-permute-start.6) | collective-permute-done | bytes 65568 | tf_op jit(solution)/shard_map/ppermute | solution.py:186
  44.4 0.6 copy-done.5
  45.0 1.7 %shard_map.113 = (f32[128,128]{1,0:T(8,128)}, f32[128,128]{1,0:T(8,128)}) custom-call(s32[1]{0:T(128)} %bitcast.2.flag_ref, f32[128,128]{1,0:T(8,128)} %copy-done.3, f32[128,128]{1,0:T(8,128)} %copy-done.5), custom_call_target="tpu_custom_call" | custom-call | tf_op jit(solution)/shard_map/pallas_call | solution.py:142
  46.7 4.9 %collective-permute-start.7 = (f32[128,128]{1,0:T(8,128)}, f32[128,128]{1,0:T(8,128)S(1)}, u32[]{:S(2)}, u32[]{:S(2)}) collective-permute-start(f32[128,128]{1,0:T(8,128)} %get-tuple-element.10.own_ref), channel_id=1, source_target_pairs={{0,8},{4,12},{8,0},{12,4},{16,24},{20,28},{24,16},{28,20},{1,9},{5... | collective-permute-start | bytes 196616 | tf_op jit(solution)/shard_map/ppermute | solution.py:186
  51.6 2.5 %collective-permute-done.7.other_ref.gap_ref = f32[128,128]{1,0:T(8,128)S(1)} collective-permute-done((f32[128,128]{1,0:T(8,128)}, f32[128,128]{1,0:T(8,128)S(1)}, u32[]{:S(2)}, u32[]{:S(2)}) %collective-permute-start.7) | collective-permute-done | bytes 65568 | tf_op jit(solution)/shard_map/ppermute | solution.py:186
  54.1 0.6 copy-done.4
  54.7 1.7 %shard_map.114 = f32[64,128]{1,0:T(8,128)} custom-call(s32[1]{0:T(128)} %bitcast.1.flag_ref, f32[128,128]{1,0:T(8,128)} %get-tuple-element.10.own_ref, f32[128,128]{1,0:T(8,128)} %copy-done.4), custom_call_target="tpu_custom_call" | custom-call | tf_op jit(solution)/shard_map/pallas_call | solution.py:142
  56.4 4.9 %collective-permute-start.8 = (f32[64,128]{1,0:T(8,128)}, f32[64,128]{1,0:T(8,128)S(1)}, u32[]{:S(2)}, u32[]{:S(2)}) collective-permute-start(f32[64,128]{1,0:T(8,128)} %shard_map.114), channel_id=1, source_target_pairs={{0,16},{29,13},{2,18},{31,15},{4,20},{25,9},{6,22},{27,11},{8,24},... | collective-permute-start | bytes 98312 | tf_op jit(solution)/shard_map/ppermute | solution.py:245
  61.4 0.7 pad_add_fusion.flags_ref
  62.0 1.2 %collective-permute-done.8.carry_ref = f32[64,128]{1,0:T(8,128)S(1)} collective-permute-done((f32[64,128]{1,0:T(8,128)}, f32[64,128]{1,0:T(8,128)S(1)}, u32[]{:S(2)}, u32[]{:S(2)}) %collective-permute-start.8) | collective-permute-done | bytes 32800 | tf_op jit(solution)/shard_map/ppermute | solution.py:245
  63.9 1.9 %shard_map.115.own_ref = f32[64,128]{1,0:T(8,128)} custom-call(s32[4]{0:T(128)} %pad_add_fusion.flags_ref, f32[64,128]{1,0:T(8,128)} %copy-done.7, f32[128,128]{1,0:T(8,128)} %copy-done.4, f32[128,128]{1,0:T(8,128)} %get-tuple-element.11.near_ref, f32[128,128]{1,0:T(8,128)} %add.19.entry_ref), custom_call_target="tpu_custom_call" | custom-call | tf_op jit(solution)/shard_map/pallas_call | solution.py:142
  65.8 1.4 %collective-permute-done.9.other_ref = f32[64,128]{1,0:T(8,128)S(1)} collective-permute-done((f32[64,128]{1,0:T(8,128)}, f32[64,128]{1,0:T(8,128)S(1)}, u32[]{:S(2)}, u32[]{:S(2)}) %collective-permute-start.9) | collective-permute-done | bytes 32800 | tf_op jit(solution)/shard_map/ppermute | solution.py:186
  67.8 3.1 %shard_map.116 = f32[128,1024]{1,0:T(8,128)} custom-call(s32[1]{0:T(128)} %bitcast.role_ref, f32[64,128]{1,0:T(8,128)} %shard_map.115.own_ref, f32[64,128]{1,0:T(8,128)} %copy-done.6, bf16[2,2,256,1024]{3,2,1,0:T(8,128)(2,1)} %get-tuple-element.9.refs_1_.left_ref, f32[128,1024]{1,0:T(8,128)} %get-tuple-element.12.loc_ref), custom_call_target="tpu_custom_call" | custom-call | tf_op jit(solution)/shard_map/pallas_call | solution.py:142
  (19 shorter events, 1.9 us)
Async XLA Ops:
  0.0 20.6 %collective-permute-start = (f32[128,1024]{1,0:T(8,128)}, f32[128,1024]{1,0:T(8,128)S(1)}, u32[]{:S(2)}, u32[]{:S(2)}) collective-permute-start(f32[128,1024]{1,0:T(8,128)} %bitcast.19), channel_id=1, source_target_pairs={{4,0},{8,4},{12,8},{16,12},{20,16},{24,20},{28,24},{5,1},{9,5},{13... | collective-permute-start | bytes 1572872 | tf_op jit(solution)/shard_map/ppermute | solution.py:183
  1.3 27.2 %collective-permute-start.3 = (f32[128,1024]{1,0:T(8,128)}, f32[128,1024]{1,0:T(8,128)S(1)}, u32[]{:S(2)}, u32[]{:S(2)}) collective-permute-start(f32[128,1024]{1,0:T(8,128)} %bitcast.21), channel_id=1, source_target_pairs={{0,4},{4,8},{8,12},{12,16},{16,20},{20,24},{24,28},{1,5},{5,9},{9,... | collective-permute-start | bytes 1572872 | tf_op jit(solution)/shard_map/ppermute | solution.py:183
  9.7 1.5 %collective-permute-start.1 = (f32[128,128]{1,0:T(8,128)}, f32[128,128]{1,0:T(8,128)S(1)}, u32[]{:S(2)}, u32[]{:S(2)}) collective-permute-start(f32[128,128]{1,0:T(8,128)} %shard_map.109), channel_id=1, source_target_pairs={{0,1},{1,0},{2,3},{3,2},{4,5},{5,4},{6,7},{7,6},{8,9},{9,8},{10,11... | collective-permute-start | bytes 196616 | tf_op jit(solution)/shard_map/ppermute | solution.py:186
  12.0 4.5 %collective-permute-start.2 = (f32[128,128]{1,0:T(8,128)S(1)}, f32[128,128]{1,0:T(8,128)S(1)}, u32[]{:S(2)}, u32[]{:S(2)}) collective-permute-start(f32[128,128]{1,0:T(8,128)S(1)} %add.18), channel_id=1, source_target_pairs={{0,2},{1,3},{2,0},{3,1},{4,6},{5,7},{6,4},{7,5},{8,10},{9,11},{10,... | collective-permute-start | bytes 196616 | tf_op jit(solution)/shard_map/ppermute | solution.py:186
  20.6 0.8 %copy-start.2 = (f32[128,1024]{1,0:T(8,128)}, f32[128,1024]{1,0:T(8,128)S(1)}, u32[]{:S(2)}) copy-start(f32[128,1024]{1,0:T(8,128)S(1)} %collective-permute-done.refs_0_) | copy-start | bytes 1572868
  24.5 7.9 %copy-start = (f32[128,128]{1,0:T(8,128)S(1)}, f32[128,128]{1,0:T(8,128)}, u32[]{:S(2)}) copy-start(f32[128,128]{1,0:T(8,128)} %shard_map.111) | copy-start | bytes 196612
  28.5 0.8 %copy-start.1 = (f32[128,1024]{1,0:T(8,128)}, f32[128,1024]{1,0:T(8,128)S(1)}, u32[]{:S(2)}) copy-start(f32[128,1024]{1,0:T(8,128)S(1)} %collective-permute-done.3.refs_0_) | copy-start | bytes 1572868
  33.2 1.3 %collective-permute-start.4 = (f32[128,128]{1,0:T(8,128)S(1)}, f32[128,128]{1,0:T(8,128)S(1)}, u32[]{:S(2)}, u32[]{:S(2)}) collective-permute-start(f32[128,128]{1,0:T(8,128)S(1)} %broadcast_select_fusion), channel_id=1, source_target_pairs={{0,1},{1,0},{2,3},{3,2},{4,5},{5,4},{6,7},{7,6},{8,9},{9,8},{10,11... | collective-permute-start | bytes 196616 | tf_op jit(solution)/shard_map/ppermute | solution.py:186
  34.5 5.0 %collective-permute-start.5 = (f32[128,128]{1,0:T(8,128)S(1)}, f32[128,128]{1,0:T(8,128)S(1)}, u32[]{:S(2)}, u32[]{:S(2)}) collective-permute-start(f32[128,128]{1,0:T(8,128)S(1)} %select_add_fusion), channel_id=1, source_target_pairs={{0,2},{1,3},{2,0},{3,1},{4,6},{5,7},{6,4},{7,5},{8,10},{9,11},{10,... | collective-permute-start | bytes 196616 | tf_op jit(solution)/shard_map/ppermute | solution.py:186
  39.6 4.8 %copy-start.3 = (f32[128,128]{1,0:T(8,128)}, f32[128,128]{1,0:T(8,128)S(1)}, u32[]{:S(2)}) copy-start(f32[128,128]{1,0:T(8,128)S(1)} %add.21.own_ref) | copy-start | bytes 196612
  39.6 4.8 %collective-permute-start.6 = (f32[128,128]{1,0:T(8,128)S(1)}, f32[128,128]{1,0:T(8,128)S(1)}, u32[]{:S(2)}, u32[]{:S(2)}) collective-permute-start(f32[128,128]{1,0:T(8,128)S(1)} %add.21.own_ref), channel_id=1, source_target_pairs={{0,4},{4,0},{8,12},{12,8},{16,20},{20,16},{24,28},{28,24},{1,5},{5... | collective-permute-start | bytes 196616 | tf_op jit(solution)/shard_map/ppermute | solution.py:186
  44.4 0.6 copy-start.5
  46.7 7.4 %collective-permute-start.7 = (f32[128,128]{1,0:T(8,128)}, f32[128,128]{1,0:T(8,128)S(1)}, u32[]{:S(2)}, u32[]{:S(2)}) collective-permute-start(f32[128,128]{1,0:T(8,128)} %get-tuple-element.10.own_ref), channel_id=1, source_target_pairs={{0,8},{4,12},{8,0},{12,4},{16,24},{20,28},{24,16},{28,20},{1,9},{5... | collective-permute-start | bytes 196616 | tf_op jit(solution)/shard_map/ppermute | solution.py:186
  54.1 0.6 copy-start.4
  56.4 6.8 %collective-permute-start.8 = (f32[64,128]{1,0:T(8,128)}, f32[64,128]{1,0:T(8,128)S(1)}, u32[]{:S(2)}, u32[]{:S(2)}) collective-permute-start(f32[64,128]{1,0:T(8,128)} %shard_map.114), channel_id=1, source_target_pairs={{0,16},{29,13},{2,18},{31,15},{4,20},{25,9},{6,22},{27,11},{8,24},... | collective-permute-start | bytes 98312 | tf_op jit(solution)/shard_map/ppermute | solution.py:245
  63.2 0.6 copy-start.7
  65.8 1.4 %collective-permute-start.9 = (f32[64,128]{1,0:T(8,128)}, f32[64,128]{1,0:T(8,128)S(1)}, u32[]{:S(2)}, u32[]{:S(2)}) collective-permute-start(f32[64,128]{1,0:T(8,128)} %shard_map.115.own_ref), channel_id=1, source_target_pairs={{0,1},{1,0},{2,3},{3,2},{4,5},{5,4},{6,7},{7,6},{8,9},{9,8},{10,11... | collective-permute-start | bytes 98312 | tf_op jit(solution)/shard_map/ppermute | solution.py:186
  67.2 0.6 copy-start.6

commit v2 on v1

v2 whole, which is shorter than its diff:
```python
import functools

import jax
import jax.numpy as jnp
from jax import lax
from jax.experimental import pallas as pl
from jax.experimental.pallas import tpu as pltpu
from jax.sharding import PartitionSpec as P

F32 = jnp.float32
BF16 = jnp.bfloat16
VMEM = pl.BlockSpec(memory_space=pltpu.VMEM)
SMEM = pl.BlockSpec(memory_space=pltpu.SMEM)


def split(value):
    high = value.astype(BF16)
    return high, (value - high.astype(F32)).astype(BF16)


def dot3(left, right, dims):
    def prod(a, b):
        return lax.dot_general(a, b, (dims, ((), ())), preferred_element_type=F32)

    return prod(left[0], right[0]) + (prod(left[0], right[1]) + prod(left[1], right[0]))


ROWS_COLS = ((1,), (0,))
ROWS_ROWS = ((1,), (1,))


def turned(value):
    half = value.shape[1] // 2
    lanes = lax.broadcasted_iota(jnp.int32, value.shape, 1)
    swapped = pltpu.roll(value, half, 1)
    return jnp.where(lanes < half, -swapped, swapped)


def joined(product):
    half = product.shape[0] // 2
    return product[:half] + turned(product[half:])


def spread(rows):
    half = rows.shape[1] // 2
    lanes = lax.broadcasted_iota(jnp.int32, rows.shape, 1)
    return jnp.concatenate([jnp.where(lanes < half, rows, -rows), pltpu.roll(rows, half, 1)], axis=0)


def apply_map(rows, step):
    rank = step.shape[1] // 2
    matrix = step[:rank]
    full = jnp.concatenate([matrix, turned(matrix)], axis=0)
    return dot3(split(rows), split(full), ROWS_COLS)


def compose(later, earlier):
    rank = later.shape[1] // 2
    out = apply_map(earlier, later)
    return jnp.concatenate([out[:rank], out[rank:] + later[rank:]], axis=0)


def advance(step, rows):
    rank = step.shape[1] // 2
    return apply_map(rows, step) + step[rank:]


def standing():
    group, depth = lax.axis_index("depth"), lax.axis_size("depth")
    role = lax.rem(lax.axis_index("lat"), 2)
    return role, jnp.where(role == 0, group, depth - 1 - group)


def entry_kernel(dp_ref, up_ref, di_ref, ui_ref, out_ref):
    for k, (proj, wave) in enumerate(((dp_ref, di_ref), (up_ref, ui_ref))):
        half = wave.shape[0] // 2
        out = dot3(split(wave[...]), split(proj[...]), ROWS_ROWS)
        out_ref[k * half : (k + 1) * half] = joined(out)


def prepare_kernel(count_ref, list_ref, src_ref, de_ref, ue_ref, dd_ref, ud_ref, entry_ref, loc_ref, left_ref):
    group, depth = lax.axis_index("depth"), lax.axis_size("depth")
    nsrc = src_ref.shape[0] // 2
    rank = de_ref.shape[0] // 2
    rows = lax.broadcasted_iota(jnp.int32, (nsrc, list_ref.shape[1]), 0)
    cols = lax.broadcasted_iota(jnp.int32, (nsrc, list_ref.shape[1]), 1)
    hit = (rows == list_ref[...]) & (cols < count_ref[0])
    mask = jnp.sum(jnp.where(hit, 1.0, 0.0), axis=1, keepdims=True)
    local = src_ref[...] * jnp.concatenate([mask, mask], axis=0)
    loc_ref[...] = local
    eye = lax.broadcasted_iota(jnp.int32, (rank, rank), 0) == lax.broadcasted_iota(jnp.int32, (rank, rank), 1)
    for k, (basis_ref, decay_ref, edge) in enumerate(((de_ref, dd_ref, 0), (ue_ref, ud_ref, depth - 1))):
        decay = jnp.sum(jnp.where(eye, decay_ref[...], 0.0), axis=1, keepdims=True)
        basis = split(basis_ref[...] * jnp.concatenate([decay, decay], axis=0))
        first = jnp.where(group == edge, entry_ref[k * nsrc : (k + 1) * nsrc], 0.0)
        trace = split(local + dot3(split(spread(first)), basis, ROWS_COLS))
        for part in (0, 1):
            left_ref[k, part, : 2 * rank] = basis[part]
            left_ref[k, part, 2 * rank :] = trace[part]


def gram_kernel(which, proj_ref, left_ref, out_ref):
    rank = proj_ref.shape[0] // 2
    out = dot3((left_ref[which, 0], left_ref[which, 1]), split(proj_ref[...]), ROWS_ROWS)
    out_ref[:rank] = joined(out[: 2 * rank])
    out_ref[rank:] = joined(out[2 * rank :])


def pair_kernel(own_ref, other_ref, near_ref, out_ref):
    place = standing()[1]
    own, other = own_ref[...], other_ref[...]
    first = lax.rem(place, 2) == 0
    near = jnp.where(first, own, other)
    near_ref[...] = near
    out_ref[...] = compose(jnp.where(first, other, own), near)


def ordered(reach, own_ref, other_ref):
    own, other = own_ref[...], other_ref[...]
    lower = lax.rem(lax.div(standing()[1], reach), 2) == 0
    return jnp.where(lower, own, other), jnp.where(lower, other, own)


def total_kernel(reach, own_ref, other_ref, out_ref):
    earlier, later = ordered(reach, own_ref, other_ref)
    out_ref[...] = compose(later, earlier)


def total_offset_kernel(reach, own_ref, other_ref, out_ref):
    earlier, later = ordered(reach, own_ref, other_ref)
    out_ref[...] = advance(later, earlier[earlier.shape[1] // 2 :])


def gap_kernel(reach, own_ref, other_ref, out_ref):
    place = standing()[1]
    own, other = own_ref[...], other_ref[...]
    started = lax.rem(place, reach) >= 2
    upper = lax.rem(lax.div(place, reach), 2) == 1
    longer = jnp.where(started, compose(own, other), other)
    out_ref[...] = jnp.where(upper, longer, own)


def final_kernel(carry_ref, gap_ref, near_ref, entry_ref, out_ref):
    depth = lax.axis_size("depth")
    role, place = standing()
    nsrc = carry_ref.shape[0]
    carry = carry_ref[...]
    carry = jnp.where(lax.rem(place, depth // 2) >= 2, advance(gap_ref[...], carry), carry)
    carry = jnp.where(lax.rem(place, 2) == 1, advance(near_ref[...], carry), carry)
    entry = jnp.where(role == 0, entry_ref[:nsrc], entry_ref[nsrc:])
    out_ref[...] = jnp.where(place == 0, entry, carry)


def expand_kernel(turn, rows_ref, left_ref, sum_ref, out_ref):
    role = lax.rem(standing()[0] + turn, 2)
    wide = rows_ref.shape[1]
    basis = (left_ref[role, 0, :wide], left_ref[role, 1, :wide])
    out_ref[...] = sum_ref[...] + dot3(split(spread(rows_ref[...])), basis, ROWS_COLS)


def call(kernel, outs, *args, scalars=0, grant=4):
    return pl.pallas_call(
        kernel,
        out_shape=outs,
        in_specs=[SMEM] * scalars + [VMEM] * (len(args) - scalars),
        out_specs=jax.tree.map(lambda _: VMEM, outs),
        compiler_params=pltpu.CompilerParams(vmem_limit_bytes=grant << 20),
    )(*args)


def shape(*dims, dtype=F32):
    return jax.ShapeDtypeStruct(dims, dtype)


def body(
    sources,
    down_expand,
    down_project,
    up_expand,
    up_project,
    down_decay,
    up_decay,
    active_list,
    active_count,
    incident_down,
    incident_up,
):
    nsrc, width = sources.shape[2:]
    rank = down_expand.shape[2]
    depth, lat = lax.axis_size("depth"), lax.axis_size("lat")
    role = lax.rem(lax.axis_index("lat"), 2)
    element = shape(rank + nsrc, 2 * rank)

    def flat(value):
        return value.reshape(value.shape[-3] * value.shape[-2], value.shape[-1])

    def shifted(value, step):
        pairs = [(k, k + step) for k in range(depth) if 0 <= k + step < depth]
        return lax.ppermute(value, "depth", pairs)

    def swapped(value, axis, bit):
        return lax.ppermute(value, axis, [(k, k ^ bit) for k in range(lax.axis_size(axis))])

    ahead = shifted(flat(down_project), -1)
    behind = shifted(flat(up_project), 1)

    entry = call(
        entry_kernel,
        shape(2 * nsrc, 2 * rank),
        flat(down_project),
        flat(up_project),
        flat(incident_down),
        flat(incident_up),
        grant=12,
    )
    bit = 1
    while bit < lat:
        entry = entry + swapped(entry, "lat", bit)
        bit *= 2
    local, left = call(
        prepare_kernel,
        (shape(2 * nsrc, width), shape(2, 2, 2 * rank + 2 * nsrc, width, dtype=BF16)),
        active_count,
        active_list,
        flat(sources),
        flat(down_expand),
        flat(up_expand),
        down_decay,
        up_decay,
        entry,
        scalars=1,
        grant=12,
    )

    def gram(which, proj):
        return call(functools.partial(gram_kernel, which), element, proj, left)

    down, up = gram(0, ahead), gram(1, behind)
    own = jnp.where(role == 0, down, up) + swapped(jnp.where(role == 0, up, down), "lat", 1)
    bit = 2
    while bit < lat:
        own = own + swapped(own, "lat", bit)
        bit *= 2

    near, total = call(pair_kernel, (element, element), own, swapped(own, "depth", 1))
    gap = near
    reach = 2
    while reach < depth // 2:
        other = swapped(total, "depth", reach)
        gap = other if reach == 2 else call(functools.partial(gap_kernel, reach), element, gap, other)
        last = reach * 2 >= depth // 2
        kernel = functools.partial(total_offset_kernel if last else total_kernel, reach)
        total = call(kernel, shape(nsrc, 2 * rank) if last else element, total, other)
        reach *= 2
    half = depth // 2
    moves = []
    for k in range(half):
        for j in range(lat):
            low, high = (k, k + half) if j % 2 == 0 else (depth - 1 - k, half - 1 - k)
            moves.append((low * lat + j, high * lat + j))
    carry = lax.ppermute(total, ("depth", "lat"), moves)
    coef = call(final_kernel, shape(nsrc, 2 * rank), carry, gap, near, entry)
    wide = shape(2 * nsrc, width)
    field = call(functools.partial(expand_kernel, 0), wide, coef, left, local)
    field = call(functools.partial(expand_kernel, 1), wide, swapped(coef, "lat", 1), left, field)
    return field.reshape(sources.shape)


def solution(mesh):
    in_specs = (
        P("depth", None, None, "lat"),
        P("depth", None, None, "lat"),
        P("depth", None, None, "lat"),
        P("depth", None, None, "lat"),
        P("depth", None, None, "lat"),
        P("depth", None),
        P("depth", None),
        P("depth", None),
        P("depth"),
        P(None, None, "lat"),
        P(None, None, "lat"),
    )
    out_specs = P("depth", None, None, "lat")
    return jax.shard_map(body, mesh=mesh, in_specs=in_specs, out_specs=out_specs, check_vma=False)
```

time: 71.5 us -> 54 us (0.76)
  Pallas kernels: 20.9 us -> 5.17 us
  waiting for transfers between devices: 18.8 us -> 23.5 us
  other arithmetic: 3.6 us -> 0.05 us
  starting transfers between devices: 22.8 us -> 19.9 us
    pallas_call x8 -> x9, Pallas kernels: 20.9 us -> 5.17 us  [call(): pl.pallas_call(kernel, out_shape=outs, in_specs=[SMEM] * scalars + [VMEM]...]
    ppermute x2, waiting for transfers between devices: 4.03 us -> 9.45 us  [shifted(): return lax.ppermute(value, 'depth', pairs)]
    ppermute x7, starting transfers between devices: 11 us -> 8.18 us  [swapped(): lax.ppermute(value, axis, [(k, k ^ bit) for k in range(lax.axis_size(axis...]
    add x2, other arithmetic: 1.47 us -> 0.02 us  [body(): entry = entry + swapped(entry, 'lat', bit)]
    another operation x2 -> x0, other arithmetic: 1.25 us -> none  [flags(): return jnp.stack([jnp.asarray(value).astype(jnp.int32) for value in values])]
    ppermute x7, waiting for transfers between devices: 13.6 us -> 12.5 us  [swapped(): lax.ppermute(value, axis, [(k, k ^ bit) for k in range(lax.axis_size(axis...]
    select_n x1, other arithmetic: 0.85 us -> 0.01 us  [body(): jnp.where(role == 0, up, down)]
    unnamed x16 -> x20, local copies, waits for them, and re-layouts: 4.05 us -> 4.18 us
  transfers between devices with their start and end apart: 10 -> 10, of which waited for: 9 -> 9; matrix products, arithmetic and copies ran while one was open for 4% -> 0% of each run, Pallas kernels for 13% -> 5%
where the time goes in v2:
time: 54 us; the launch traced here: 53.7 us
  waiting for transfers between devices  23.5 us (44%)
  starting transfers between devices  19.9 us (37%)
  Pallas kernels  5.17 us (10%)
  local copies, waits for them, and re-layouts  4.18 us (8%)
  between operations  0.84 us (2%)
    ppermute x7, waiting for transfers between devices, swapped(): lax.ppermute(value, axis, [(k, k ^ bit) for k in range(lax.axis_size(axis...  12.5 us
    ppermute x2, waiting for transfers between devices, shifted(): return lax.ppermute(value, 'depth', pairs)  9.45 us
    ppermute x7, starting transfers between devices, swapped(): lax.ppermute(value, axis, [(k, k ^ bit) for k in range(lax.axis_size(axis...  8.18 us
    ppermute x2, starting transfers between devices, shifted(): return lax.ppermute(value, 'depth', pairs)  6.99 us
    pallas_call x9, Pallas kernels, call(): pl.pallas_call(kernel, out_shape=outs, in_specs=[SMEM] * scalars + [VMEM]...  5.17 us
    ppermute x1, starting transfers between devices, body(): carry = lax.ppermute(total, ('depth', 'lat'), moves)  4.77 us
    unnamed x20, local copies, waits for them, and re-layouts  4.18 us
    ppermute x1, waiting for transfers between devices, body(): carry = lax.ppermute(total, ('depth', 'lat'), moves)  1.58 us
  transfers between devices with their start and end apart: 10, of which 9 were waited for; matrix products, arithmetic and copies ran while one was open for 0% of the time, Pallas kernels for 5%

profile of v2, /device:TPU:0, one launch (start us, length us, event | category | flops | bytes accessed | tf_op | source)
XLA Modules:
  0.0 53.7 jit_solution(377779712624662086)
XLA Ops:
  0.0 1.4 %collective-permute-start = (f32[128,1024]{1,0:T(8,128)}, f32[128,1024]{1,0:T(8,128)S(1)}, u32[]{:S(2)}, u32[]{:S(2)}) collective-permute-start(f32[128,1024]{1,0:T(8,128)} %bitcast.13), channel_id=1, source_target_pairs={{4,0},{8,4},{12,8},{16,12},{20,16},{24,20},{28,24},{5,1},{9,5},{13... | collective-permute-start | bytes 1572872 | tf_op jit(solution)/shard_map/ppermute | solution.py:199
  1.4 5.6 %collective-permute-start.3 = (f32[128,1024]{1,0:T(8,128)}, f32[128,1024]{1,0:T(8,128)S(1)}, u32[]{:S(2)}, u32[]{:S(2)}) collective-permute-start(f32[128,1024]{1,0:T(8,128)} %bitcast.15), channel_id=1, source_target_pairs={{0,4},{4,8},{8,12},{12,16},{16,20},{20,24},{24,28},{1,5},{5,9},{9,... | collective-permute-start | bytes 1572872 | tf_op jit(solution)/shard_map/ppermute | solution.py:199
  7.0 1.0 %copy-done.3 = f32[2,64,1024]{2,1,0:T(8,128)S(1)} copy-done((f32[2,64,1024]{2,1,0:T(8,128)S(1)}, f32[2,64,1024]{2,1,0:T(8,128)}, u32[]{:S(2)}) %copy-start.3) | copy-done | bytes 524312
  8.1 1.0 %copy-done.4 = f32[2,64,1024]{2,1,0:T(8,128)S(1)} copy-done((f32[2,64,1024]{2,1,0:T(8,128)S(1)}, f32[2,64,1024]{2,1,0:T(8,128)}, u32[]{:S(2)}) %copy-start.4) | copy-done | bytes 524312
  9.1 1.0 %copy-done.5 = f32[1,2,64,1024]{3,2,1,0:T(8,128)S(1)} copy-done((f32[1,2,64,1024]{3,2,1,0:T(8,128)S(1)}, f32[1,2,64,1024]{3,2,1,0:T(8,128)}, u32[]{:S(2)}) %copy-start.5) | copy-done | bytes 524312
  10.1 1.0 %copy-done.6 = f32[1,2,64,1024]{3,2,1,0:T(8,128)S(1)} copy-done((f32[1,2,64,1024]{3,2,1,0:T(8,128)S(1)}, f32[1,2,64,1024]{3,2,1,0:T(8,128)}, u32[]{:S(2)}) %copy-start.6) | copy-done | bytes 524312
  11.2 0.7 %shard_map.109 = f32[128,128]{1,0:T(8,128)S(1)} custom-call(f32[128,1024]{1,0:T(8,128)S(1)} %bitcast.14, f32[128,1024]{1,0:T(8,128)S(1)} %bitcast.16, f32[128,1024]{1,0:T(8,128)S(1)} %bitcast.11, f32[128,1024]{1,0:T(8,128)S(1)} %bitcast.12), custom_call_target="tpu_custom_call" | custom-call | tf_op jit(solution)/shard_map/pallas_call | solution.py:162
  11.8 0.1 collective-permute-start.1
  11.9 1.2 %collective-permute-done.1 = f32[128,128]{1,0:T(8,128)S(1)} collective-permute-done((f32[128,128]{1,0:T(8,128)S(1)}, f32[128,128]{1,0:T(8,128)S(1)}, u32[]{:S(2)}, u32[]{:S(2)}) %collective-permute-start.1) | collective-permute-done | bytes 65568 | tf_op jit(solution)/shard_map/ppermute | solution.py:202
  13.2 2.1 %collective-permute-start.2 = (f32[128,128]{1,0:T(8,128)S(1)}, f32[128,128]{1,0:T(8,128)S(1)}, u32[]{:S(2)}, u32[]{:S(2)}) collective-permute-start(f32[128,128]{1,0:T(8,128)S(1)} %add.12), channel_id=1, source_target_pairs={{0,2},{1,3},{2,0},{3,1},{4,6},{5,7},{6,4},{7,5},{8,10},{9,11},{10,... | collective-permute-start | bytes 196616 | tf_op jit(solution)/shard_map/ppermute | solution.py:202
  15.9 1.8 %collective-permute-done.2 = f32[128,128]{1,0:T(8,128)S(1)} collective-permute-done((f32[128,128]{1,0:T(8,128)S(1)}, f32[128,128]{1,0:T(8,128)S(1)}, u32[]{:S(2)}, u32[]{:S(2)}) %collective-permute-start.2) | collective-permute-done | bytes 65568 | tf_op jit(solution)/shard_map/ppermute | solution.py:202
  17.7 0.8 %shard_map.110 = (f32[128,1024]{1,0:T(8,128)S(1)}, bf16[2,2,256,1024]{3,2,1,0:T(8,128)(2,1)S(1)}) custom-call(s32[1]{0:T(128)S(6)} %copy.12.count_ref, s32[1,64]{1,0:T(1,128)S(1)} %copy-done.7, f32[128,1024]{1,0:T(8,128)S(1)} %bitcast.8, f32[128,1024]{1,0:T(8,128)S(1)} %bitcast.9, f32[128,1024]{1,0:T(8,128)S(1)} %bitcast.10, f32[1,64]{1,0:T(1,128)S(1)} %copy-done.8, ...), custom_call_target="tpu_custom_call" | custom-call | tf_op jit(solution)/shard_map/pallas_call | solution.py:162
  18.6 0.7 %shard_map.111 = f32[128,128]{1,0:T(8,128)S(1)} custom-call(f32[128,1024]{1,0:T(8,128)S(1)} %collective-permute-done.proj_ref, bf16[2,2,256,1024]{3,2,1,0:T(8,128)(2,1)S(1)} %get-tuple-element.9.left_ref), custom_call_target="tpu_custom_call" | custom-call | tf_op jit(solution)/shard_map/pallas_call | solution.py:162
  19.2 9.4 %collective-permute-done.3.proj_ref = f32[128,1024]{1,0:T(8,128)S(1)} collective-permute-done((f32[128,1024]{1,0:T(8,128)}, f32[128,1024]{1,0:T(8,128)S(1)}, u32[]{:S(2)}, u32[]{:S(2)}) %collective-permute-start.3) | collective-permute-done | bytes 524320 | tf_op jit(solution)/shard_map/ppermute | solution.py:199
  28.7 0.7 %shard_map.112 = f32[128,128]{1,0:T(8,128)S(1)} custom-call(f32[128,1024]{1,0:T(8,128)S(1)} %collective-permute-done.3.proj_ref, bf16[2,2,256,1024]{3,2,1,0:T(8,128)(2,1)S(1)} %get-tuple-element.9.left_ref), custom_call_target="tpu_custom_call" | custom-call | tf_op jit(solution)/shard_map/pallas_call | solution.py:162
  29.3 0.1 collective-permute-start.4
  29.4 1.2 %collective-permute-done.4 = f32[128,128]{1,0:T(8,128)S(1)} collective-permute-done((f32[128,128]{1,0:T(8,128)S(1)}, f32[128,128]{1,0:T(8,128)S(1)}, u32[]{:S(2)}, u32[]{:S(2)}) %collective-permute-start.4) | collective-permute-done | bytes 65568 | tf_op jit(solution)/shard_map/ppermute | solution.py:202
  30.7 1.6 %collective-permute-start.5 = (f32[128,128]{1,0:T(8,128)S(1)}, f32[128,128]{1,0:T(8,128)S(1)}, u32[]{:S(2)}, u32[]{:S(2)}) collective-permute-start(f32[128,128]{1,0:T(8,128)S(1)} %select_add_fusion), channel_id=1, source_target_pairs={{0,2},{1,3},{2,0},{3,1},{4,6},{5,7},{6,4},{7,5},{8,10},{9,11},{10,... | collective-permute-start | bytes 196616 | tf_op jit(solution)/shard_map/ppermute | solution.py:202
  32.2 2.8 %collective-permute-done.5 = f32[128,128]{1,0:T(8,128)S(1)} collective-permute-done((f32[128,128]{1,0:T(8,128)S(1)}, f32[128,128]{1,0:T(8,128)S(1)}, u32[]{:S(2)}, u32[]{:S(2)}) %collective-permute-start.5) | collective-permute-done | bytes 65568 | tf_op jit(solution)/shard_map/ppermute | solution.py:202
  35.0 2.4 %collective-permute-start.6 = (f32[128,128]{1,0:T(8,128)S(1)}, f32[128,128]{1,0:T(8,128)S(1)}, u32[]{:S(2)}, u32[]{:S(2)}) collective-permute-start(f32[128,128]{1,0:T(8,128)S(1)} %add.15.own_ref), channel_id=1, source_target_pairs={{0,4},{4,0},{8,12},{12,8},{16,20},{20,16},{24,28},{28,24},{1,5},{5... | collective-permute-start | bytes 196616 | tf_op jit(solution)/shard_map/ppermute | solution.py:202
  37.5 2.2 %collective-permute-done.6.other_ref = f32[128,128]{1,0:T(8,128)S(1)} collective-permute-done((f32[128,128]{1,0:T(8,128)S(1)}, f32[128,128]{1,0:T(8,128)S(1)}, u32[]{:S(2)}, u32[]{:S(2)}) %collective-permute-start.6) | collective-permute-done | bytes 65568 | tf_op jit(solution)/shard_map/ppermute | solution.py:202
  39.7 0.2 shard_map.113
  40.0 1.9 %collective-permute-start.7 = (f32[128,128]{1,0:T(8,128)S(1)}, f32[128,128]{1,0:T(8,128)S(1)}, u32[]{:S(2)}, u32[]{:S(2)}) collective-permute-start(f32[128,128]{1,0:T(8,128)S(1)} %get-tuple-element.10.own_ref), channel_id=1, source_target_pairs={{0,8},{4,12},{8,0},{12,4},{16,24},{20,28},{24,16},{28,20},{1,9},{5... | collective-permute-start | bytes 196616 | tf_op jit(solution)/shard_map/ppermute | solution.py:202
  41.9 2.4 %collective-permute-done.7.other_ref.gap_ref = f32[128,128]{1,0:T(8,128)S(1)} collective-permute-done((f32[128,128]{1,0:T(8,128)S(1)}, f32[128,128]{1,0:T(8,128)S(1)}, u32[]{:S(2)}, u32[]{:S(2)}) %collective-permute-start.7) | collective-permute-done | bytes 65568 | tf_op jit(solution)/shard_map/ppermute | solution.py:202
  44.3 0.2 shard_map.114
  44.5 4.8 %collective-permute-start.8 = (f32[64,128]{1,0:T(8,128)S(1)}, f32[64,128]{1,0:T(8,128)S(1)}, u32[]{:S(2)}, u32[]{:S(2)}) collective-permute-start(f32[64,128]{1,0:T(8,128)S(1)} %shard_map.114), channel_id=1, source_target_pairs={{0,16},{29,13},{2,18},{31,15},{4,20},{25,9},{6,22},{27,11},{8,24},... | collective-permute-start | bytes 98312 | tf_op jit(solution)/shard_map/ppermute | solution.py:261
  49.3 1.6 %collective-permute-done.8.carry_ref = f32[64,128]{1,0:T(8,128)S(1)} collective-permute-done((f32[64,128]{1,0:T(8,128)S(1)}, f32[64,128]{1,0:T(8,128)S(1)}, u32[]{:S(2)}, u32[]{:S(2)}) %collective-permute-start.8) | collective-permute-done | bytes 32800 | tf_op jit(solution)/shard_map/ppermute | solution.py:261
  50.9 0.4 shard_map.115.rows_ref
  51.2 0.1 collective-permute-start.9
  51.3 0.4 shard_map.116.sum_ref
  51.7 0.8 %collective-permute-done.9.rows_ref = f32[64,128]{1,0:T(8,128)S(1)} collective-permute-done((f32[64,128]{1,0:T(8,128)S(1)}, f32[64,128]{1,0:T(8,128)S(1)}, u32[]{:S(2)}, u32[]{:S(2)}) %collective-permute-start.9) | collective-permute-done | bytes 32800 | tf_op jit(solution)/shard_map/ppermute | solution.py:202
  52.5 1.2 %shard_map.117 = f32[128,1024]{1,0:T(8,128)} custom-call(f32[64,128]{1,0:T(8,128)S(1)} %collective-permute-done.9.rows_ref, bf16[2,2,256,1024]{3,2,1,0:T(8,128)(2,1)S(1)} %get-tuple-element.9.left_ref, f32[128,1024]{1,0:T(8,128)S(1)} %shard_map.116.sum_ref), custom_call_target="tpu_custom_call" | custom-call | tf_op jit(solution)/shard_map/pallas_call | solution.py:162
  (22 shorter events, 0.1 us)
Async XLA Ops:
  0.0 17.7 %copy-start = (f32[1,2,64,1024]{3,2,1,0:T(8,128)S(1)}, f32[1,2,64,1024]{3,2,1,0:T(8,128)}, u32[]{:S(2)}) copy-start(f32[1,2,64,1024]{3,2,1,0:T(8,128)} %param.11) | copy-start | bytes 1572868
  0.0 17.7 %copy-start.1 = (f32[1,2,64,1024]{3,2,1,0:T(8,128)S(1)}, f32[1,2,64,1024]{3,2,1,0:T(8,128)}, u32[]{:S(2)}) copy-start(f32[1,2,64,1024]{3,2,1,0:T(8,128)} %param.12) | copy-start | bytes 1572868
  0.0 17.7 %copy-start.2 = (f32[1,2,64,1024]{3,2,1,0:T(8,128)S(1)}, f32[1,2,64,1024]{3,2,1,0:T(8,128)}, u32[]{:S(2)}) copy-start(f32[1,2,64,1024]{3,2,1,0:T(8,128)} %param.14) | copy-start | bytes 1572868
  0.0 18.5 %collective-permute-start = (f32[128,1024]{1,0:T(8,128)}, f32[128,1024]{1,0:T(8,128)S(1)}, u32[]{:S(2)}, u32[]{:S(2)}) collective-permute-start(f32[128,1024]{1,0:T(8,128)} %bitcast.13), channel_id=1, source_target_pairs={{4,0},{8,4},{12,8},{16,12},{20,16},{24,20},{28,24},{5,1},{9,5},{13... | collective-permute-start | bytes 1572872 | tf_op jit(solution)/shard_map/ppermute | solution.py:199
  1.4 27.2 %collective-permute-start.3 = (f32[128,1024]{1,0:T(8,128)}, f32[128,1024]{1,0:T(8,128)S(1)}, u32[]{:S(2)}, u32[]{:S(2)}) collective-permute-start(f32[128,1024]{1,0:T(8,128)} %bitcast.15), channel_id=1, source_target_pairs={{0,4},{4,8},{8,12},{12,16},{16,20},{20,24},{24,28},{1,5},{5,9},{9,... | collective-permute-start | bytes 1572872 | tf_op jit(solution)/shard_map/ppermute | solution.py:199
  7.0 1.0 %copy-start.3 = (f32[2,64,1024]{2,1,0:T(8,128)S(1)}, f32[2,64,1024]{2,1,0:T(8,128)}, u32[]{:S(2)}) copy-start(f32[2,64,1024]{2,1,0:T(8,128)} %param.20) | copy-start | bytes 1572868
  8.1 1.0 %copy-start.4 = (f32[2,64,1024]{2,1,0:T(8,128)S(1)}, f32[2,64,1024]{2,1,0:T(8,128)}, u32[]{:S(2)}) copy-start(f32[2,64,1024]{2,1,0:T(8,128)} %param.21) | copy-start | bytes 1572868
  9.1 1.0 %copy-start.5 = (f32[1,2,64,1024]{3,2,1,0:T(8,128)S(1)}, f32[1,2,64,1024]{3,2,1,0:T(8,128)}, u32[]{:S(2)}) copy-start(f32[1,2,64,1024]{3,2,1,0:T(8,128)} %param.13) | copy-start | bytes 1572868
  10.1 1.0 %copy-start.6 = (f32[1,2,64,1024]{3,2,1,0:T(8,128)S(1)}, f32[1,2,64,1024]{3,2,1,0:T(8,128)}, u32[]{:S(2)}) copy-start(f32[1,2,64,1024]{3,2,1,0:T(8,128)} %param.15) | copy-start | bytes 1572868
  11.2 6.5 %copy-start.7 = (s32[1,64]{1,0:T(1,128)S(1)}, s32[1,64]{1,0:T(1,128)}, u32[]{:S(2)}) copy-start(s32[1,64]{1,0:T(1,128)} %list_ref.1) | copy-start | bytes 772
  11.2 6.5 %copy-start.8 = (f32[1,64]{1,0:T(1,128)S(1)}, f32[1,64]{1,0:T(1,128)}, u32[]{:S(2)}) copy-start(f32[1,64]{1,0:T(1,128)} %dd_ref.1) | copy-start | bytes 772
  11.2 6.5 %copy-start.9 = (f32[1,64]{1,0:T(1,128)S(1)}, f32[1,64]{1,0:T(1,128)}, u32[]{:S(2)}) copy-start(f32[1,64]{1,0:T(1,128)} %ud_ref.1) | copy-start | bytes 772
  11.8 1.3 %collective-permute-start.1 = (f32[128,128]{1,0:T(8,128)S(1)}, f32[128,128]{1,0:T(8,128)S(1)}, u32[]{:S(2)}, u32[]{:S(2)}) collective-permute-start(f32[128,128]{1,0:T(8,128)S(1)} %shard_map.109), channel_id=1, source_target_pairs={{0,1},{1,0},{2,3},{3,2},{4,5},{5,4},{6,7},{7,6},{8,9},{9,8},{10,11... | collective-permute-start | bytes 196616 | tf_op jit(solution)/shard_map/ppermute | solution.py:202
  13.2 4.5 %collective-permute-start.2 = (f32[128,128]{1,0:T(8,128)S(1)}, f32[128,128]{1,0:T(8,128)S(1)}, u32[]{:S(2)}, u32[]{:S(2)}) collective-permute-start(f32[128,128]{1,0:T(8,128)S(1)} %add.12), channel_id=1, source_target_pairs={{0,2},{1,3},{2,0},{3,1},{4,6},{5,7},{6,4},{7,5},{8,10},{9,11},{10,... | collective-permute-start | bytes 196616 | tf_op jit(solution)/shard_map/ppermute | solution.py:202
  29.3 1.3 %collective-permute-start.4 = (f32[128,128]{1,0:T(8,128)S(1)}, f32[128,128]{1,0:T(8,128)S(1)}, u32[]{:S(2)}, u32[]{:S(2)}) collective-permute-start(f32[128,128]{1,0:T(8,128)S(1)} %broadcast_select_fusion), channel_id=1, source_target_pairs={{0,1},{1,0},{2,3},{3,2},{4,5},{5,4},{6,7},{7,6},{8,9},{9,8},{10,11... | collective-permute-start | bytes 196616 | tf_op jit(solution)/shard_map/ppermute | solution.py:202
  30.7 4.3 %collective-permute-start.5 = (f32[128,128]{1,0:T(8,128)S(1)}, f32[128,128]{1,0:T(8,128)S(1)}, u32[]{:S(2)}, u32[]{:S(2)}) collective-permute-start(f32[128,128]{1,0:T(8,128)S(1)} %select_add_fusion), channel_id=1, source_target_pairs={{0,2},{1,3},{2,0},{3,1},{4,6},{5,7},{6,4},{7,5},{8,10},{9,11},{10,... | collective-permute-start | bytes 196616 | tf_op jit(solution)/shard_map/ppermute | solution.py:202
  35.0 4.7 %collective-permute-start.6 = (f32[128,128]{1,0:T(8,128)S(1)}, f32[128,128]{1,0:T(8,128)S(1)}, u32[]{:S(2)}, u32[]{:S(2)}) collective-permute-start(f32[128,128]{1,0:T(8,128)S(1)} %add.15.own_ref), channel_id=1, source_target_pairs={{0,4},{4,0},{8,12},{12,8},{16,20},{20,16},{24,28},{28,24},{1,5},{5... | collective-permute-start | bytes 196616 | tf_op jit(solution)/shard_map/ppermute | solution.py:202
  40.0 4.3 %collective-permute-start.7 = (f32[128,128]{1,0:T(8,128)S(1)}, f32[128,128]{1,0:T(8,128)S(1)}, u32[]{:S(2)}, u32[]{:S(2)}) collective-permute-start(f32[128,128]{1,0:T(8,128)S(1)} %get-tuple-element.10.own_ref), channel_id=1, source_target_pairs={{0,8},{4,12},{8,0},{12,4},{16,24},{20,28},{24,16},{28,20},{1,9},{5... | collective-permute-start | bytes 196616 | tf_op jit(solution)/shard_map/ppermute | solution.py:202
  44.5 6.4 %collective-permute-start.8 = (f32[64,128]{1,0:T(8,128)S(1)}, f32[64,128]{1,0:T(8,128)S(1)}, u32[]{:S(2)}, u32[]{:S(2)}) collective-permute-start(f32[64,128]{1,0:T(8,128)S(1)} %shard_map.114), channel_id=1, source_target_pairs={{0,16},{29,13},{2,18},{31,15},{4,20},{25,9},{6,22},{27,11},{8,24},... | collective-permute-start | bytes 98312 | tf_op jit(solution)/shard_map/ppermute | solution.py:261
  51.2 1.3 %collective-permute-start.9 = (f32[64,128]{1,0:T(8,128)S(1)}, f32[64,128]{1,0:T(8,128)S(1)}, u32[]{:S(2)}, u32[]{:S(2)}) collective-permute-start(f32[64,128]{1,0:T(8,128)S(1)} %shard_map.115.rows_ref), channel_id=1, source_target_pairs={{0,1},{1,0},{2,3},{3,2},{4,5},{5,4},{6,7},{7,6},{8,9},{9,8},{10,11... | collective-permute-start | bytes 98312 | tf_op jit(solution)/shard_map/ppermute | solution.py:202

commit v3 on v2

--- a/solution.py
+++ b/solution.py
@@ -140,22 +140,45 @@
     out_ref[...] = jnp.where(upper, longer, own)
 
 
-def final_kernel(carry_ref, gap_ref, near_ref, entry_ref, out_ref):
-    depth = lax.axis_size("depth")
+def prefix_kernel(half, near_ref, gap_ref, out_ref):
+    place = standing()[1]
+    near, gap = near_ref[...], gap_ref[...]
+    odd = lax.rem(place, 2) == 1
+    both = jnp.where(odd, compose(near, gap), gap)
+    out_ref[...] = jnp.where(lax.rem(place, half) >= 2, both, near)
+
+
+def final_kernel(half, carry_ref, prefix_ref, entry_ref, out_ref):
     role, place = standing()
     nsrc = carry_ref.shape[0]
-    carry = carry_ref[...]
-    carry = jnp.where(lax.rem(place, depth // 2) >= 2, advance(gap_ref[...], carry), carry)
-    carry = jnp.where(lax.rem(place, 2) == 1, advance(near_ref[...], carry), carry)
+    carry = jnp.where(place >= half, carry_ref[...], 0.0)
+    carry = jnp.where(lax.rem(place, half) > 0, advance(prefix_ref[...], carry), carry)
     entry = jnp.where(role == 0, entry_ref[:nsrc], entry_ref[nsrc:])
     out_ref[...] = jnp.where(place == 0, entry, carry)
 
 
-def expand_kernel(turn, rows_ref, left_ref, sum_ref, out_ref):
+def expanded(turn, rows_ref, left_ref, sum_ref, columns):
     role = lax.rem(standing()[0] + turn, 2)
     wide = rows_ref.shape[1]
-    basis = (left_ref[role, 0, :wide], left_ref[role, 1, :wide])
-    out_ref[...] = sum_ref[...] + dot3(split(spread(rows_ref[...])), basis, ROWS_COLS)
+    basis = (left_ref[role, 0, :wide, columns], left_ref[role, 1, :wide, columns])
+    return sum_ref[:, columns] + dot3(split(spread(rows_ref[...])), basis, ROWS_COLS)
+
+
+def expand_kernel(rows_ref, left_ref, sum_ref, out_ref):
+    out_ref[...] = expanded(0, rows_ref, left_ref, sum_ref, slice(None))
+
+
+def finish_kernel(rows_ref, left_ref, sum_ref, out_ref, held_ref, done):
+    chunks = done.shape[0]
+    width = held_ref.shape[1] // chunks
+    copies = []
+    for k in range(chunks):
+        columns = slice(k * width, (k + 1) * width)
+        held_ref[:, columns] = expanded(1, rows_ref, left_ref, sum_ref, columns)
+        copies.append(pltpu.make_async_copy(held_ref.at[:, columns], out_ref.at[:, columns], done.at[k]))
+        copies[-1].start()
+    for copy in copies:
+        copy.wait()
 
 
 def call(kernel, outs, *args, scalars=0, grant=4):
@@ -195,8 +218,7 @@
         return value.reshape(value.shape[-3] * value.shape[-2], value.shape[-1])
 
     def shifted(value, step):
-        pairs = [(k, k + step) for k in range(depth) if 0 <= k + step < depth]
-        return lax.ppermute(value, "depth", pairs)
+        return lax.ppermute(value, "depth", [(k, (k + step) % depth) for k in range(depth)])
 
     def swapped(value, axis, bit):
         return lax.ppermute(value, axis, [(k, k ^ bit) for k in range(lax.axis_size(axis))])
@@ -237,32 +259,40 @@
 
     down, up = gram(0, ahead), gram(1, behind)
     own = jnp.where(role == 0, down, up) + swapped(jnp.where(role == 0, up, down), "lat", 1)
-    bit = 2
+    bit = 4
     while bit < lat:
         own = own + swapped(own, "lat", bit)
         bit *= 2
-
-    near, total = call(pair_kernel, (element, element), own, swapped(own, "depth", 1))
+    other = swapped(own, "depth", 1)
+    if lat > 2:
+        across = [(g * lat + j, (g ^ 1) * lat + (j ^ 2)) for g in range(depth) for j in range(lat)]
+        other = other + lax.ppermute(own, ("depth", "lat"), across)
+        own = own + swapped(own, "lat", 2)
+
+    near, total = call(pair_kernel, (element, element), own, other)
     gap = near
-    reach = 2
-    while reach < depth // 2:
+    reach, half = 2, depth // 2
+    while reach < half:
         other = swapped(total, "depth", reach)
         gap = other if reach == 2 else call(functools.partial(gap_kernel, reach), element, gap, other)
-        last = reach * 2 >= depth // 2
+        last = reach * 2 >= half
         kernel = functools.partial(total_offset_kernel if last else total_kernel, reach)
         total = call(kernel, shape(nsrc, 2 * rank) if last else element, total, other)
         reach *= 2
-    half = depth // 2
-    moves = []
-    for k in range(half):
-        for j in range(lat):
-            low, high = (k, k + half) if j % 2 == 0 else (depth - 1 - k, half - 1 - k)
-            moves.append((low * lat + j, high * lat + j))
-    carry = lax.ppermute(total, ("depth", "lat"), moves)
-    coef = call(final_kernel, shape(nsrc, 2 * rank), carry, gap, near, entry)
+    carry = swapped(total, "depth", half)
+    prefix = call(functools.partial(prefix_kernel, half), element, near, gap)
+    coef = call(functools.partial(final_kernel, half), shape(nsrc, 2 * rank), carry, prefix, entry)
     wide = shape(2 * nsrc, width)
-    field = call(functools.partial(expand_kernel, 0), wide, coef, left, local)
-    field = call(functools.partial(expand_kernel, 1), wide, swapped(coef, "lat", 1), left, field)
+    field = call(expand_kernel, wide, coef, left, local)
+    chunks = 4
+    field = pl.pallas_call(
+        finish_kernel,
+        out_shape=wide,
+        in_specs=[VMEM] * 3,
+        out_specs=pl.BlockSpec(memory_space=pl.ANY),
+        scratch_shapes=[pltpu.VMEM(wide.shape, F32), pltpu.SemaphoreType.DMA((chunks,))],
+        compiler_params=pltpu.CompilerParams(vmem_limit_bytes=4 << 20),
+    )(swapped(coef, "lat", 1), left, field)
     return field.reshape(sources.shape)
 
 

time: 54 us -> 50.4 us (0.933)
  starting transfers between devices: 19.9 us -> 14.4 us
  waiting for transfers between devices: 23.5 us -> 25.5 us
    ppermute x3, starting transfers between devices: 11.8 us -> 6.13 us  [the longest x2 6.09 us: shifted(): lax.ppermute(value, 'depth', [(k, (k + step) % depth) for k in range(dept...]
    ppermute x7 -> x8, waiting for transfers between devices: 12.5 us -> 13.9 us  [swapped(): lax.ppermute(value, axis, [(k, k ^ bit) for k in range(lax.axis_size(axis...]
    pallas_call x0 -> x1, Pallas kernels: none -> 1.12 us  [body(): pl.pallas_call(finish_kernel, out_shape=wide, in_specs=[VMEM] * 3, out_sp...]
    pallas_call x9, Pallas kernels: 5.17 us -> 4.07 us  [call(): pl.pallas_call(kernel, out_shape=outs, in_specs=[SMEM] * scalars + [VMEM]...]
    ppermute x3, waiting for transfers between devices: 11 us -> 11.6 us  [the longest x2 8.93 us: shifted(): lax.ppermute(value, 'depth', [(k, (k + step) % depth) for k in range(dept...]
    ppermute x7 -> x8, starting transfers between devices: 8.18 us -> 8.25 us  [swapped(): lax.ppermute(value, axis, [(k, k ^ bit) for k in range(lax.axis_size(axis...]
  transfers between devices with their start and end apart: 10 -> 11, of which waited for: 9 -> 10; matrix products, arithmetic and copies ran while one was open for 0% -> 0% of each run, Pallas kernels for 5% -> 5%
where the time goes in v3:
time: 50.4 us; the launch traced here: 50.1 us
  waiting for transfers between devices  25.5 us (51%)
  starting transfers between devices  14.4 us (29%)
  Pallas kernels  5.19 us (10%)
  local copies, waits for them, and re-layouts  4.19 us (8%)
  between operations  0.84 us (2%)
    ppermute x8, waiting for transfers between devices, swapped(): lax.ppermute(value, axis, [(k, k ^ bit) for k in range(lax.axis_size(axis...  13.9 us
    ppermute x2, waiting for transfers between devices, shifted(): lax.ppermute(value, 'depth', [(k, (k + step) % depth) for k in range(dept...  8.93 us
    ppermute x8, starting transfers between devices, swapped(): lax.ppermute(value, axis, [(k, k ^ bit) for k in range(lax.axis_size(axis...  8.25 us
    ppermute x2, starting transfers between devices, shifted(): lax.ppermute(value, 'depth', [(k, (k + step) % depth) for k in range(dept...  6.09 us
    unnamed x20, local copies, waits for them, and re-layouts  4.19 us
    pallas_call x9, Pallas kernels, call(): pl.pallas_call(kernel, out_shape=outs, in_specs=[SMEM] * scalars + [VMEM]...  4.07 us
    ppermute x1, waiting for transfers between devices, body(): other = other + lax.ppermute(own, ('depth', 'lat'), across)  2.64 us
    pallas_call x1, Pallas kernels, body(): pl.pallas_call(finish_kernel, out_shape=wide, in_specs=[VMEM] * 3, out_sp...  1.12 us
  transfers between devices with their start and end apart: 11, of which 10 were waited for; matrix products, arithmetic and copies ran while one was open for 0% of the time, Pallas kernels for 5%

profile of v3, /device:TPU:0, one launch (start us, length us, event | category | flops | bytes accessed | tf_op | source)
XLA Modules:
  0.0 50.1 jit_solution(16700278760521585956)
XLA Ops:
  0.0 6.1 %collective-permute-start = (f32[128,1024]{1,0:T(8,128)}, f32[128,1024]{1,0:T(8,128)S(1)}, u32[]{:S(2)}, u32[]{:S(2)}) collective-permute-start(f32[128,1024]{1,0:T(8,128)} %bitcast.13), channel_id=1, source_target_pairs={{0,28},{4,0},{8,4},{12,8},{16,12},{20,16},{24,20},{28,24},{1,29},{... | collective-permute-start | bytes 1572872 | tf_op jit(solution)/shard_map/ppermute | solution.py:221
  6.1 1.0 %copy-done.3 = f32[2,64,1024]{2,1,0:T(8,128)S(1)} copy-done((f32[2,64,1024]{2,1,0:T(8,128)S(1)}, f32[2,64,1024]{2,1,0:T(8,128)}, u32[]{:S(2)}) %copy-start.3) | copy-done | bytes 524312
  7.1 1.0 %copy-done.4 = f32[2,64,1024]{2,1,0:T(8,128)S(1)} copy-done((f32[2,64,1024]{2,1,0:T(8,128)S(1)}, f32[2,64,1024]{2,1,0:T(8,128)}, u32[]{:S(2)}) %copy-start.4) | copy-done | bytes 524312
  8.2 1.0 %copy-done.5 = f32[1,2,64,1024]{3,2,1,0:T(8,128)S(1)} copy-done((f32[1,2,64,1024]{3,2,1,0:T(8,128)S(1)}, f32[1,2,64,1024]{3,2,1,0:T(8,128)}, u32[]{:S(2)}) %copy-start.5) | copy-done | bytes 524312
  9.2 1.0 %copy-done.6 = f32[1,2,64,1024]{3,2,1,0:T(8,128)S(1)} copy-done((f32[1,2,64,1024]{3,2,1,0:T(8,128)S(1)}, f32[1,2,64,1024]{3,2,1,0:T(8,128)}, u32[]{:S(2)}) %copy-start.6) | copy-done | bytes 524312
  10.3 0.7 %shard_map.109 = f32[128,128]{1,0:T(8,128)S(1)} custom-call(f32[128,1024]{1,0:T(8,128)S(1)} %bitcast.14, f32[128,1024]{1,0:T(8,128)S(1)} %bitcast.16, f32[128,1024]{1,0:T(8,128)S(1)} %bitcast.11, f32[128,1024]{1,0:T(8,128)S(1)} %bitcast.12), custom_call_target="tpu_custom_call" | custom-call | tf_op jit(solution)/shard_map/pallas_call | solution.py:185
  10.9 0.1 collective-permute-start.1
  11.0 1.2 %collective-permute-done.1 = f32[128,128]{1,0:T(8,128)S(1)} collective-permute-done((f32[128,128]{1,0:T(8,128)S(1)}, f32[128,128]{1,0:T(8,128)S(1)}, u32[]{:S(2)}, u32[]{:S(2)}) %collective-permute-start.1) | collective-permute-done | bytes 65568 | tf_op jit(solution)/shard_map/ppermute | solution.py:224
  12.3 1.6 %collective-permute-start.2 = (f32[128,128]{1,0:T(8,128)S(1)}, f32[128,128]{1,0:T(8,128)S(1)}, u32[]{:S(2)}, u32[]{:S(2)}) collective-permute-start(f32[128,128]{1,0:T(8,128)S(1)} %add.15), channel_id=1, source_target_pairs={{0,2},{1,3},{2,0},{3,1},{4,6},{5,7},{6,4},{7,5},{8,10},{9,11},{10,... | collective-permute-start | bytes 196616 | tf_op jit(solution)/shard_map/ppermute | solution.py:224
  14.5 2.1 %collective-permute-done.2 = f32[128,128]{1,0:T(8,128)S(1)} collective-permute-done((f32[128,128]{1,0:T(8,128)S(1)}, f32[128,128]{1,0:T(8,128)S(1)}, u32[]{:S(2)}, u32[]{:S(2)}) %collective-permute-start.2) | collective-permute-done | bytes 65568 | tf_op jit(solution)/shard_map/ppermute | solution.py:224
  16.7 0.8 %shard_map.110 = (f32[128,1024]{1,0:T(8,128)S(1)}, bf16[2,2,256,1024]{3,2,1,0:T(8,128)(2,1)S(1)}) custom-call(s32[1]{0:T(128)S(6)} %copy.12.count_ref, s32[1,64]{1,0:T(1,128)S(1)} %copy-done.7, f32[128,1024]{1,0:T(8,128)S(1)} %bitcast.8, f32[128,1024]{1,0:T(8,128)S(1)} %bitcast.9, f32[128,1024]{1,0:T(8,128)S(1)} %bitcast.10, f32[1,64]{1,0:T(1,128)S(1)} %copy-done.8, ...), custom_call_target="tpu_custom_call" | custom-call | tf_op jit(solution)/shard_map/pallas_call | solution.py:185
  17.5 8.9 %collective-permute-done.proj_ref = f32[128,1024]{1,0:T(8,128)S(1)} collective-permute-done((f32[128,1024]{1,0:T(8,128)}, f32[128,1024]{1,0:T(8,128)S(1)}, u32[]{:S(2)}, u32[]{:S(2)}) %collective-permute-start) | collective-permute-done | bytes 524320 | tf_op jit(solution)/shard_map/ppermute | solution.py:221
  26.4 0.7 %shard_map.111 = f32[128,128]{1,0:T(8,128)S(1)} custom-call(f32[128,1024]{1,0:T(8,128)S(1)} %collective-permute-done.proj_ref, bf16[2,2,256,1024]{3,2,1,0:T(8,128)(2,1)S(1)} %get-tuple-element.9.left_ref), custom_call_target="tpu_custom_call" | custom-call | tf_op jit(solution)/shard_map/pallas_call | solution.py:185
  27.1 0.7 %shard_map.112 = f32[128,128]{1,0:T(8,128)S(1)} custom-call(f32[128,1024]{1,0:T(8,128)S(1)} %collective-permute-done.3.proj_ref, bf16[2,2,256,1024]{3,2,1,0:T(8,128)(2,1)S(1)} %get-tuple-element.9.left_ref), custom_call_target="tpu_custom_call" | custom-call | tf_op jit(solution)/shard_map/pallas_call | solution.py:185
  27.9 1.2 %collective-permute-done.4 = f32[128,128]{1,0:T(8,128)S(1)} collective-permute-done((f32[128,128]{1,0:T(8,128)S(1)}, f32[128,128]{1,0:T(8,128)S(1)}, u32[]{:S(2)}, u32[]{:S(2)}) %collective-permute-start.4) | collective-permute-done | bytes 65568 | tf_op jit(solution)/shard_map/ppermute | solution.py:224
  29.1 1.8 %collective-permute-start.5 = (f32[128,128]{1,0:T(8,128)S(1)}, f32[128,128]{1,0:T(8,128)S(1)}, u32[]{:S(2)}, u32[]{:S(2)}) collective-permute-start(f32[128,128]{1,0:T(8,128)S(1)} %select_add_fusion), channel_id=1, source_target_pairs={{0,2},{1,3},{2,0},{3,1},{4,6},{5,7},{6,4},{7,5},{8,10},{9,11},{10,... | collective-permute-start | bytes 196616 | tf_op jit(solution)/shard_map/ppermute | solution.py:224
  30.9 1.7 %collective-permute-start.6 = (f32[128,128]{1,0:T(8,128)S(1)}, f32[128,128]{1,0:T(8,128)S(1)}, u32[]{:S(2)}, u32[]{:S(2)}) collective-permute-start(f32[128,128]{1,0:T(8,128)S(1)} %select_add_fusion), channel_id=1, source_target_pairs={{0,4},{4,0},{8,12},{12,8},{16,20},{20,16},{24,28},{28,24},{1,5},{5... | collective-permute-start | bytes 196616 | tf_op jit(solution)/shard_map/ppermute | solution.py:224
  32.7 0.8 %collective-permute-done.5 = f32[128,128]{1,0:T(8,128)S(1)} collective-permute-done((f32[128,128]{1,0:T(8,128)S(1)}, f32[128,128]{1,0:T(8,128)S(1)}, u32[]{:S(2)}, u32[]{:S(2)}) %collective-permute-start.5) | collective-permute-done | bytes 65568 | tf_op jit(solution)/shard_map/ppermute | solution.py:224
  33.5 1.7 %collective-permute-done.6 = f32[128,128]{1,0:T(8,128)S(1)} collective-permute-done((f32[128,128]{1,0:T(8,128)S(1)}, f32[128,128]{1,0:T(8,128)S(1)}, u32[]{:S(2)}, u32[]{:S(2)}) %collective-permute-start.6) | collective-permute-done | bytes 65568 | tf_op jit(solution)/shard_map/ppermute | solution.py:224
  35.2 2.6 %collective-permute-done.7 = f32[128,128]{1,0:T(8,128)S(1)} collective-permute-done((f32[128,128]{1,0:T(8,128)S(1)}, f32[128,128]{1,0:T(8,128)S(1)}, u32[]{:S(2)}, u32[]{:S(2)}) %collective-permute-start.7) | collective-permute-done | bytes 65568 | tf_op jit(solution)/shard_map/ppermute | solution.py:269
  37.8 0.2 shard_map.113
  38.1 1.0 %collective-permute-start.8 = (f32[128,128]{1,0:T(8,128)S(1)}, f32[128,128]{1,0:T(8,128)S(1)}, u32[]{:S(2)}, u32[]{:S(2)}) collective-permute-start(f32[128,128]{1,0:T(8,128)S(1)} %get-tuple-element.10.own_ref), channel_id=1, source_target_pairs={{0,8},{4,12},{8,0},{12,4},{16,24},{20,28},{24,16},{28,20},{1,9},{5... | collective-permute-start | bytes 196616 | tf_op jit(solution)/shard_map/ppermute | solution.py:224
  39.0 3.4 %collective-permute-done.8.other_ref.gap_ref = f32[128,128]{1,0:T(8,128)S(1)} collective-permute-done((f32[128,128]{1,0:T(8,128)S(1)}, f32[128,128]{1,0:T(8,128)S(1)}, u32[]{:S(2)}, u32[]{:S(2)}) %collective-permute-start.8) | collective-permute-done | bytes 65568 | tf_op jit(solution)/shard_map/ppermute | solution.py:224
  42.4 0.2 shard_map.114
  42.6 2.0 %collective-permute-start.9 = (f32[64,128]{1,0:T(8,128)S(1)}, f32[64,128]{1,0:T(8,128)S(1)}, u32[]{:S(2)}, u32[]{:S(2)}) collective-permute-start(f32[64,128]{1,0:T(8,128)S(1)} %shard_map.114), channel_id=1, source_target_pairs={{0,16},{4,20},{8,24},{12,28},{16,0},{20,4},{24,8},{28,12},{1,17},{... | collective-permute-start | bytes 98312 | tf_op jit(solution)/shard_map/ppermute | solution.py:224
  44.6 0.2 shard_map.115.prefix_ref
  44.8 2.7 %collective-permute-done.9.carry_ref = f32[64,128]{1,0:T(8,128)S(1)} collective-permute-done((f32[64,128]{1,0:T(8,128)S(1)}, f32[64,128]{1,0:T(8,128)S(1)}, u32[]{:S(2)}, u32[]{:S(2)}) %collective-permute-start.9) | collective-permute-done | bytes 32800 | tf_op jit(solution)/shard_map/ppermute | solution.py:224
  47.5 0.2 shard_map.116.rows_ref
  47.7 0.1 collective-permute-start.10
  47.8 0.4 shard_map.117.sum_ref
  48.2 0.8 %collective-permute-done.10.rows_ref = f32[64,128]{1,0:T(8,128)S(1)} collective-permute-done((f32[64,128]{1,0:T(8,128)S(1)}, f32[64,128]{1,0:T(8,128)S(1)}, u32[]{:S(2)}, u32[]{:S(2)}) %collective-permute-start.10) | collective-permute-done | bytes 32800 | tf_op jit(solution)/shard_map/ppermute | solution.py:224
  49.0 1.1 %shard_map.118 = f32[128,1024]{1,0:T(8,128)} custom-call(f32[64,128]{1,0:T(8,128)S(1)} %collective-permute-done.10.rows_ref, bf16[2,2,256,1024]{3,2,1,0:T(8,128)(2,1)S(1)} %get-tuple-element.9.left_ref, f32[128,1024]{1,0:T(8,128)S(1)} %shard_map.117.sum_ref), custom_call_target="tpu_custom_call" | custom-call | tf_op jit(solution)/shard_map/pallas_call | solution.py:288
  (26 shorter events, 0.2 us)
Async XLA Ops:
  0.0 16.6 %copy-start = (f32[1,2,64,1024]{3,2,1,0:T(8,128)S(1)}, f32[1,2,64,1024]{3,2,1,0:T(8,128)}, u32[]{:S(2)}) copy-start(f32[1,2,64,1024]{3,2,1,0:T(8,128)} %param.11) | copy-start | bytes 1572868
  0.0 16.6 %copy-start.1 = (f32[1,2,64,1024]{3,2,1,0:T(8,128)S(1)}, f32[1,2,64,1024]{3,2,1,0:T(8,128)}, u32[]{:S(2)}) copy-start(f32[1,2,64,1024]{3,2,1,0:T(8,128)} %param.12) | copy-start | bytes 1572868
  0.0 16.6 %copy-start.2 = (f32[1,2,64,1024]{3,2,1,0:T(8,128)S(1)}, f32[1,2,64,1024]{3,2,1,0:T(8,128)}, u32[]{:S(2)}) copy-start(f32[1,2,64,1024]{3,2,1,0:T(8,128)} %param.14) | copy-start | bytes 1572868
  0.0 26.4 %collective-permute-start = (f32[128,1024]{1,0:T(8,128)}, f32[128,1024]{1,0:T(8,128)S(1)}, u32[]{:S(2)}, u32[]{:S(2)}) collective-permute-start(f32[128,1024]{1,0:T(8,128)} %bitcast.13), channel_id=1, source_target_pairs={{0,28},{4,0},{8,4},{12,8},{16,12},{20,16},{24,20},{28,24},{1,29},{... | collective-permute-start | bytes 1572872 | tf_op jit(solution)/shard_map/ppermute | solution.py:221
  6.1 21.0 %collective-permute-start.3 = (f32[128,1024]{1,0:T(8,128)}, f32[128,1024]{1,0:T(8,128)S(1)}, u32[]{:S(2)}, u32[]{:S(2)}) collective-permute-start(f32[128,1024]{1,0:T(8,128)} %bitcast.15), channel_id=1, source_target_pairs={{0,4},{4,8},{8,12},{12,16},{16,20},{20,24},{24,28},{28,0},{1,5},{5... | collective-permute-start | bytes 1572872 | tf_op jit(solution)/shard_map/ppermute | solution.py:221
  6.1 1.0 %copy-start.3 = (f32[2,64,1024]{2,1,0:T(8,128)S(1)}, f32[2,64,1024]{2,1,0:T(8,128)}, u32[]{:S(2)}) copy-start(f32[2,64,1024]{2,1,0:T(8,128)} %param.20) | copy-start | bytes 1572868
  7.1 1.0 %copy-start.4 = (f32[2,64,1024]{2,1,0:T(8,128)S(1)}, f32[2,64,1024]{2,1,0:T(8,128)}, u32[]{:S(2)}) copy-start(f32[2,64,1024]{2,1,0:T(8,128)} %param.21) | copy-start | bytes 1572868
  8.2 1.0 %copy-start.5 = (f32[1,2,64,1024]{3,2,1,0:T(8,128)S(1)}, f32[1,2,64,1024]{3,2,1,0:T(8,128)}, u32[]{:S(2)}) copy-start(f32[1,2,64,1024]{3,2,1,0:T(8,128)} %param.13) | copy-start | bytes 1572868
  9.2 1.0 %copy-start.6 = (f32[1,2,64,1024]{3,2,1,0:T(8,128)S(1)}, f32[1,2,64,1024]{3,2,1,0:T(8,128)}, u32[]{:S(2)}) copy-start(f32[1,2,64,1024]{3,2,1,0:T(8,128)} %param.15) | copy-start | bytes 1572868
  10.3 6.4 %copy-start.7 = (s32[1,64]{1,0:T(1,128)S(1)}, s32[1,64]{1,0:T(1,128)}, u32[]{:S(2)}) copy-start(s32[1,64]{1,0:T(1,128)} %list_ref.1) | copy-start | bytes 772
  10.3 6.4 %copy-start.8 = (f32[1,64]{1,0:T(1,128)S(1)}, f32[1,64]{1,0:T(1,128)}, u32[]{:S(2)}) copy-start(f32[1,64]{1,0:T(1,128)} %dd_ref.1) | copy-start | bytes 772
  10.3 6.4 %copy-start.9 = (f32[1,64]{1,0:T(1,128)S(1)}, f32[1,64]{1,0:T(1,128)}, u32[]{:S(2)}) copy-start(f32[1,64]{1,0:T(1,128)} %ud_ref.1) | copy-start | bytes 772
  10.9 1.3 %collective-permute-start.1 = (f32[128,128]{1,0:T(8,128)S(1)}, f32[128,128]{1,0:T(8,128)S(1)}, u32[]{:S(2)}, u32[]{:S(2)}) collective-permute-start(f32[128,128]{1,0:T(8,128)S(1)} %shard_map.109), channel_id=1, source_target_pairs={{0,1},{1,0},{2,3},{3,2},{4,5},{5,4},{6,7},{7,6},{8,9},{9,8},{10,11... | collective-permute-start | bytes 196616 | tf_op jit(solution)/shard_map/ppermute | solution.py:224
  12.3 4.3 %collective-permute-start.2 = (f32[128,128]{1,0:T(8,128)S(1)}, f32[128,128]{1,0:T(8,128)S(1)}, u32[]{:S(2)}, u32[]{:S(2)}) collective-permute-start(f32[128,128]{1,0:T(8,128)S(1)} %add.15), channel_id=1, source_target_pairs={{0,2},{1,3},{2,0},{3,1},{4,6},{5,7},{6,4},{7,5},{8,10},{9,11},{10,... | collective-permute-start | bytes 196616 | tf_op jit(solution)/shard_map/ppermute | solution.py:224
  27.8 1.3 %collective-permute-start.4 = (f32[128,128]{1,0:T(8,128)S(1)}, f32[128,128]{1,0:T(8,128)S(1)}, u32[]{:S(2)}, u32[]{:S(2)}) collective-permute-start(f32[128,128]{1,0:T(8,128)S(1)} %broadcast_select_fusion), channel_id=1, source_target_pairs={{0,1},{1,0},{2,3},{3,2},{4,5},{5,4},{6,7},{7,6},{8,9},{9,8},{10,11... | collective-permute-start | bytes 196616 | tf_op jit(solution)/shard_map/ppermute | solution.py:224
  29.1 4.3 %collective-permute-start.5 = (f32[128,128]{1,0:T(8,128)S(1)}, f32[128,128]{1,0:T(8,128)S(1)}, u32[]{:S(2)}, u32[]{:S(2)}) collective-permute-start(f32[128,128]{1,0:T(8,128)S(1)} %select_add_fusion), channel_id=1, source_target_pairs={{0,2},{1,3},{2,0},{3,1},{4,6},{5,7},{6,4},{7,5},{8,10},{9,11},{10,... | collective-permute-start | bytes 196616 | tf_op jit(solution)/shard_map/ppermute | solution.py:224
  30.9 4.3 %collective-permute-start.6 = (f32[128,128]{1,0:T(8,128)S(1)}, f32[128,128]{1,0:T(8,128)S(1)}, u32[]{:S(2)}, u32[]{:S(2)}) collective-permute-start(f32[128,128]{1,0:T(8,128)S(1)} %select_add_fusion), channel_id=1, source_target_pairs={{0,4},{4,0},{8,12},{12,8},{16,20},{20,16},{24,28},{28,24},{1,5},{5... | collective-permute-start | bytes 196616 | tf_op jit(solution)/shard_map/ppermute | solution.py:224
  32.6 5.2 %collective-permute-start.7 = (f32[128,128]{1,0:T(8,128)S(1)}, f32[128,128]{1,0:T(8,128)S(1)}, u32[]{:S(2)}, u32[]{:S(2)}) collective-permute-start(f32[128,128]{1,0:T(8,128)S(1)} %select_add_fusion), channel_id=1, source_target_pairs={{0,6},{1,7},{2,4},{3,5},{4,2},{5,3},{6,0},{7,1},{8,14},{9,15},{10,... | collective-permute-start | bytes 196616 | tf_op jit(solution)/shard_map/ppermute | solution.py:269
  38.1 4.3 %collective-permute-start.8 = (f32[128,128]{1,0:T(8,128)S(1)}, f32[128,128]{1,0:T(8,128)S(1)}, u32[]{:S(2)}, u32[]{:S(2)}) collective-permute-start(f32[128,128]{1,0:T(8,128)S(1)} %get-tuple-element.10.own_ref), channel_id=1, source_target_pairs={{0,8},{4,12},{8,0},{12,4},{16,24},{20,28},{24,16},{28,20},{1,9},{5... | collective-permute-start | bytes 196616 | tf_op jit(solution)/shard_map/ppermute | solution.py:224
  42.6 4.9 %collective-permute-start.9 = (f32[64,128]{1,0:T(8,128)S(1)}, f32[64,128]{1,0:T(8,128)S(1)}, u32[]{:S(2)}, u32[]{:S(2)}) collective-permute-start(f32[64,128]{1,0:T(8,128)S(1)} %shard_map.114), channel_id=1, source_target_pairs={{0,16},{4,20},{8,24},{12,28},{16,0},{20,4},{24,8},{28,12},{1,17},{... | collective-permute-start | bytes 98312 | tf_op jit(solution)/shard_map/ppermute | solution.py:224
  47.7 1.3 %collective-permute-start.10 = (f32[64,128]{1,0:T(8,128)S(1)}, f32[64,128]{1,0:T(8,128)S(1)}, u32[]{:S(2)}, u32[]{:S(2)}) collective-permute-start(f32[64,128]{1,0:T(8,128)S(1)} %shard_map.116.rows_ref), channel_id=1, source_target_pairs={{0,1},{1,0},{2,3},{3,2},{4,5},{5,4},{6,7},{7,6},{8,9},{9,8},{10,11... | collective-permute-start | bytes 98312 | tf_op jit(solution)/shard_map/ppermute | solution.py:224

commit v4 on v3

--- a/solution.py
+++ b/solution.py
@@ -18,15 +18,19 @@
     return high, (value - high.astype(F32)).astype(BF16)
 
 
+ROWS_COLS = ((1,), (0,))
+ROWS_ROWS = ((1,), (1,))
+
+
 def dot3(left, right, dims):
     def prod(a, b):
         return lax.dot_general(a, b, (dims, ((), ())), preferred_element_type=F32)
 
-    return prod(left[0], right[0]) + (prod(left[0], right[1]) + prod(left[1], right[0]))
-
-
-ROWS_COLS = ((1,), (0,))
-ROWS_ROWS = ((1,), (1,))
+    if dims == ROWS_COLS:
+        return prod(jnp.concatenate([left[0], left[0], left[1]], 1), jnp.concatenate([right[0], right[1], right[0]], 0))
+    count = right[0].shape[0]
+    both = prod(left[0], jnp.concatenate(right, 0))
+    return both[:, :count] + (both[:, count:] + prod(left[1], right[0]))
 
 
 def turned(value):
@@ -65,9 +69,16 @@
     return apply_map(rows, step) + step[rank:]
 
 
+def parity(value):
+    odd = value & 1
+    for bit in range(1, 16):
+        odd = odd ^ ((value >> bit) & 1)
+    return odd
+
+
 def standing():
     group, depth = lax.axis_index("depth"), lax.axis_size("depth")
-    role = lax.rem(lax.axis_index("lat"), 2)
+    role = parity(group ^ lax.axis_index("lat"))
     return role, jnp.where(role == 0, group, depth - 1 - group)
 
 
@@ -211,7 +222,7 @@
     nsrc, width = sources.shape[2:]
     rank = down_expand.shape[2]
     depth, lat = lax.axis_size("depth"), lax.axis_size("lat")
-    role = lax.rem(lax.axis_index("lat"), 2)
+    role = standing()[0]
     element = shape(rank + nsrc, 2 * rank)
 
     def flat(value):
@@ -220,8 +231,12 @@
     def shifted(value, step):
         return lax.ppermute(value, "depth", [(k, (k + step) % depth) for k in range(depth)])
 
-    def swapped(value, axis, bit):
-        return lax.ppermute(value, axis, [(k, k ^ bit) for k in range(lax.axis_size(axis))])
+    def swapped(value, deep, wide):
+        pairs = [(g * lat + j, (g ^ deep) * lat + (j ^ wide)) for g in range(depth) for j in range(lat)]
+        return lax.ppermute(value, ("depth", "lat"), pairs)
+
+    def met(value, deep, wide):
+        return swapped(value, deep, wide ^ parity(deep ^ wide))
 
     ahead = shifted(flat(down_project), -1)
     behind = shifted(flat(up_project), 1)
@@ -237,7 +252,7 @@
     )
     bit = 1
     while bit < lat:
-        entry = entry + swapped(entry, "lat", bit)
+        entry = entry + swapped(entry, 0, bit)
         bit *= 2
     local, left = call(
         prepare_kernel,
@@ -258,28 +273,27 @@
         return call(functools.partial(gram_kernel, which), element, proj, left)
 
     down, up = gram(0, ahead), gram(1, behind)
-    own = jnp.where(role == 0, down, up) + swapped(jnp.where(role == 0, up, down), "lat", 1)
+    own = jnp.where(role == 0, down, up) + swapped(jnp.where(role == 0, up, down), 0, 1)
     bit = 4
     while bit < lat:
-        own = own + swapped(own, "lat", bit)
+        own = own + met(own, 0, bit)
         bit *= 2
-    other = swapped(own, "depth", 1)
+    other = met(own, 1, 0)
     if lat > 2:
-        across = [(g * lat + j, (g ^ 1) * lat + (j ^ 2)) for g in range(depth) for j in range(lat)]
-        other = other + lax.ppermute(own, ("depth", "lat"), across)
-        own = own + swapped(own, "lat", 2)
+        other = other + met(own, 1, 2)
+        own = own + met(own, 0, 2)
 
     near, total = call(pair_kernel, (element, element), own, other)
     gap = near
     reach, half = 2, depth // 2
     while reach < half:
-        other = swapped(total, "depth", reach)
+        other = met(total, reach, 0)
         gap = other if reach == 2 else call(functools.partial(gap_kernel, reach), element, gap, other)
         last = reach * 2 >= half
         kernel = functools.partial(total_offset_kernel if last else total_kernel, reach)
         total = call(kernel, shape(nsrc, 2 * rank) if last else element, total, other)
         reach *= 2
-    carry = swapped(total, "depth", half)
+    carry = met(total, half, 0)
     prefix = call(functools.partial(prefix_kernel, half), element, near, gap)
     coef = call(functools.partial(final_kernel, half), shape(nsrc, 2 * rank), carry, prefix, entry)
     wide = shape(2 * nsrc, width)
@@ -292,7 +306,7 @@
         out_specs=pl.BlockSpec(memory_space=pl.ANY),
         scratch_shapes=[pltpu.VMEM(wide.shape, F32), pltpu.SemaphoreType.DMA((chunks,))],
         compiler_params=pltpu.CompilerParams(vmem_limit_bytes=4 << 20),
-    )(swapped(coef, "lat", 1), left, field)
+    )(swapped(coef, 0, 1), left, field)
     return field.reshape(sources.shape)
 
 

time: 50.4 us -> 49.6 us (0.984)
  waiting for transfers between devices: 25.5 us -> 24.7 us
    ppermute x9, waiting for transfers between devices: 16.5 us -> 14.8 us  [swapped(): return lax.ppermute(value, ('depth', 'lat'), pairs)]
    ppermute x2, waiting for transfers between devices: 8.93 us -> 9.89 us  [shifted(): lax.ppermute(value, 'depth', [(k, (k + step) % depth) for k in range(dept...]
  transfers between devices with their start and end apart: 11 -> 11, of which waited for: 10 -> 11; matrix products, arithmetic and copies ran while one was open for 0% -> 0% of each run, Pallas kernels for 5% -> 5%
where the time goes in v4:
time: 49.6 us; the launch traced here: 49.3 us
  waiting for transfers between devices  24.7 us (50%)
  starting transfers between devices  14.7 us (30%)
  Pallas kernels  4.79 us (10%)
  local copies, waits for them, and re-layouts  4.19 us (8%)
  between operations  0.84 us (2%)
    ppermute x9, waiting for transfers between devices, swapped(): return lax.ppermute(value, ('depth', 'lat'), pairs)  14.8 us
    ppermute x2, waiting for transfers between devices, shifted(): lax.ppermute(value, 'depth', [(k, (k + step) % depth) for k in range(dept...  9.89 us
    ppermute x9, starting transfers between devices, swapped(): return lax.ppermute(value, ('depth', 'lat'), pairs)  8.59 us
    ppermute x2, starting transfers between devices, shifted(): lax.ppermute(value, 'depth', [(k, (k + step) % depth) for k in range(dept...  6.15 us
    unnamed x20, local copies, waits for them, and re-layouts  4.19 us
    pallas_call x9, Pallas kernels, call(): pl.pallas_call(kernel, out_shape=outs, in_specs=[SMEM] * scalars + [VMEM]...  3.7 us
    pallas_call x1, Pallas kernels, body(): pl.pallas_call(finish_kernel, out_shape=wide, in_specs=[VMEM] * 3, out_sp...  1.09 us
  transfers between devices with their start and end apart: 11, of which 11 were waited for; matrix products, arithmetic and copies ran while one was open for 0% of the time, Pallas kernels for 5%

profile of v4, /device:TPU:0, one launch (start us, length us, event | category | flops | bytes accessed | tf_op | source)
XLA Modules:
  0.0 49.3 jit_solution(14642696711681044893)
XLA Ops:
  0.0 3.0 %collective-permute-start.3 = (f32[128,1024]{1,0:T(8,128)}, f32[128,1024]{1,0:T(8,128)S(1)}, u32[]{:S(2)}, u32[]{:S(2)}) collective-permute-start(f32[128,1024]{1,0:T(8,128)} %bitcast.13), channel_id=1, source_target_pairs={{0,4},{4,8},{8,12},{12,16},{16,20},{20,24},{24,28},{28,0},{1,5},{5... | collective-permute-start | bytes 1572872 | tf_op jit(solution)/shard_map/ppermute | solution.py:232
  3.1 3.1 %collective-permute-start = (f32[128,1024]{1,0:T(8,128)}, f32[128,1024]{1,0:T(8,128)S(1)}, u32[]{:S(2)}, u32[]{:S(2)}) collective-permute-start(f32[128,1024]{1,0:T(8,128)} %bitcast.15), channel_id=1, source_target_pairs={{0,28},{4,0},{8,4},{12,8},{16,12},{20,16},{24,20},{28,24},{1,29},{... | collective-permute-start | bytes 1572872 | tf_op jit(solution)/shard_map/ppermute | solution.py:232
  6.2 1.0 %copy-done.3 = f32[2,64,1024]{2,1,0:T(8,128)S(1)} copy-done((f32[2,64,1024]{2,1,0:T(8,128)S(1)}, f32[2,64,1024]{2,1,0:T(8,128)}, u32[]{:S(2)}) %copy-start.3) | copy-done | bytes 524312
  7.2 1.0 %copy-done.4 = f32[2,64,1024]{2,1,0:T(8,128)S(1)} copy-done((f32[2,64,1024]{2,1,0:T(8,128)S(1)}, f32[2,64,1024]{2,1,0:T(8,128)}, u32[]{:S(2)}) %copy-start.4) | copy-done | bytes 524312
  8.2 1.0 %copy-done.5 = f32[1,2,64,1024]{3,2,1,0:T(8,128)S(1)} copy-done((f32[1,2,64,1024]{3,2,1,0:T(8,128)S(1)}, f32[1,2,64,1024]{3,2,1,0:T(8,128)}, u32[]{:S(2)}) %copy-start.5) | copy-done | bytes 524312
  9.3 1.0 %copy-done.6 = f32[1,2,64,1024]{3,2,1,0:T(8,128)S(1)} copy-done((f32[1,2,64,1024]{3,2,1,0:T(8,128)S(1)}, f32[1,2,64,1024]{3,2,1,0:T(8,128)}, u32[]{:S(2)}) %copy-start.6) | copy-done | bytes 524312
  10.3 0.7 %shard_map.109 = f32[128,128]{1,0:T(8,128)S(1)} custom-call(f32[128,1024]{1,0:T(8,128)S(1)} %bitcast.16, f32[128,1024]{1,0:T(8,128)S(1)} %bitcast.14, f32[128,1024]{1,0:T(8,128)S(1)} %bitcast.11, f32[128,1024]{1,0:T(8,128)S(1)} %bitcast.12), custom_call_target="tpu_custom_call" | custom-call | tf_op jit(solution)/shard_map/pallas_call | solution.py:196
  11.1 1.2 %collective-permute-done.1 = f32[128,128]{1,0:T(8,128)S(1)} collective-permute-done((f32[128,128]{1,0:T(8,128)S(1)}, f32[128,128]{1,0:T(8,128)S(1)}, u32[]{:S(2)}, u32[]{:S(2)}) %collective-permute-start.1) | collective-permute-done | bytes 65568 | tf_op jit(solution)/shard_map/ppermute | solution.py:236
  12.4 1.7 %collective-permute-start.2 = (f32[128,128]{1,0:T(8,128)S(1)}, f32[128,128]{1,0:T(8,128)S(1)}, u32[]{:S(2)}, u32[]{:S(2)}) collective-permute-start(f32[128,128]{1,0:T(8,128)S(1)} %add.15), channel_id=1, source_target_pairs={{0,2},{1,3},{2,0},{3,1},{4,6},{5,7},{6,4},{7,5},{8,10},{9,11},{10,... | collective-permute-start | bytes 196616 | tf_op jit(solution)/shard_map/ppermute | solution.py:236
  14.7 2.0 %collective-permute-done.2 = f32[128,128]{1,0:T(8,128)S(1)} collective-permute-done((f32[128,128]{1,0:T(8,128)S(1)}, f32[128,128]{1,0:T(8,128)S(1)}, u32[]{:S(2)}, u32[]{:S(2)}) %collective-permute-start.2) | collective-permute-done | bytes 65568 | tf_op jit(solution)/shard_map/ppermute | solution.py:236
  16.8 0.7 %shard_map.110 = (f32[128,1024]{1,0:T(8,128)S(1)}, bf16[2,2,256,1024]{3,2,1,0:T(8,128)(2,1)S(1)}) custom-call(s32[1]{0:T(128)S(6)} %copy.12.count_ref, s32[1,64]{1,0:T(1,128)S(1)} %copy-done.7, f32[128,1024]{1,0:T(8,128)S(1)} %bitcast.8, f32[128,1024]{1,0:T(8,128)S(1)} %bitcast.9, f32[128,1024]{1,0:T(8,128)S(1)} %bitcast.10, f32[1,64]{1,0:T(1,128)S(1)} %copy-done.8, ...), custom_call_target="tpu_custom_call" | custom-call | tf_op jit(solution)/shard_map/pallas_call | solution.py:196
  17.5 8.3 %collective-permute-done.3.proj_ref = f32[128,1024]{1,0:T(8,128)S(1)} collective-permute-done((f32[128,1024]{1,0:T(8,128)}, f32[128,1024]{1,0:T(8,128)S(1)}, u32[]{:S(2)}, u32[]{:S(2)}) %collective-permute-start.3) | collective-permute-done | bytes 524320 | tf_op jit(solution)/shard_map/ppermute | solution.py:232
  25.8 0.5 %shard_map.112 = f32[128,128]{1,0:T(8,128)S(1)} custom-call(f32[128,1024]{1,0:T(8,128)S(1)} %collective-permute-done.3.proj_ref, bf16[2,2,256,1024]{3,2,1,0:T(8,128)(2,1)S(1)} %get-tuple-element.9.left_ref), custom_call_target="tpu_custom_call" | custom-call | tf_op jit(solution)/shard_map/pallas_call | solution.py:196
  26.3 1.6 %collective-permute-done.proj_ref = f32[128,1024]{1,0:T(8,128)S(1)} collective-permute-done((f32[128,1024]{1,0:T(8,128)}, f32[128,1024]{1,0:T(8,128)S(1)}, u32[]{:S(2)}, u32[]{:S(2)}) %collective-permute-start) | collective-permute-done | bytes 524320 | tf_op jit(solution)/shard_map/ppermute | solution.py:232
  27.9 0.5 %shard_map.111 = f32[128,128]{1,0:T(8,128)S(1)} custom-call(f32[128,1024]{1,0:T(8,128)S(1)} %collective-permute-done.proj_ref, bf16[2,2,256,1024]{3,2,1,0:T(8,128)(2,1)S(1)} %get-tuple-element.9.left_ref), custom_call_target="tpu_custom_call" | custom-call | tf_op jit(solution)/shard_map/pallas_call | solution.py:196
  28.5 1.2 %collective-permute-done.4 = f32[128,128]{1,0:T(8,128)S(1)} collective-permute-done((f32[128,128]{1,0:T(8,128)S(1)}, f32[128,128]{1,0:T(8,128)S(1)}, u32[]{:S(2)}, u32[]{:S(2)}) %collective-permute-start.4) | collective-permute-done | bytes 65568 | tf_op jit(solution)/shard_map/ppermute | solution.py:236
  29.8 1.3 %collective-permute-start.5 = (f32[128,128]{1,0:T(8,128)S(1)}, f32[128,128]{1,0:T(8,128)S(1)}, u32[]{:S(2)}, u32[]{:S(2)}) collective-permute-start(f32[128,128]{1,0:T(8,128)S(1)} %select_add_fusion), channel_id=1, source_target_pairs={{0,3},{1,2},{2,1},{3,0},{4,7},{5,6},{6,5},{7,4},{8,11},{9,10},{10,... | collective-permute-start | bytes 196616 | tf_op jit(solution)/shard_map/ppermute | solution.py:236
  31.1 0.8 %collective-permute-start.6 = (f32[128,128]{1,0:T(8,128)S(1)}, f32[128,128]{1,0:T(8,128)S(1)}, u32[]{:S(2)}, u32[]{:S(2)}) collective-permute-start(f32[128,128]{1,0:T(8,128)S(1)} %select_add_fusion), channel_id=1, source_target_pairs={{0,5},{1,4},{2,7},{3,6},{4,1},{5,0},{6,3},{7,2},{8,13},{9,12},{10,... | collective-permute-start | bytes 196616 | tf_op jit(solution)/shard_map/ppermute | solution.py:236
  31.9 1.2 %collective-permute-start.7 = (f32[128,128]{1,0:T(8,128)S(1)}, f32[128,128]{1,0:T(8,128)S(1)}, u32[]{:S(2)}, u32[]{:S(2)}) collective-permute-start(f32[128,128]{1,0:T(8,128)S(1)} %select_add_fusion), channel_id=1, source_target_pairs={{0,6},{1,7},{2,4},{3,5},{4,2},{5,3},{6,0},{7,1},{8,14},{9,15},{10,... | collective-permute-start | bytes 196616 | tf_op jit(solution)/shard_map/ppermute | solution.py:236
  33.1 0.8 %collective-permute-done.5 = f32[128,128]{1,0:T(8,128)S(1)} collective-permute-done((f32[128,128]{1,0:T(8,128)S(1)}, f32[128,128]{1,0:T(8,128)S(1)}, u32[]{:S(2)}, u32[]{:S(2)}) %collective-permute-start.5) | collective-permute-done | bytes 65568 | tf_op jit(solution)/shard_map/ppermute | solution.py:236
  33.9 1.0 %collective-permute-done.6 = f32[128,128]{1,0:T(8,128)S(1)} collective-permute-done((f32[128,128]{1,0:T(8,128)S(1)}, f32[128,128]{1,0:T(8,128)S(1)}, u32[]{:S(2)}, u32[]{:S(2)}) %collective-permute-start.6) | collective-permute-done | bytes 65568 | tf_op jit(solution)/shard_map/ppermute | solution.py:236
  35.0 2.1 %collective-permute-done.7 = f32[128,128]{1,0:T(8,128)S(1)} collective-permute-done((f32[128,128]{1,0:T(8,128)S(1)}, f32[128,128]{1,0:T(8,128)S(1)}, u32[]{:S(2)}, u32[]{:S(2)}) %collective-permute-start.7) | collective-permute-done | bytes 65568 | tf_op jit(solution)/shard_map/ppermute | solution.py:236
  37.1 0.3 shard_map.113
  37.3 0.3 collective-permute-start.8
  37.6 4.1 %collective-permute-done.8.other_ref.gap_ref = f32[128,128]{1,0:T(8,128)S(1)} collective-permute-done((f32[128,128]{1,0:T(8,128)S(1)}, f32[128,128]{1,0:T(8,128)S(1)}, u32[]{:S(2)}, u32[]{:S(2)}) %collective-permute-start.8) | collective-permute-done | bytes 65568 | tf_op jit(solution)/shard_map/ppermute | solution.py:236
  41.9 2.4 %collective-permute-start.9 = (f32[64,128]{1,0:T(8,128)S(1)}, f32[64,128]{1,0:T(8,128)S(1)}, u32[]{:S(2)}, u32[]{:S(2)}) collective-permute-start(f32[64,128]{1,0:T(8,128)S(1)} %shard_map.114), channel_id=1, source_target_pairs={{0,17},{1,16},{2,19},{3,18},{4,21},{5,20},{6,23},{7,22},{8,25},{9,... | collective-permute-start | bytes 98312 | tf_op jit(solution)/shard_map/ppermute | solution.py:236
  44.3 0.2 shard_map.115.prefix_ref
  44.5 1.7 %collective-permute-done.9.carry_ref = f32[64,128]{1,0:T(8,128)S(1)} collective-permute-done((f32[64,128]{1,0:T(8,128)S(1)}, f32[64,128]{1,0:T(8,128)S(1)}, u32[]{:S(2)}, u32[]{:S(2)}) %collective-permute-start.9) | collective-permute-done | bytes 32800 | tf_op jit(solution)/shard_map/ppermute | solution.py:236
  46.5 0.9 %collective-permute-start.10 = (f32[64,128]{1,0:T(8,128)S(1)}, f32[64,128]{1,0:T(8,128)S(1)}, u32[]{:S(2)}, u32[]{:S(2)}) collective-permute-start(f32[64,128]{1,0:T(8,128)S(1)} %shard_map.116.rows_ref), channel_id=1, source_target_pairs={{0,1},{1,0},{2,3},{3,2},{4,5},{5,4},{6,7},{7,6},{8,9},{9,8},{10,11... | collective-permute-start | bytes 98312 | tf_op jit(solution)/shard_map/ppermute | solution.py:236
  47.4 0.3 shard_map.117.sum_ref
  47.7 0.5 %collective-permute-done.10.rows_ref = f32[64,128]{1,0:T(8,128)S(1)} collective-permute-done((f32[64,128]{1,0:T(8,128)S(1)}, f32[64,128]{1,0:T(8,128)S(1)}, u32[]{:S(2)}, u32[]{:S(2)}) %collective-permute-start.10) | collective-permute-done | bytes 32800 | tf_op jit(solution)/shard_map/ppermute | solution.py:236
  48.2 1.1 %shard_map.118 = f32[128,1024]{1,0:T(8,128)} custom-call(f32[64,128]{1,0:T(8,128)S(1)} %collective-permute-done.10.rows_ref, bf16[2,2,256,1024]{3,2,1,0:T(8,128)(2,1)S(1)} %get-tuple-element.9.left_ref, f32[128,1024]{1,0:T(8,128)S(1)} %shard_map.117.sum_ref), custom_call_target="tpu_custom_call" | custom-call | tf_op jit(solution)/shard_map/pallas_call | solution.py:302
  (26 shorter events, 0.7 us)
Async XLA Ops:
  0.0 16.7 %copy-start = (f32[1,2,64,1024]{3,2,1,0:T(8,128)S(1)}, f32[1,2,64,1024]{3,2,1,0:T(8,128)}, u32[]{:S(2)}) copy-start(f32[1,2,64,1024]{3,2,1,0:T(8,128)} %param.11) | copy-start | bytes 1572868
  0.0 16.7 %copy-start.1 = (f32[1,2,64,1024]{3,2,1,0:T(8,128)S(1)}, f32[1,2,64,1024]{3,2,1,0:T(8,128)}, u32[]{:S(2)}) copy-start(f32[1,2,64,1024]{3,2,1,0:T(8,128)} %param.12) | copy-start | bytes 1572868
  0.0 16.7 %copy-start.2 = (f32[1,2,64,1024]{3,2,1,0:T(8,128)S(1)}, f32[1,2,64,1024]{3,2,1,0:T(8,128)}, u32[]{:S(2)}) copy-start(f32[1,2,64,1024]{3,2,1,0:T(8,128)} %param.14) | copy-start | bytes 1572868
  0.0 25.8 %collective-permute-start.3 = (f32[128,1024]{1,0:T(8,128)}, f32[128,1024]{1,0:T(8,128)S(1)}, u32[]{:S(2)}, u32[]{:S(2)}) collective-permute-start(f32[128,1024]{1,0:T(8,128)} %bitcast.13), channel_id=1, source_target_pairs={{0,4},{4,8},{8,12},{12,16},{16,20},{20,24},{24,28},{28,0},{1,5},{5... | collective-permute-start | bytes 1572872 | tf_op jit(solution)/shard_map/ppermute | solution.py:232
  3.1 24.8 %collective-permute-start = (f32[128,1024]{1,0:T(8,128)}, f32[128,1024]{1,0:T(8,128)S(1)}, u32[]{:S(2)}, u32[]{:S(2)}) collective-permute-start(f32[128,1024]{1,0:T(8,128)} %bitcast.15), channel_id=1, source_target_pairs={{0,28},{4,0},{8,4},{12,8},{16,12},{20,16},{24,20},{28,24},{1,29},{... | collective-permute-start | bytes 1572872 | tf_op jit(solution)/shard_map/ppermute | solution.py:232
  6.2 1.0 %copy-start.3 = (f32[2,64,1024]{2,1,0:T(8,128)S(1)}, f32[2,64,1024]{2,1,0:T(8,128)}, u32[]{:S(2)}) copy-start(f32[2,64,1024]{2,1,0:T(8,128)} %param.20) | copy-start | bytes 1572868
  7.2 1.0 %copy-start.4 = (f32[2,64,1024]{2,1,0:T(8,128)S(1)}, f32[2,64,1024]{2,1,0:T(8,128)}, u32[]{:S(2)}) copy-start(f32[2,64,1024]{2,1,0:T(8,128)} %param.21) | copy-start | bytes 1572868
  8.2 1.0 %copy-start.5 = (f32[1,2,64,1024]{3,2,1,0:T(8,128)S(1)}, f32[1,2,64,1024]{3,2,1,0:T(8,128)}, u32[]{:S(2)}) copy-start(f32[1,2,64,1024]{3,2,1,0:T(8,128)} %param.15) | copy-start | bytes 1572868
  9.3 1.0 %copy-start.6 = (f32[1,2,64,1024]{3,2,1,0:T(8,128)S(1)}, f32[1,2,64,1024]{3,2,1,0:T(8,128)}, u32[]{:S(2)}) copy-start(f32[1,2,64,1024]{3,2,1,0:T(8,128)} %param.13) | copy-start | bytes 1572868
  10.3 6.4 %copy-start.7 = (s32[1,64]{1,0:T(1,128)S(1)}, s32[1,64]{1,0:T(1,128)}, u32[]{:S(2)}) copy-start(s32[1,64]{1,0:T(1,128)} %list_ref.1) | copy-start | bytes 772
  10.3 6.4 %copy-start.8 = (f32[1,64]{1,0:T(1,128)S(1)}, f32[1,64]{1,0:T(1,128)}, u32[]{:S(2)}) copy-start(f32[1,64]{1,0:T(1,128)} %dd_ref.1) | copy-start | bytes 772
  10.3 6.4 %copy-start.9 = (f32[1,64]{1,0:T(1,128)S(1)}, f32[1,64]{1,0:T(1,128)}, u32[]{:S(2)}) copy-start(f32[1,64]{1,0:T(1,128)} %ud_ref.1) | copy-start | bytes 772
  11.0 1.3 %collective-permute-start.1 = (f32[128,128]{1,0:T(8,128)S(1)}, f32[128,128]{1,0:T(8,128)S(1)}, u32[]{:S(2)}, u32[]{:S(2)}) collective-permute-start(f32[128,128]{1,0:T(8,128)S(1)} %shard_map.109), channel_id=1, source_target_pairs={{0,1},{1,0},{2,3},{3,2},{4,5},{5,4},{6,7},{7,6},{8,9},{9,8},{10,11... | collective-permute-start | bytes 196616 | tf_op jit(solution)/shard_map/ppermute | solution.py:236
  12.4 4.3 %collective-permute-start.2 = (f32[128,128]{1,0:T(8,128)S(1)}, f32[128,128]{1,0:T(8,128)S(1)}, u32[]{:S(2)}, u32[]{:S(2)}) collective-permute-start(f32[128,128]{1,0:T(8,128)S(1)} %add.15), channel_id=1, source_target_pairs={{0,2},{1,3},{2,0},{3,1},{4,6},{5,7},{6,4},{7,5},{8,10},{9,11},{10,... | collective-permute-start | bytes 196616 | tf_op jit(solution)/shard_map/ppermute | solution.py:236
  28.4 1.3 %collective-permute-start.4 = (f32[128,128]{1,0:T(8,128)S(1)}, f32[128,128]{1,0:T(8,128)S(1)}, u32[]{:S(2)}, u32[]{:S(2)}) collective-permute-start(f32[128,128]{1,0:T(8,128)S(1)} %broadcast_select_fusion), channel_id=1, source_target_pairs={{0,1},{1,0},{2,3},{3,2},{4,5},{5,4},{6,7},{7,6},{8,9},{9,8},{10,11... | collective-permute-start | bytes 196616 | tf_op jit(solution)/shard_map/ppermute | solution.py:236
  29.8 4.1 %collective-permute-start.5 = (f32[128,128]{1,0:T(8,128)S(1)}, f32[128,128]{1,0:T(8,128)S(1)}, u32[]{:S(2)}, u32[]{:S(2)}) collective-permute-start(f32[128,128]{1,0:T(8,128)S(1)} %select_add_fusion), channel_id=1, source_target_pairs={{0,3},{1,2},{2,1},{3,0},{4,7},{5,6},{6,5},{7,4},{8,11},{9,10},{10,... | collective-permute-start | bytes 196616 | tf_op jit(solution)/shard_map/ppermute | solution.py:236
  31.1 3.9 %collective-permute-start.6 = (f32[128,128]{1,0:T(8,128)S(1)}, f32[128,128]{1,0:T(8,128)S(1)}, u32[]{:S(2)}, u32[]{:S(2)}) collective-permute-start(f32[128,128]{1,0:T(8,128)S(1)} %select_add_fusion), channel_id=1, source_target_pairs={{0,5},{1,4},{2,7},{3,6},{4,1},{5,0},{6,3},{7,2},{8,13},{9,12},{10,... | collective-permute-start | bytes 196616 | tf_op jit(solution)/shard_map/ppermute | solution.py:236
  31.9 5.2 %collective-permute-start.7 = (f32[128,128]{1,0:T(8,128)S(1)}, f32[128,128]{1,0:T(8,128)S(1)}, u32[]{:S(2)}, u32[]{:S(2)}) collective-permute-start(f32[128,128]{1,0:T(8,128)S(1)} %select_add_fusion), channel_id=1, source_target_pairs={{0,6},{1,7},{2,4},{3,5},{4,2},{5,3},{6,0},{7,1},{8,14},{9,15},{10,... | collective-permute-start | bytes 196616 | tf_op jit(solution)/shard_map/ppermute | solution.py:236
  37.3 4.3 %collective-permute-start.8 = (f32[128,128]{1,0:T(8,128)S(1)}, f32[128,128]{1,0:T(8,128)S(1)}, u32[]{:S(2)}, u32[]{:S(2)}) collective-permute-start(f32[128,128]{1,0:T(8,128)S(1)} %get-tuple-element.10.own_ref), channel_id=1, source_target_pairs={{0,9},{1,8},{2,11},{3,10},{4,13},{5,12},{6,15},{7,14},{8,1},{9,0},... | collective-permute-start | bytes 196616 | tf_op jit(solution)/shard_map/ppermute | solution.py:236
  41.9 4.4 %collective-permute-start.9 = (f32[64,128]{1,0:T(8,128)S(1)}, f32[64,128]{1,0:T(8,128)S(1)}, u32[]{:S(2)}, u32[]{:S(2)}) collective-permute-start(f32[64,128]{1,0:T(8,128)S(1)} %shard_map.114), channel_id=1, source_target_pairs={{0,17},{1,16},{2,19},{3,18},{4,21},{5,20},{6,23},{7,22},{8,25},{9,... | collective-permute-start | bytes 98312 | tf_op jit(solution)/shard_map/ppermute | solution.py:236
  46.5 1.7 %collective-permute-start.10 = (f32[64,128]{1,0:T(8,128)S(1)}, f32[64,128]{1,0:T(8,128)S(1)}, u32[]{:S(2)}, u32[]{:S(2)}) collective-permute-start(f32[64,128]{1,0:T(8,128)S(1)} %shard_map.116.rows_ref), channel_id=1, source_target_pairs={{0,1},{1,0},{2,3},{3,2},{4,5},{5,4},{6,7},{7,6},{8,9},{9,8},{10,11... | collective-permute-start | bytes 98312 | tf_op jit(solution)/shard_map/ppermute | solution.py:236

commit v5 on v4

--- a/solution.py
+++ b/solution.py
@@ -110,17 +110,28 @@
             left_ref[k, part, 2 * rank :] = trace[part]
 
 
-def gram_kernel(which, proj_ref, left_ref, out_ref):
+def gram(which, proj_ref, left_ref):
     rank = proj_ref.shape[0] // 2
     out = dot3((left_ref[which, 0], left_ref[which, 1]), split(proj_ref[...]), ROWS_ROWS)
-    out_ref[:rank] = joined(out[: 2 * rank])
-    out_ref[rank:] = joined(out[2 * rank :])
-
-
-def pair_kernel(own_ref, other_ref, near_ref, out_ref):
-    place = standing()[1]
-    own, other = own_ref[...], other_ref[...]
-    first = lax.rem(place, 2) == 0
+    return jnp.concatenate([joined(out[: 2 * rank]), joined(out[2 * rank :])], 0)
+
+
+def first_gram_kernel(proj_ref, left_ref, out_ref):
+    out_ref[...] = gram(1, proj_ref, left_ref)
+
+
+def second_gram_kernel(proj_ref, left_ref, first_ref, keep_ref, give_ref):
+    down, up = gram(0, proj_ref, left_ref), first_ref[...]
+    ours = standing()[0] == 0
+    keep_ref[...] = jnp.where(ours, down, up)
+    give_ref[...] = jnp.where(ours, up, down)
+
+
+def pair_kernel(count, *refs):
+    parts, (near_ref, out_ref) = refs[:-2], refs[-2:]
+    other = sum((ref[...] for ref in parts[1:count]), parts[0][...])
+    own = sum((ref[...] for ref in parts[count + 1 :]), parts[count][...])
+    first = lax.rem(standing()[1], 2) == 0
     near = jnp.where(first, own, other)
     near_ref[...] = near
     out_ref[...] = compose(jnp.where(first, other, own), near)
@@ -180,11 +191,10 @@
 
 
 def finish_kernel(rows_ref, left_ref, sum_ref, out_ref, held_ref, done):
-    chunks = done.shape[0]
-    width = held_ref.shape[1] // chunks
+    width = held_ref.shape[1]
     copies = []
-    for k in range(chunks):
-        columns = slice(k * width, (k + 1) * width)
+    for k, (start, stop) in enumerate(((0, width // 4), (width // 4, width))):
+        columns = slice(start, stop)
         held_ref[:, columns] = expanded(1, rows_ref, left_ref, sum_ref, columns)
         copies.append(pltpu.make_async_copy(held_ref.at[:, columns], out_ref.at[:, columns], done.at[k]))
         copies[-1].start()
@@ -222,7 +232,6 @@
     nsrc, width = sources.shape[2:]
     rank = down_expand.shape[2]
     depth, lat = lax.axis_size("depth"), lax.axis_size("lat")
-    role = standing()[0]
     element = shape(rank + nsrc, 2 * rank)
 
     def flat(value):
@@ -269,21 +278,20 @@
         grant=12,
     )
 
-    def gram(which, proj):
-        return call(functools.partial(gram_kernel, which), element, proj, left)
-
-    down, up = gram(0, ahead), gram(1, behind)
-    own = jnp.where(role == 0, down, up) + swapped(jnp.where(role == 0, up, down), 0, 1)
+    first = call(first_gram_kernel, element, behind, left)
+    keep, give = call(second_gram_kernel, (element, element), ahead, left, first)
+    own = keep + swapped(give, 0, 1)
     bit = 4
     while bit < lat:
         own = own + met(own, 0, bit)
         bit *= 2
-    other = met(own, 1, 0)
+    owns, others = [own], []
     if lat > 2:
-        other = other + met(own, 1, 2)
-        own = own + met(own, 0, 2)
-
-    near, total = call(pair_kernel, (element, element), own, other)
+        others.append(met(own, 1, 2))
+        owns.append(met(own, 0, 2))
+    others.append(met(own, 1, 0))
+
+    near, total = call(functools.partial(pair_kernel, len(others)), (element, element), *others, *owns)
     gap = near
     reach, half = 2, depth // 2
     while reach < half:
@@ -298,13 +306,12 @@
     coef = call(functools.partial(final_kernel, half), shape(nsrc, 2 * rank), carry, prefix, entry)
     wide = shape(2 * nsrc, width)
     field = call(expand_kernel, wide, coef, left, local)
-    chunks = 4
     field = pl.pallas_call(
         finish_kernel,
         out_shape=wide,
         in_specs=[VMEM] * 3,
         out_specs=pl.BlockSpec(memory_space=pl.ANY),
-        scratch_shapes=[pltpu.VMEM(wide.shape, F32), pltpu.SemaphoreType.DMA((chunks,))],
+        scratch_shapes=[pltpu.VMEM(wide.shape, F32), pltpu.SemaphoreType.DMA((2,))],
         compiler_params=pltpu.CompilerParams(vmem_limit_bytes=4 << 20),
     )(swapped(coef, 0, 1), left, field)
     return field.reshape(sources.shape)

time: 49.6 us -> 48.2 us (0.972)
  waiting for transfers between devices: 24.7 us -> 23.5 us
    ppermute x9, waiting for transfers between devices: 14.8 us -> 13.6 us  [swapped(): return lax.ppermute(value, ('depth', 'lat'), pairs)]
  transfers between devices with their start and end apart: 11 -> 11, of which waited for: 11 -> 10; matrix products, arithmetic and copies ran while one was open for 0% -> 0% of each run, Pallas kernels for 5% -> 5%
where the time goes in v5:
time: 48.2 us; the launch traced here: 47.9 us
  waiting for transfers between devices  23.5 us (49%)
  starting transfers between devices  14.6 us (30%)
  Pallas kernels  4.86 us (10%)
  local copies, waits for them, and re-layouts  4.19 us (9%)
  between operations  0.8 us (2%)
    ppermute x9, waiting for transfers between devices, swapped(): return lax.ppermute(value, ('depth', 'lat'), pairs)  13.6 us
    ppermute x2, waiting for transfers between devices, shifted(): lax.ppermute(value, 'depth', [(k, (k + step) % depth) for k in range(dept...  9.85 us
    ppermute x9, starting transfers between devices, swapped(): return lax.ppermute(value, ('depth', 'lat'), pairs)  8.44 us
    ppermute x2, starting transfers between devices, shifted(): lax.ppermute(value, 'depth', [(k, (k + step) % depth) for k in range(dept...  6.15 us
    unnamed x20, local copies, waits for them, and re-layouts  4.19 us
    pallas_call x9, Pallas kernels, call(): pl.pallas_call(kernel, out_shape=outs, in_specs=[SMEM] * scalars + [VMEM]...  3.75 us
    pallas_call x1, Pallas kernels, body(): pl.pallas_call(finish_kernel, out_shape=wide, in_specs=[VMEM] * 3, out_sp...  1.11 us
  transfers between devices with their start and end apart: 11, of which 10 were waited for; matrix products, arithmetic and copies ran while one was open for 0% of the time, Pallas kernels for 5%

profile of v5, /device:TPU:0, one launch (start us, length us, event | category | flops | bytes accessed | tf_op | source)
XLA Modules:
  0.0 47.9 jit_solution(2056198209131171813)
XLA Ops:
  0.0 3.0 %collective-permute-start.3 = (f32[128,1024]{1,0:T(8,128)}, f32[128,1024]{1,0:T(8,128)S(1)}, u32[]{:S(2)}, u32[]{:S(2)}) collective-permute-start(f32[128,1024]{1,0:T(8,128)} %bitcast.13), channel_id=1, source_target_pairs={{0,4},{4,8},{8,12},{12,16},{16,20},{20,24},{24,28},{28,0},{1,5},{5... | collective-permute-start | bytes 1572872 | tf_op jit(solution)/shard_map/ppermute | solution.py:241
  3.1 3.1 %collective-permute-start = (f32[128,1024]{1,0:T(8,128)}, f32[128,1024]{1,0:T(8,128)S(1)}, u32[]{:S(2)}, u32[]{:S(2)}) collective-permute-start(f32[128,1024]{1,0:T(8,128)} %bitcast.15), channel_id=1, source_target_pairs={{0,28},{4,0},{8,4},{12,8},{16,12},{20,16},{24,20},{28,24},{1,29},{... | collective-permute-start | bytes 1572872 | tf_op jit(solution)/shard_map/ppermute | solution.py:241
  6.2 1.0 %copy-done.3 = f32[2,64,1024]{2,1,0:T(8,128)S(1)} copy-done((f32[2,64,1024]{2,1,0:T(8,128)S(1)}, f32[2,64,1024]{2,1,0:T(8,128)}, u32[]{:S(2)}) %copy-start.3) | copy-done | bytes 524312
  7.2 1.0 %copy-done.4 = f32[2,64,1024]{2,1,0:T(8,128)S(1)} copy-done((f32[2,64,1024]{2,1,0:T(8,128)S(1)}, f32[2,64,1024]{2,1,0:T(8,128)}, u32[]{:S(2)}) %copy-start.4) | copy-done | bytes 524312
  8.2 1.0 %copy-done.5 = f32[1,2,64,1024]{3,2,1,0:T(8,128)S(1)} copy-done((f32[1,2,64,1024]{3,2,1,0:T(8,128)S(1)}, f32[1,2,64,1024]{3,2,1,0:T(8,128)}, u32[]{:S(2)}) %copy-start.5) | copy-done | bytes 524312
  9.3 1.0 %copy-done.6 = f32[1,2,64,1024]{3,2,1,0:T(8,128)S(1)} copy-done((f32[1,2,64,1024]{3,2,1,0:T(8,128)S(1)}, f32[1,2,64,1024]{3,2,1,0:T(8,128)}, u32[]{:S(2)}) %copy-start.6) | copy-done | bytes 524312
  10.3 0.7 %shard_map.109 = f32[128,128]{1,0:T(8,128)S(1)} custom-call(f32[128,1024]{1,0:T(8,128)S(1)} %bitcast.16, f32[128,1024]{1,0:T(8,128)S(1)} %bitcast.14, f32[128,1024]{1,0:T(8,128)S(1)} %bitcast.11, f32[128,1024]{1,0:T(8,128)S(1)} %bitcast.12), custom_call_target="tpu_custom_call" | custom-call | tf_op jit(solution)/shard_map/pallas_call | solution.py:206
  11.1 1.2 %collective-permute-done.1 = f32[128,128]{1,0:T(8,128)S(1)} collective-permute-done((f32[128,128]{1,0:T(8,128)S(1)}, f32[128,128]{1,0:T(8,128)S(1)}, u32[]{:S(2)}, u32[]{:S(2)}) %collective-permute-start.1) | collective-permute-done | bytes 65568 | tf_op jit(solution)/shard_map/ppermute | solution.py:245
  12.4 1.7 %collective-permute-start.2 = (f32[128,128]{1,0:T(8,128)S(1)}, f32[128,128]{1,0:T(8,128)S(1)}, u32[]{:S(2)}, u32[]{:S(2)}) collective-permute-start(f32[128,128]{1,0:T(8,128)S(1)} %add.9), channel_id=1, source_target_pairs={{0,2},{1,3},{2,0},{3,1},{4,6},{5,7},{6,4},{7,5},{8,10},{9,11},{10,... | collective-permute-start | bytes 196616 | tf_op jit(solution)/shard_map/ppermute | solution.py:245
  14.7 2.0 %collective-permute-done.2 = f32[128,128]{1,0:T(8,128)S(1)} collective-permute-done((f32[128,128]{1,0:T(8,128)S(1)}, f32[128,128]{1,0:T(8,128)S(1)}, u32[]{:S(2)}, u32[]{:S(2)}) %collective-permute-start.2) | collective-permute-done | bytes 65568 | tf_op jit(solution)/shard_map/ppermute | solution.py:245
  16.8 0.7 %shard_map.110 = (f32[128,1024]{1,0:T(8,128)S(1)}, bf16[2,2,256,1024]{3,2,1,0:T(8,128)(2,1)S(1)}) custom-call(s32[1]{0:T(128)S(6)} %copy.12.count_ref, s32[1,64]{1,0:T(1,128)S(1)} %copy-done.7, f32[128,1024]{1,0:T(8,128)S(1)} %bitcast.8, f32[128,1024]{1,0:T(8,128)S(1)} %bitcast.9, f32[128,1024]{1,0:T(8,128)S(1)} %bitcast.10, f32[1,64]{1,0:T(1,128)S(1)} %copy-done.8, ...), custom_call_target="tpu_custom_call" | custom-call | tf_op jit(solution)/shard_map/pallas_call | solution.py:206
  17.5 8.3 %collective-permute-done.3.proj_ref = f32[128,1024]{1,0:T(8,128)S(1)} collective-permute-done((f32[128,1024]{1,0:T(8,128)}, f32[128,1024]{1,0:T(8,128)S(1)}, u32[]{:S(2)}, u32[]{:S(2)}) %collective-permute-start.3) | collective-permute-done | bytes 524320 | tf_op jit(solution)/shard_map/ppermute | solution.py:241
  25.8 0.5 %shard_map.111.first_ref = f32[128,128]{1,0:T(8,128)S(1)} custom-call(f32[128,1024]{1,0:T(8,128)S(1)} %collective-permute-done.3.proj_ref, bf16[2,2,256,1024]{3,2,1,0:T(8,128)(2,1)S(1)} %get-tuple-element.11.left_ref), custom_call_target="tpu_custom_call" | custom-call | tf_op jit(solution)/shard_map/pallas_call | solution.py:206
  26.3 1.5 %collective-permute-done.proj_ref = f32[128,1024]{1,0:T(8,128)S(1)} collective-permute-done((f32[128,1024]{1,0:T(8,128)}, f32[128,1024]{1,0:T(8,128)S(1)}, u32[]{:S(2)}, u32[]{:S(2)}) %collective-permute-start) | collective-permute-done | bytes 524320 | tf_op jit(solution)/shard_map/ppermute | solution.py:241
  27.9 0.5 %shard_map.112 = (f32[128,128]{1,0:T(8,128)S(1)}, f32[128,128]{1,0:T(8,128)S(1)}) custom-call(f32[128,1024]{1,0:T(8,128)S(1)} %collective-permute-done.proj_ref, bf16[2,2,256,1024]{3,2,1,0:T(8,128)(2,1)S(1)} %get-tuple-element.11.left_ref, f32[128,128]{1,0:T(8,128)S(1)} %shard_map.111.first_ref), custom_call_target="tpu_custom_call" | custom-call | tf_op jit(solution)/shard_map/pallas_call | solution.py:206
  28.5 1.2 %collective-permute-done.4 = f32[128,128]{1,0:T(8,128)S(1)} collective-permute-done((f32[128,128]{1,0:T(8,128)S(1)}, f32[128,128]{1,0:T(8,128)S(1)}, u32[]{:S(2)}, u32[]{:S(2)}) %collective-permute-start.4) | collective-permute-done | bytes 65568 | tf_op jit(solution)/shard_map/ppermute | solution.py:245
  29.8 1.8 %collective-permute-start.5 = (f32[128,128]{1,0:T(8,128)S(1)}, f32[128,128]{1,0:T(8,128)S(1)}, u32[]{:S(2)}, u32[]{:S(2)}) collective-permute-start(f32[128,128]{1,0:T(8,128)S(1)} %add.11.refs_2_), channel_id=1, source_target_pairs={{0,6},{1,7},{2,4},{3,5},{4,2},{5,3},{6,0},{7,1},{8,14},{9,15},{10,... | collective-permute-start | bytes 196616 | tf_op jit(solution)/shard_map/ppermute | solution.py:245
  31.6 0.7 %collective-permute-start.6 = (f32[128,128]{1,0:T(8,128)S(1)}, f32[128,128]{1,0:T(8,128)S(1)}, u32[]{:S(2)}, u32[]{:S(2)}) collective-permute-start(f32[128,128]{1,0:T(8,128)S(1)} %add.11.refs_2_), channel_id=1, source_target_pairs={{0,5},{1,4},{2,7},{3,6},{4,1},{5,0},{6,3},{7,2},{8,13},{9,12},{10,... | collective-permute-start | bytes 196616 | tf_op jit(solution)/shard_map/ppermute | solution.py:245
  32.3 0.8 %collective-permute-start.7 = (f32[128,128]{1,0:T(8,128)S(1)}, f32[128,128]{1,0:T(8,128)S(1)}, u32[]{:S(2)}, u32[]{:S(2)}) collective-permute-start(f32[128,128]{1,0:T(8,128)S(1)} %add.11.refs_2_), channel_id=1, source_target_pairs={{0,3},{1,2},{2,1},{3,0},{4,7},{5,6},{6,5},{7,4},{8,11},{9,10},{10,... | collective-permute-start | bytes 196616 | tf_op jit(solution)/shard_map/ppermute | solution.py:245
  33.0 2.0 %collective-permute-done.5.refs_0_ = f32[128,128]{1,0:T(8,128)S(1)} collective-permute-done((f32[128,128]{1,0:T(8,128)S(1)}, f32[128,128]{1,0:T(8,128)S(1)}, u32[]{:S(2)}, u32[]{:S(2)}) %collective-permute-start.5) | collective-permute-done | bytes 65568 | tf_op jit(solution)/shard_map/ppermute | solution.py:245
  35.0 1.4 %collective-permute-done.6.refs_1_ = f32[128,128]{1,0:T(8,128)S(1)} collective-permute-done((f32[128,128]{1,0:T(8,128)S(1)}, f32[128,128]{1,0:T(8,128)S(1)}, u32[]{:S(2)}, u32[]{:S(2)}) %collective-permute-start.6) | collective-permute-done | bytes 65568 | tf_op jit(solution)/shard_map/ppermute | solution.py:245
  36.4 0.3 shard_map.113
  36.7 1.1 %collective-permute-start.8 = (f32[128,128]{1,0:T(8,128)S(1)}, f32[128,128]{1,0:T(8,128)S(1)}, u32[]{:S(2)}, u32[]{:S(2)}) collective-permute-start(f32[128,128]{1,0:T(8,128)S(1)} %get-tuple-element.14.own_ref), channel_id=1, source_target_pairs={{0,9},{1,8},{2,11},{3,10},{4,13},{5,12},{6,15},{7,14},{8,1},{9,0},... | collective-permute-start | bytes 196616 | tf_op jit(solution)/shard_map/ppermute | solution.py:245
  37.8 3.0 %collective-permute-done.8.other_ref.gap_ref = f32[128,128]{1,0:T(8,128)S(1)} collective-permute-done((f32[128,128]{1,0:T(8,128)S(1)}, f32[128,128]{1,0:T(8,128)S(1)}, u32[]{:S(2)}, u32[]{:S(2)}) %collective-permute-start.8) | collective-permute-done | bytes 65568 | tf_op jit(solution)/shard_map/ppermute | solution.py:245
  40.8 0.2 shard_map.114
  41.0 2.1 %collective-permute-start.9 = (f32[64,128]{1,0:T(8,128)S(1)}, f32[64,128]{1,0:T(8,128)S(1)}, u32[]{:S(2)}, u32[]{:S(2)}) collective-permute-start(f32[64,128]{1,0:T(8,128)S(1)} %shard_map.114), channel_id=1, source_target_pairs={{0,17},{1,16},{2,19},{3,18},{4,21},{5,20},{6,23},{7,22},{8,25},{9,... | collective-permute-start | bytes 98312 | tf_op jit(solution)/shard_map/ppermute | solution.py:245
  43.1 0.2 shard_map.115.prefix_ref
  43.3 2.0 %collective-permute-done.9.carry_ref = f32[64,128]{1,0:T(8,128)S(1)} collective-permute-done((f32[64,128]{1,0:T(8,128)S(1)}, f32[64,128]{1,0:T(8,128)S(1)}, u32[]{:S(2)}, u32[]{:S(2)}) %collective-permute-start.9) | collective-permute-done | bytes 32800 | tf_op jit(solution)/shard_map/ppermute | solution.py:245
  45.6 0.2 collective-permute-start.10
  45.8 0.3 shard_map.117.sum_ref
  46.1 0.7 %collective-permute-done.10.rows_ref = f32[64,128]{1,0:T(8,128)S(1)} collective-permute-done((f32[64,128]{1,0:T(8,128)S(1)}, f32[64,128]{1,0:T(8,128)S(1)}, u32[]{:S(2)}, u32[]{:S(2)}) %collective-permute-start.10) | collective-permute-done | bytes 32800 | tf_op jit(solution)/shard_map/ppermute | solution.py:245
  46.8 1.1 %shard_map.118 = f32[128,1024]{1,0:T(8,128)} custom-call(f32[64,128]{1,0:T(8,128)S(1)} %collective-permute-done.10.rows_ref, bf16[2,2,256,1024]{3,2,1,0:T(8,128)(2,1)S(1)} %get-tuple-element.11.left_ref, f32[128,1024]{1,0:T(8,128)S(1)} %shard_map.117.sum_ref), custom_call_target="tpu_custom_call" | custom-call | tf_op jit(solution)/shard_map/pallas_call | solution.py:309
  (23 shorter events, 0.4 us)
Async XLA Ops:
  0.0 16.7 %copy-start = (f32[1,2,64,1024]{3,2,1,0:T(8,128)S(1)}, f32[1,2,64,1024]{3,2,1,0:T(8,128)}, u32[]{:S(2)}) copy-start(f32[1,2,64,1024]{3,2,1,0:T(8,128)} %param.11) | copy-start | bytes 1572868
  0.0 16.7 %copy-start.1 = (f32[1,2,64,1024]{3,2,1,0:T(8,128)S(1)}, f32[1,2,64,1024]{3,2,1,0:T(8,128)}, u32[]{:S(2)}) copy-start(f32[1,2,64,1024]{3,2,1,0:T(8,128)} %param.12) | copy-start | bytes 1572868
  0.0 16.7 %copy-start.2 = (f32[1,2,64,1024]{3,2,1,0:T(8,128)S(1)}, f32[1,2,64,1024]{3,2,1,0:T(8,128)}, u32[]{:S(2)}) copy-start(f32[1,2,64,1024]{3,2,1,0:T(8,128)} %param.14) | copy-start | bytes 1572868
  0.0 25.8 %collective-permute-start.3 = (f32[128,1024]{1,0:T(8,128)}, f32[128,1024]{1,0:T(8,128)S(1)}, u32[]{:S(2)}, u32[]{:S(2)}) collective-permute-start(f32[128,1024]{1,0:T(8,128)} %bitcast.13), channel_id=1, source_target_pairs={{0,4},{4,8},{8,12},{12,16},{16,20},{20,24},{24,28},{28,0},{1,5},{5... | collective-permute-start | bytes 1572872 | tf_op jit(solution)/shard_map/ppermute | solution.py:241
  3.1 24.8 %collective-permute-start = (f32[128,1024]{1,0:T(8,128)}, f32[128,1024]{1,0:T(8,128)S(1)}, u32[]{:S(2)}, u32[]{:S(2)}) collective-permute-start(f32[128,1024]{1,0:T(8,128)} %bitcast.15), channel_id=1, source_target_pairs={{0,28},{4,0},{8,4},{12,8},{16,12},{20,16},{24,20},{28,24},{1,29},{... | collective-permute-start | bytes 1572872 | tf_op jit(solution)/shard_map/ppermute | solution.py:241
  6.2 1.0 %copy-start.3 = (f32[2,64,1024]{2,1,0:T(8,128)S(1)}, f32[2,64,1024]{2,1,0:T(8,128)}, u32[]{:S(2)}) copy-start(f32[2,64,1024]{2,1,0:T(8,128)} %param.20) | copy-start | bytes 1572868
  7.2 1.0 %copy-start.4 = (f32[2,64,1024]{2,1,0:T(8,128)S(1)}, f32[2,64,1024]{2,1,0:T(8,128)}, u32[]{:S(2)}) copy-start(f32[2,64,1024]{2,1,0:T(8,128)} %param.21) | copy-start | bytes 1572868
  8.2 1.0 %copy-start.5 = (f32[1,2,64,1024]{3,2,1,0:T(8,128)S(1)}, f32[1,2,64,1024]{3,2,1,0:T(8,128)}, u32[]{:S(2)}) copy-start(f32[1,2,64,1024]{3,2,1,0:T(8,128)} %param.15) | copy-start | bytes 1572868
  9.3 1.0 %copy-start.6 = (f32[1,2,64,1024]{3,2,1,0:T(8,128)S(1)}, f32[1,2,64,1024]{3,2,1,0:T(8,128)}, u32[]{:S(2)}) copy-start(f32[1,2,64,1024]{3,2,1,0:T(8,128)} %param.13) | copy-start | bytes 1572868
  10.3 6.4 %copy-start.7 = (s32[1,64]{1,0:T(1,128)S(1)}, s32[1,64]{1,0:T(1,128)}, u32[]{:S(2)}) copy-start(s32[1,64]{1,0:T(1,128)} %list_ref.1) | copy-start | bytes 772
  10.3 6.4 %copy-start.8 = (f32[1,64]{1,0:T(1,128)S(1)}, f32[1,64]{1,0:T(1,128)}, u32[]{:S(2)}) copy-start(f32[1,64]{1,0:T(1,128)} %dd_ref.1) | copy-start | bytes 772
  10.3 6.4 %copy-start.9 = (f32[1,64]{1,0:T(1,128)S(1)}, f32[1,64]{1,0:T(1,128)}, u32[]{:S(2)}) copy-start(f32[1,64]{1,0:T(1,128)} %ud_ref.1) | copy-start | bytes 772
  11.0 1.3 %collective-permute-start.1 = (f32[128,128]{1,0:T(8,128)S(1)}, f32[128,128]{1,0:T(8,128)S(1)}, u32[]{:S(2)}, u32[]{:S(2)}) collective-permute-start(f32[128,128]{1,0:T(8,128)S(1)} %shard_map.109), channel_id=1, source_target_pairs={{0,1},{1,0},{2,3},{3,2},{4,5},{5,4},{6,7},{7,6},{8,9},{9,8},{10,11... | collective-permute-start | bytes 196616 | tf_op jit(solution)/shard_map/ppermute | solution.py:245
  12.4 4.3 %collective-permute-start.2 = (f32[128,128]{1,0:T(8,128)S(1)}, f32[128,128]{1,0:T(8,128)S(1)}, u32[]{:S(2)}, u32[]{:S(2)}) collective-permute-start(f32[128,128]{1,0:T(8,128)S(1)} %add.9), channel_id=1, source_target_pairs={{0,2},{1,3},{2,0},{3,1},{4,6},{5,7},{6,4},{7,5},{8,10},{9,11},{10,... | collective-permute-start | bytes 196616 | tf_op jit(solution)/shard_map/ppermute | solution.py:245
  28.4 1.3 %collective-permute-start.4 = (f32[128,128]{1,0:T(8,128)S(1)}, f32[128,128]{1,0:T(8,128)S(1)}, u32[]{:S(2)}, u32[]{:S(2)}) collective-permute-start(f32[128,128]{1,0:T(8,128)S(1)} %get-tuple-element.13), channel_id=1, source_target_pairs={{0,1},{1,0},{2,3},{3,2},{4,5},{5,4},{6,7},{7,6},{8,9},{9,8},{10,11... | collective-permute-start | bytes 196616 | tf_op jit(solution)/shard_map/ppermute | solution.py:245
  29.8 5.3 %collective-permute-start.5 = (f32[128,128]{1,0:T(8,128)S(1)}, f32[128,128]{1,0:T(8,128)S(1)}, u32[]{:S(2)}, u32[]{:S(2)}) collective-permute-start(f32[128,128]{1,0:T(8,128)S(1)} %add.11.refs_2_), channel_id=1, source_target_pairs={{0,6},{1,7},{2,4},{3,5},{4,2},{5,3},{6,0},{7,1},{8,14},{9,15},{10,... | collective-permute-start | bytes 196616 | tf_op jit(solution)/shard_map/ppermute | solution.py:245
  31.6 4.8 %collective-permute-start.6 = (f32[128,128]{1,0:T(8,128)S(1)}, f32[128,128]{1,0:T(8,128)S(1)}, u32[]{:S(2)}, u32[]{:S(2)}) collective-permute-start(f32[128,128]{1,0:T(8,128)S(1)} %add.11.refs_2_), channel_id=1, source_target_pairs={{0,5},{1,4},{2,7},{3,6},{4,1},{5,0},{6,3},{7,2},{8,13},{9,12},{10,... | collective-permute-start | bytes 196616 | tf_op jit(solution)/shard_map/ppermute | solution.py:245
  32.3 4.1 %collective-permute-start.7 = (f32[128,128]{1,0:T(8,128)S(1)}, f32[128,128]{1,0:T(8,128)S(1)}, u32[]{:S(2)}, u32[]{:S(2)}) collective-permute-start(f32[128,128]{1,0:T(8,128)S(1)} %add.11.refs_2_), channel_id=1, source_target_pairs={{0,3},{1,2},{2,1},{3,0},{4,7},{5,6},{6,5},{7,4},{8,11},{9,10},{10,... | collective-permute-start | bytes 196616 | tf_op jit(solution)/shard_map/ppermute | solution.py:245
  36.7 4.1 %collective-permute-start.8 = (f32[128,128]{1,0:T(8,128)S(1)}, f32[128,128]{1,0:T(8,128)S(1)}, u32[]{:S(2)}, u32[]{:S(2)}) collective-permute-start(f32[128,128]{1,0:T(8,128)S(1)} %get-tuple-element.14.own_ref), channel_id=1, source_target_pairs={{0,9},{1,8},{2,11},{3,10},{4,13},{5,12},{6,15},{7,14},{8,1},{9,0},... | collective-permute-start | bytes 196616 | tf_op jit(solution)/shard_map/ppermute | solution.py:245
  41.0 4.3 %collective-permute-start.9 = (f32[64,128]{1,0:T(8,128)S(1)}, f32[64,128]{1,0:T(8,128)S(1)}, u32[]{:S(2)}, u32[]{:S(2)}) collective-permute-start(f32[64,128]{1,0:T(8,128)S(1)} %shard_map.114), channel_id=1, source_target_pairs={{0,17},{1,16},{2,19},{3,18},{4,21},{5,20},{6,23},{7,22},{8,25},{9,... | collective-permute-start | bytes 98312 | tf_op jit(solution)/shard_map/ppermute | solution.py:245
  45.6 1.3 %collective-permute-start.10 = (f32[64,128]{1,0:T(8,128)S(1)}, f32[64,128]{1,0:T(8,128)S(1)}, u32[]{:S(2)}, u32[]{:S(2)}) collective-permute-start(f32[64,128]{1,0:T(8,128)S(1)} %shard_map.116.rows_ref), channel_id=1, source_target_pairs={{0,1},{1,0},{2,3},{3,2},{4,5},{5,4},{6,7},{7,6},{8,9},{9,8},{10,11... | collective-permute-start | bytes 98312 | tf_op jit(solution)/shard_map/ppermute | solution.py:245

commit v6 on v5

--- a/solution.py
+++ b/solution.py
@@ -129,8 +129,8 @@
 
 def pair_kernel(count, *refs):
     parts, (near_ref, out_ref) = refs[:-2], refs[-2:]
-    other = sum((ref[...] for ref in parts[1:count]), parts[0][...])
-    own = sum((ref[...] for ref in parts[count + 1 :]), parts[count][...])
+    other = parts[0][...] + parts[2][...]
+    own = parts[3][...] + parts[1][...]
     first = lax.rem(standing()[1], 2) == 0
     near = jnp.where(first, own, other)
     near_ref[...] = near
@@ -146,11 +146,6 @@
 def total_kernel(reach, own_ref, other_ref, out_ref):
     earlier, later = ordered(reach, own_ref, other_ref)
     out_ref[...] = compose(later, earlier)
-
-
-def total_offset_kernel(reach, own_ref, other_ref, out_ref):
-    earlier, later = ordered(reach, own_ref, other_ref)
-    out_ref[...] = advance(later, earlier[earlier.shape[1] // 2 :])
 
 
 def gap_kernel(reach, own_ref, other_ref, out_ref):
@@ -162,19 +157,29 @@
     out_ref[...] = jnp.where(upper, longer, own)
 
 
-def prefix_kernel(half, near_ref, gap_ref, out_ref):
-    place = standing()[1]
-    near, gap = near_ref[...], gap_ref[...]
-    odd = lax.rem(place, 2) == 1
-    both = jnp.where(odd, compose(near, gap), gap)
-    out_ref[...] = jnp.where(lax.rem(place, half) >= 2, both, near)
-
-
-def final_kernel(half, carry_ref, prefix_ref, entry_ref, out_ref):
+def offset(step):
+    return step[step.shape[1] // 2 :]
+
+
+def final_kernel(quarter, order, *refs):
+    parts, (near_ref, gap_ref, entry_ref, out_ref) = refs[:-4], refs[-4:]
     role, place = standing()
-    nsrc = carry_ref.shape[0]
-    carry = jnp.where(place >= half, carry_ref[...], 0.0)
-    carry = jnp.where(lax.rem(place, half) > 0, advance(prefix_ref[...], carry), carry)
+    mine = lax.div(place, quarter)
+    totals = [parts[order.index(bits + 1)][...] for bits in range(len(order))]
+
+    def earlier(k):
+        chosen = totals[-1]
+        for bits in range(len(totals) - 1, 0, -1):
+            chosen = jnp.where(mine == (k ^ bits), totals[bits - 1], chosen)
+        return chosen
+
+    carry = jnp.where(mine > 0, offset(earlier(0)), 0.0)
+    for k in range(1, len(totals)):
+        carry = jnp.where(mine > k, advance(earlier(k), carry), carry)
+    if quarter > 2:
+        carry = jnp.where(lax.rem(place, quarter) >= 2, advance(gap_ref[...], carry), carry)
+    carry = jnp.where(lax.rem(place, 2) == 1, advance(near_ref[...], carry), carry)
+    nsrc = carry.shape[0]
     entry = jnp.where(role == 0, entry_ref[:nsrc], entry_ref[nsrc:])
     out_ref[...] = jnp.where(place == 0, entry, carry)
 
@@ -285,25 +290,32 @@
     while bit < lat:
         own = own + met(own, 0, bit)
         bit *= 2
-    owns, others = [own], []
-    if lat > 2:
-        others.append(met(own, 1, 2))
-        owns.append(met(own, 0, 2))
-    others.append(met(own, 1, 0))
-
-    near, total = call(functools.partial(pair_kernel, len(others)), (element, element), *others, *owns)
+    m = dict(xy=met(own, 1, 2), x=met(own, 0, 2), y=met(own, 1, 0), o=own)
+    near, total = call(functools.partial(pair_kernel, 2), (element, element), *[m[k] for k in ['xy', 'x', 'y', 'o']])
     gap = near
-    reach, half = 2, depth // 2
-    while reach < half:
+    quarter = max(depth // 4, 2)
+    reach = 2
+    while reach < quarter:
         other = met(total, reach, 0)
         gap = other if reach == 2 else call(functools.partial(gap_kernel, reach), element, gap, other)
-        last = reach * 2 >= half
-        kernel = functools.partial(total_offset_kernel if last else total_kernel, reach)
-        total = call(kernel, shape(nsrc, 2 * rank) if last else element, total, other)
+        total = call(functools.partial(total_kernel, reach), element, total, other)
         reach *= 2
-    carry = met(total, half, 0)
-    prefix = call(functools.partial(prefix_kernel, half), element, near, gap)
-    coef = call(functools.partial(final_kernel, half), shape(nsrc, 2 * rank), carry, prefix, entry)
+    parts = []
+    for bits in (2, 3, 1):
+        if bits >= depth // quarter:
+            continue
+        moves = []
+        for g in range(depth):
+            for j in range(lat):
+                up = parity(g ^ j) == 1
+                place = depth - 1 - g if up else g
+                deep = bits * quarter
+                ahead_of = place < (place ^ deep)
+                goal = (g ^ deep, j ^ parity(deep)) if ahead_of else (g, j ^ 1)
+                moves.append((g * lat + j, goal[0] * lat + goal[1]))
+        parts.append((bits, lax.ppermute(total, ("depth", "lat"), moves)))
+    order = [bits for bits, _ in parts]
+    coef = call(functools.partial(final_kernel, quarter, order), shape(nsrc, 2 * rank), *[part for _, part in parts], near, gap, entry)
     wide = shape(2 * nsrc, width)
     field = call(expand_kernel, wide, coef, left, local)
     field = pl.pallas_call(

time: 48.2 us -> 46.1 us (0.956)
  waiting for transfers between devices: 23.5 us -> 20 us
  starting transfers between devices: 14.6 us -> 16.1 us
    ppermute x9 -> x7, waiting for transfers between devices: 13.6 us -> 7.96 us  [swapped(): return lax.ppermute(value, ('depth', 'lat'), pairs)]
    ppermute x0 -> x3, starting transfers between devices: none -> 4.19 us  [body(): parts.append((bits, lax.ppermute(total, ('depth', 'lat'), moves)))]
    ppermute x9 -> x7, starting transfers between devices: 8.44 us -> 5.79 us  [swapped(): return lax.ppermute(value, ('depth', 'lat'), pairs)]
    ppermute x0 -> x3, waiting for transfers between devices: none -> 2.22 us  [body(): parts.append((bits, lax.ppermute(total, ('depth', 'lat'), moves)))]
    pallas_call x9 -> x7, Pallas kernels: 3.75 us -> 3.54 us  [call(): pl.pallas_call(kernel, out_shape=outs, in_specs=[SMEM] * scalars + [VMEM]...]
  transfers between devices with their start and end apart: 11 -> 12, of which waited for: 10 -> 10; matrix products, arithmetic and copies ran while one was open for 0% -> 0% of each run, Pallas kernels for 5% -> 5%
where the time goes in v6:
time: 46.1 us; the launch traced here: 45.8 us
  waiting for transfers between devices  20 us (43%)
  starting transfers between devices  16.1 us (35%)
  Pallas kernels  4.65 us (10%)
  local copies, waits for them, and re-layouts  4.19 us (9%)
  between operations  0.8 us (2%)
    ppermute x2, waiting for transfers between devices, shifted(): lax.ppermute(value, 'depth', [(k, (k + step) % depth) for k in range(dept...  9.85 us
    ppermute x7, waiting for transfers between devices, swapped(): return lax.ppermute(value, ('depth', 'lat'), pairs)  7.96 us
    ppermute x2, starting transfers between devices, shifted(): lax.ppermute(value, 'depth', [(k, (k + step) % depth) for k in range(dept...  6.15 us
    ppermute x7, starting transfers between devices, swapped(): return lax.ppermute(value, ('depth', 'lat'), pairs)  5.79 us
    ppermute x3, starting transfers between devices, body(): parts.append((bits, lax.ppermute(total, ('depth', 'lat'), moves)))  4.19 us
    unnamed x20, local copies, waits for them, and re-layouts  4.19 us
    pallas_call x7, Pallas kernels, call(): pl.pallas_call(kernel, out_shape=outs, in_specs=[SMEM] * scalars + [VMEM]...  3.54 us
    ppermute x3, waiting for transfers between devices, body(): parts.append((bits, lax.ppermute(total, ('depth', 'lat'), moves)))  2.22 us
  transfers between devices with their start and end apart: 12, of which 10 were waited for; matrix products, arithmetic and copies ran while one was open for 0% of the time, Pallas kernels for 5%

profile of v6, /device:TPU:0, one launch (start us, length us, event | category | flops | bytes accessed | tf_op | source)
XLA Modules:
  0.0 45.8 jit_solution(15862811575485999884)
XLA Ops:
  0.0 3.0 %collective-permute-start.3 = (f32[128,1024]{1,0:T(8,128)}, f32[128,1024]{1,0:T(8,128)S(1)}, u32[]{:S(2)}, u32[]{:S(2)}) collective-permute-start(f32[128,1024]{1,0:T(8,128)} %bitcast.13), channel_id=1, source_target_pairs={{0,4},{4,8},{8,12},{12,16},{16,20},{20,24},{24,28},{28,0},{1,5},{5... | collective-permute-start | bytes 1572872 | tf_op jit(solution)/shard_map/ppermute | solution.py:246
  3.1 3.1 %collective-permute-start = (f32[128,1024]{1,0:T(8,128)}, f32[128,1024]{1,0:T(8,128)S(1)}, u32[]{:S(2)}, u32[]{:S(2)}) collective-permute-start(f32[128,1024]{1,0:T(8,128)} %bitcast.15), channel_id=1, source_target_pairs={{0,28},{4,0},{8,4},{12,8},{16,12},{20,16},{24,20},{28,24},{1,29},{... | collective-permute-start | bytes 1572872 | tf_op jit(solution)/shard_map/ppermute | solution.py:246
  6.2 1.0 %copy-done.3 = f32[2,64,1024]{2,1,0:T(8,128)S(1)} copy-done((f32[2,64,1024]{2,1,0:T(8,128)S(1)}, f32[2,64,1024]{2,1,0:T(8,128)}, u32[]{:S(2)}) %copy-start.3) | copy-done | bytes 524312
  7.2 1.0 %copy-done.4 = f32[2,64,1024]{2,1,0:T(8,128)S(1)} copy-done((f32[2,64,1024]{2,1,0:T(8,128)S(1)}, f32[2,64,1024]{2,1,0:T(8,128)}, u32[]{:S(2)}) %copy-start.4) | copy-done | bytes 524312
  8.2 1.0 %copy-done.5 = f32[1,2,64,1024]{3,2,1,0:T(8,128)S(1)} copy-done((f32[1,2,64,1024]{3,2,1,0:T(8,128)S(1)}, f32[1,2,64,1024]{3,2,1,0:T(8,128)}, u32[]{:S(2)}) %copy-start.5) | copy-done | bytes 524312
  9.3 1.0 %copy-done.6 = f32[1,2,64,1024]{3,2,1,0:T(8,128)S(1)} copy-done((f32[1,2,64,1024]{3,2,1,0:T(8,128)S(1)}, f32[1,2,64,1024]{3,2,1,0:T(8,128)}, u32[]{:S(2)}) %copy-start.6) | copy-done | bytes 524312
  10.3 0.7 %shard_map.109 = f32[128,128]{1,0:T(8,128)S(1)} custom-call(f32[128,1024]{1,0:T(8,128)S(1)} %bitcast.16, f32[128,1024]{1,0:T(8,128)S(1)} %bitcast.14, f32[128,1024]{1,0:T(8,128)S(1)} %bitcast.11, f32[128,1024]{1,0:T(8,128)S(1)} %bitcast.12), custom_call_target="tpu_custom_call" | custom-call | tf_op jit(solution)/shard_map/pallas_call | solution.py:211
  11.0 0.1 collective-permute-start.1
  11.1 1.2 %collective-permute-done.1 = f32[128,128]{1,0:T(8,128)S(1)} collective-permute-done((f32[128,128]{1,0:T(8,128)S(1)}, f32[128,128]{1,0:T(8,128)S(1)}, u32[]{:S(2)}, u32[]{:S(2)}) %collective-permute-start.1) | collective-permute-done | bytes 65568 | tf_op jit(solution)/shard_map/ppermute | solution.py:250
  12.4 1.7 %collective-permute-start.2 = (f32[128,128]{1,0:T(8,128)S(1)}, f32[128,128]{1,0:T(8,128)S(1)}, u32[]{:S(2)}, u32[]{:S(2)}) collective-permute-start(f32[128,128]{1,0:T(8,128)S(1)} %add.9), channel_id=1, source_target_pairs={{0,2},{1,3},{2,0},{3,1},{4,6},{5,7},{6,4},{7,5},{8,10},{9,11},{10,... | collective-permute-start | bytes 196616 | tf_op jit(solution)/shard_map/ppermute | solution.py:250
  14.7 2.0 %collective-permute-done.2 = f32[128,128]{1,0:T(8,128)S(1)} collective-permute-done((f32[128,128]{1,0:T(8,128)S(1)}, f32[128,128]{1,0:T(8,128)S(1)}, u32[]{:S(2)}, u32[]{:S(2)}) %collective-permute-start.2) | collective-permute-done | bytes 65568 | tf_op jit(solution)/shard_map/ppermute | solution.py:250
  16.8 0.7 %shard_map.110 = (f32[128,1024]{1,0:T(8,128)S(1)}, bf16[2,2,256,1024]{3,2,1,0:T(8,128)(2,1)S(1)}) custom-call(s32[1]{0:T(128)S(6)} %copy.12.count_ref, s32[1,64]{1,0:T(1,128)S(1)} %copy-done.7, f32[128,1024]{1,0:T(8,128)S(1)} %bitcast.8, f32[128,1024]{1,0:T(8,128)S(1)} %bitcast.9, f32[128,1024]{1,0:T(8,128)S(1)} %bitcast.10, f32[1,64]{1,0:T(1,128)S(1)} %copy-done.8, ...), custom_call_target="tpu_custom_call" | custom-call | tf_op jit(solution)/shard_map/pallas_call | solution.py:211
  17.5 8.3 %collective-permute-done.3.proj_ref = f32[128,1024]{1,0:T(8,128)S(1)} collective-permute-done((f32[128,1024]{1,0:T(8,128)}, f32[128,1024]{1,0:T(8,128)S(1)}, u32[]{:S(2)}, u32[]{:S(2)}) %collective-permute-start.3) | collective-permute-done | bytes 524320 | tf_op jit(solution)/shard_map/ppermute | solution.py:246
  25.8 0.5 %shard_map.111.first_ref = f32[128,128]{1,0:T(8,128)S(1)} custom-call(f32[128,1024]{1,0:T(8,128)S(1)} %collective-permute-done.3.proj_ref, bf16[2,2,256,1024]{3,2,1,0:T(8,128)(2,1)S(1)} %get-tuple-element.11.left_ref), custom_call_target="tpu_custom_call" | custom-call | tf_op jit(solution)/shard_map/pallas_call | solution.py:211
  26.3 1.5 %collective-permute-done.proj_ref = f32[128,1024]{1,0:T(8,128)S(1)} collective-permute-done((f32[128,1024]{1,0:T(8,128)}, f32[128,1024]{1,0:T(8,128)S(1)}, u32[]{:S(2)}, u32[]{:S(2)}) %collective-permute-start) | collective-permute-done | bytes 524320 | tf_op jit(solution)/shard_map/ppermute | solution.py:246
  27.9 0.5 %shard_map.112 = (f32[128,128]{1,0:T(8,128)S(1)}, f32[128,128]{1,0:T(8,128)S(1)}) custom-call(f32[128,1024]{1,0:T(8,128)S(1)} %collective-permute-done.proj_ref, bf16[2,2,256,1024]{3,2,1,0:T(8,128)(2,1)S(1)} %get-tuple-element.11.left_ref, f32[128,128]{1,0:T(8,128)S(1)} %shard_map.111.first_ref), custom_call_target="tpu_custom_call" | custom-call | tf_op jit(solution)/shard_map/pallas_call | solution.py:211
  28.5 1.2 %collective-permute-done.4 = f32[128,128]{1,0:T(8,128)S(1)} collective-permute-done((f32[128,128]{1,0:T(8,128)S(1)}, f32[128,128]{1,0:T(8,128)S(1)}, u32[]{:S(2)}, u32[]{:S(2)}) %collective-permute-start.4) | collective-permute-done | bytes 65568 | tf_op jit(solution)/shard_map/ppermute | solution.py:250
  29.8 1.8 %collective-permute-start.5 = (f32[128,128]{1,0:T(8,128)S(1)}, f32[128,128]{1,0:T(8,128)S(1)}, u32[]{:S(2)}, u32[]{:S(2)}) collective-permute-start(f32[128,128]{1,0:T(8,128)S(1)} %add.11.refs_3_), channel_id=1, source_target_pairs={{0,6},{1,7},{2,4},{3,5},{4,2},{5,3},{6,0},{7,1},{8,14},{9,15},{10,... | collective-permute-start | bytes 196616 | tf_op jit(solution)/shard_map/ppermute | solution.py:250
  31.6 1.4 %collective-permute-start.7 = (f32[128,128]{1,0:T(8,128)S(1)}, f32[128,128]{1,0:T(8,128)S(1)}, u32[]{:S(2)}, u32[]{:S(2)}) collective-permute-start(f32[128,128]{1,0:T(8,128)S(1)} %add.11.refs_3_), channel_id=1, source_target_pairs={{0,5},{1,4},{2,7},{3,6},{4,1},{5,0},{6,3},{7,2},{8,13},{9,12},{10,... | collective-permute-start | bytes 196616 | tf_op jit(solution)/shard_map/ppermute | solution.py:250
  33.0 2.0 %collective-permute-done.5.refs_0_ = f32[128,128]{1,0:T(8,128)S(1)} collective-permute-done((f32[128,128]{1,0:T(8,128)S(1)}, f32[128,128]{1,0:T(8,128)S(1)}, u32[]{:S(2)}, u32[]{:S(2)}) %collective-permute-start.5) | collective-permute-done | bytes 65568 | tf_op jit(solution)/shard_map/ppermute | solution.py:250
  35.0 0.9 %collective-permute-done.6.refs_1_ = f32[128,128]{1,0:T(8,128)S(1)} collective-permute-done((f32[128,128]{1,0:T(8,128)S(1)}, f32[128,128]{1,0:T(8,128)S(1)}, u32[]{:S(2)}, u32[]{:S(2)}) %collective-permute-start.6) | collective-permute-done | bytes 65568 | tf_op jit(solution)/shard_map/ppermute | solution.py:250
  36.0 0.2 shard_map.113
  36.2 1.3 %collective-permute-start.10 = (f32[128,128]{1,0:T(8,128)S(1)}, f32[128,128]{1,0:T(8,128)S(1)}, u32[]{:S(2)}, u32[]{:S(2)}) collective-permute-start(f32[128,128]{1,0:T(8,128)S(1)} %get-tuple-element.14), channel_id=1, source_target_pairs={{0,9},{1,0},{2,3},{3,10},{4,5},{5,12},{6,15},{7,6},{8,1},{9,8},{10... | collective-permute-start | bytes 196616 | tf_op jit(solution)/shard_map/ppermute | solution.py:316
  37.6 2.6 %collective-permute-start.8 = (f32[128,128]{1,0:T(8,128)S(1)}, f32[128,128]{1,0:T(8,128)S(1)}, u32[]{:S(2)}, u32[]{:S(2)}) collective-permute-start(f32[128,128]{1,0:T(8,128)S(1)} %get-tuple-element.14), channel_id=1, source_target_pairs={{0,17},{1,0},{2,3},{3,18},{4,5},{5,20},{6,23},{7,6},{8,9},{9,24},{... | collective-permute-start | bytes 196616 | tf_op jit(solution)/shard_map/ppermute | solution.py:316
  40.1 0.3 collective-permute-start.9
  40.4 1.6 %collective-permute-done.8.refs_0_ = f32[128,128]{1,0:T(8,128)S(1)} collective-permute-done((f32[128,128]{1,0:T(8,128)S(1)}, f32[128,128]{1,0:T(8,128)S(1)}, u32[]{:S(2)}, u32[]{:S(2)}) %collective-permute-start.8) | collective-permute-done | bytes 65568 | tf_op jit(solution)/shard_map/ppermute | solution.py:316
  42.0 0.6 %collective-permute-done.9.refs_1_ = f32[128,128]{1,0:T(8,128)S(1)} collective-permute-done((f32[128,128]{1,0:T(8,128)S(1)}, f32[128,128]{1,0:T(8,128)S(1)}, u32[]{:S(2)}, u32[]{:S(2)}) %collective-permute-start.9) | collective-permute-done | bytes 65568 | tf_op jit(solution)/shard_map/ppermute | solution.py:316
  42.7 0.5 %shard_map.114.rows_ref = f32[64,128]{1,0:T(8,128)S(1)} custom-call(f32[128,128]{1,0:T(8,128)S(1)} %collective-permute-done.8.refs_0_, f32[128,128]{1,0:T(8,128)S(1)} %collective-permute-done.9.refs_1_, f32[128,128]{1,0:T(8,128)S(1)} %collective-permute-done.10.refs_2_, f32[128,128]{1,0:T(8,128)S(1)} %get-tuple-element.15.refs_3_.refs_4_, ...), custom_call_target="tpu_custom_call" | custom-call | tf_op jit(solution)/shard_map/pallas_call | solution.py:211
  43.1 0.7 %collective-permute-start.11 = (f32[64,128]{1,0:T(8,128)S(1)}, f32[64,128]{1,0:T(8,128)S(1)}, u32[]{:S(2)}, u32[]{:S(2)}) collective-permute-start(f32[64,128]{1,0:T(8,128)S(1)} %shard_map.114.rows_ref), channel_id=1, source_target_pairs={{0,1},{1,0},{2,3},{3,2},{4,5},{5,4},{6,7},{7,6},{8,9},{9,8},{10,11... | collective-permute-start | bytes 98312 | tf_op jit(solution)/shard_map/ppermute | solution.py:250
  43.9 0.3 shard_map.115.sum_ref
  44.2 0.5 %collective-permute-done.11.rows_ref = f32[64,128]{1,0:T(8,128)S(1)} collective-permute-done((f32[64,128]{1,0:T(8,128)S(1)}, f32[64,128]{1,0:T(8,128)S(1)}, u32[]{:S(2)}, u32[]{:S(2)}) %collective-permute-start.11) | collective-permute-done | bytes 32800 | tf_op jit(solution)/shard_map/ppermute | solution.py:250
  44.7 1.1 %shard_map.116 = f32[128,1024]{1,0:T(8,128)} custom-call(f32[64,128]{1,0:T(8,128)S(1)} %collective-permute-done.11.rows_ref, bf16[2,2,256,1024]{3,2,1,0:T(8,128)(2,1)S(1)} %get-tuple-element.11.left_ref, f32[128,1024]{1,0:T(8,128)S(1)} %shard_map.115.sum_ref), custom_call_target="tpu_custom_call" | custom-call | tf_op jit(solution)/shard_map/pallas_call | solution.py:321
  (23 shorter events, 0.2 us)
Async XLA Ops:
  0.0 16.7 %copy-start = (f32[1,2,64,1024]{3,2,1,0:T(8,128)S(1)}, f32[1,2,64,1024]{3,2,1,0:T(8,128)}, u32[]{:S(2)}) copy-start(f32[1,2,64,1024]{3,2,1,0:T(8,128)} %param.11) | copy-start | bytes 1572868
  0.0 16.7 %copy-start.1 = (f32[1,2,64,1024]{3,2,1,0:T(8,128)S(1)}, f32[1,2,64,1024]{3,2,1,0:T(8,128)}, u32[]{:S(2)}) copy-start(f32[1,2,64,1024]{3,2,1,0:T(8,128)} %param.12) | copy-start | bytes 1572868
  0.0 16.7 %copy-start.2 = (f32[1,2,64,1024]{3,2,1,0:T(8,128)S(1)}, f32[1,2,64,1024]{3,2,1,0:T(8,128)}, u32[]{:S(2)}) copy-start(f32[1,2,64,1024]{3,2,1,0:T(8,128)} %param.14) | copy-start | bytes 1572868
  0.0 25.8 %collective-permute-start.3 = (f32[128,1024]{1,0:T(8,128)}, f32[128,1024]{1,0:T(8,128)S(1)}, u32[]{:S(2)}, u32[]{:S(2)}) collective-permute-start(f32[128,1024]{1,0:T(8,128)} %bitcast.13), channel_id=1, source_target_pairs={{0,4},{4,8},{8,12},{12,16},{16,20},{20,24},{24,28},{28,0},{1,5},{5... | collective-permute-start | bytes 1572872 | tf_op jit(solution)/shard_map/ppermute | solution.py:246
  3.1 24.8 %collective-permute-start = (f32[128,1024]{1,0:T(8,128)}, f32[128,1024]{1,0:T(8,128)S(1)}, u32[]{:S(2)}, u32[]{:S(2)}) collective-permute-start(f32[128,1024]{1,0:T(8,128)} %bitcast.15), channel_id=1, source_target_pairs={{0,28},{4,0},{8,4},{12,8},{16,12},{20,16},{24,20},{28,24},{1,29},{... | collective-permute-start | bytes 1572872 | tf_op jit(solution)/shard_map/ppermute | solution.py:246
  6.2 1.0 %copy-start.3 = (f32[2,64,1024]{2,1,0:T(8,128)S(1)}, f32[2,64,1024]{2,1,0:T(8,128)}, u32[]{:S(2)}) copy-start(f32[2,64,1024]{2,1,0:T(8,128)} %param.20) | copy-start | bytes 1572868
  7.2 1.0 %copy-start.4 = (f32[2,64,1024]{2,1,0:T(8,128)S(1)}, f32[2,64,1024]{2,1,0:T(8,128)}, u32[]{:S(2)}) copy-start(f32[2,64,1024]{2,1,0:T(8,128)} %param.21) | copy-start | bytes 1572868
  8.2 1.0 %copy-start.5 = (f32[1,2,64,1024]{3,2,1,0:T(8,128)S(1)}, f32[1,2,64,1024]{3,2,1,0:T(8,128)}, u32[]{:S(2)}) copy-start(f32[1,2,64,1024]{3,2,1,0:T(8,128)} %param.15) | copy-start | bytes 1572868
  9.3 1.0 %copy-start.6 = (f32[1,2,64,1024]{3,2,1,0:T(8,128)S(1)}, f32[1,2,64,1024]{3,2,1,0:T(8,128)}, u32[]{:S(2)}) copy-start(f32[1,2,64,1024]{3,2,1,0:T(8,128)} %param.13) | copy-start | bytes 1572868
  10.3 6.4 %copy-start.7 = (s32[1,64]{1,0:T(1,128)S(1)}, s32[1,64]{1,0:T(1,128)}, u32[]{:S(2)}) copy-start(s32[1,64]{1,0:T(1,128)} %list_ref.1) | copy-start | bytes 772
  10.3 6.4 %copy-start.8 = (f32[1,64]{1,0:T(1,128)S(1)}, f32[1,64]{1,0:T(1,128)}, u32[]{:S(2)}) copy-start(f32[1,64]{1,0:T(1,128)} %dd_ref.1) | copy-start | bytes 772
  10.3 6.4 %copy-start.9 = (f32[1,64]{1,0:T(1,128)S(1)}, f32[1,64]{1,0:T(1,128)}, u32[]{:S(2)}) copy-start(f32[1,64]{1,0:T(1,128)} %ud_ref.1) | copy-start | bytes 772
  11.0 1.3 %collective-permute-start.1 = (f32[128,128]{1,0:T(8,128)S(1)}, f32[128,128]{1,0:T(8,128)S(1)}, u32[]{:S(2)}, u32[]{:S(2)}) collective-permute-start(f32[128,128]{1,0:T(8,128)S(1)} %shard_map.109), channel_id=1, source_target_pairs={{0,1},{1,0},{2,3},{3,2},{4,5},{5,4},{6,7},{7,6},{8,9},{9,8},{10,11... | collective-permute-start | bytes 196616 | tf_op jit(solution)/shard_map/ppermute | solution.py:250
  12.4 4.3 %collective-permute-start.2 = (f32[128,128]{1,0:T(8,128)S(1)}, f32[128,128]{1,0:T(8,128)S(1)}, u32[]{:S(2)}, u32[]{:S(2)}) collective-permute-start(f32[128,128]{1,0:T(8,128)S(1)} %add.9), channel_id=1, source_target_pairs={{0,2},{1,3},{2,0},{3,1},{4,6},{5,7},{6,4},{7,5},{8,10},{9,11},{10,... | collective-permute-start | bytes 196616 | tf_op jit(solution)/shard_map/ppermute | solution.py:250
  28.4 1.3 %collective-permute-start.4 = (f32[128,128]{1,0:T(8,128)S(1)}, f32[128,128]{1,0:T(8,128)S(1)}, u32[]{:S(2)}, u32[]{:S(2)}) collective-permute-start(f32[128,128]{1,0:T(8,128)S(1)} %get-tuple-element.13), channel_id=1, source_target_pairs={{0,1},{1,0},{2,3},{3,2},{4,5},{5,4},{6,7},{7,6},{8,9},{9,8},{10,11... | collective-permute-start | bytes 196616 | tf_op jit(solution)/shard_map/ppermute | solution.py:250
  29.8 5.3 %collective-permute-start.5 = (f32[128,128]{1,0:T(8,128)S(1)}, f32[128,128]{1,0:T(8,128)S(1)}, u32[]{:S(2)}, u32[]{:S(2)}) collective-permute-start(f32[128,128]{1,0:T(8,128)S(1)} %add.11.refs_3_), channel_id=1, source_target_pairs={{0,6},{1,7},{2,4},{3,5},{4,2},{5,3},{6,0},{7,1},{8,14},{9,15},{10,... | collective-permute-start | bytes 196616 | tf_op jit(solution)/shard_map/ppermute | solution.py:250
  31.6 4.3 %collective-permute-start.6 = (f32[128,128]{1,0:T(8,128)S(1)}, f32[128,128]{1,0:T(8,128)S(1)}, u32[]{:S(2)}, u32[]{:S(2)}) collective-permute-start(f32[128,128]{1,0:T(8,128)S(1)} %add.11.refs_3_), channel_id=1, source_target_pairs={{0,3},{1,2},{2,1},{3,0},{4,7},{5,6},{6,5},{7,4},{8,11},{9,10},{10,... | collective-permute-start | bytes 196616 | tf_op jit(solution)/shard_map/ppermute | solution.py:250
  31.6 4.4 %collective-permute-start.7 = (f32[128,128]{1,0:T(8,128)S(1)}, f32[128,128]{1,0:T(8,128)S(1)}, u32[]{:S(2)}, u32[]{:S(2)}) collective-permute-start(f32[128,128]{1,0:T(8,128)S(1)} %add.11.refs_3_), channel_id=1, source_target_pairs={{0,5},{1,4},{2,7},{3,6},{4,1},{5,0},{6,3},{7,2},{8,13},{9,12},{10,... | collective-permute-start | bytes 196616 | tf_op jit(solution)/shard_map/ppermute | solution.py:250
  36.2 4.2 %collective-permute-start.10 = (f32[128,128]{1,0:T(8,128)S(1)}, f32[128,128]{1,0:T(8,128)S(1)}, u32[]{:S(2)}, u32[]{:S(2)}) collective-permute-start(f32[128,128]{1,0:T(8,128)S(1)} %get-tuple-element.14), channel_id=1, source_target_pairs={{0,9},{1,0},{2,3},{3,10},{4,5},{5,12},{6,15},{7,6},{8,1},{9,8},{10... | collective-permute-start | bytes 196616 | tf_op jit(solution)/shard_map/ppermute | solution.py:316
  37.6 4.5 %collective-permute-start.8 = (f32[128,128]{1,0:T(8,128)S(1)}, f32[128,128]{1,0:T(8,128)S(1)}, u32[]{:S(2)}, u32[]{:S(2)}) collective-permute-start(f32[128,128]{1,0:T(8,128)S(1)} %get-tuple-element.14), channel_id=1, source_target_pairs={{0,17},{1,0},{2,3},{3,18},{4,5},{5,20},{6,23},{7,6},{8,9},{9,24},{... | collective-permute-start | bytes 196616 | tf_op jit(solution)/shard_map/ppermute | solution.py:316
  40.1 2.5 %collective-permute-start.9 = (f32[128,128]{1,0:T(8,128)S(1)}, f32[128,128]{1,0:T(8,128)S(1)}, u32[]{:S(2)}, u32[]{:S(2)}) collective-permute-start(f32[128,128]{1,0:T(8,128)S(1)} %get-tuple-element.14), channel_id=1, source_target_pairs={{0,24},{1,0},{2,3},{3,27},{4,5},{5,29},{6,30},{7,6},{8,9},{9,17},{... | collective-permute-start | bytes 196616 | tf_op jit(solution)/shard_map/ppermute | solution.py:316
  43.1 1.6 %collective-permute-start.11 = (f32[64,128]{1,0:T(8,128)S(1)}, f32[64,128]{1,0:T(8,128)S(1)}, u32[]{:S(2)}, u32[]{:S(2)}) collective-permute-start(f32[64,128]{1,0:T(8,128)S(1)} %shard_map.114.rows_ref), channel_id=1, source_target_pairs={{0,1},{1,0},{2,3},{3,2},{4,5},{5,4},{6,7},{7,6},{8,9},{9,8},{10,11... | collective-permute-start | bytes 98312 | tf_op jit(solution)/shard_map/ppermute | solution.py:250

commit v7 on v6

--- a/solution.py
+++ b/solution.py
@@ -127,10 +127,11 @@
     give_ref[...] = jnp.where(ours, up, down)
 
 
-def pair_kernel(count, *refs):
+def pair_kernel(*refs):
     parts, (near_ref, out_ref) = refs[:-2], refs[-2:]
-    other = parts[0][...] + parts[2][...]
-    own = parts[3][...] + parts[1][...]
+    other, own = parts[0][...], parts[1][...]
+    for other_ref, own_ref in zip(parts[2::2], parts[3::2]):
+        other, own = other + other_ref[...], own + own_ref[...]
     first = lax.rem(standing()[1], 2) == 0
     near = jnp.where(first, own, other)
     near_ref[...] = near
@@ -290,8 +291,13 @@
     while bit < lat:
         own = own + met(own, 0, bit)
         bit *= 2
-    m = dict(xy=met(own, 1, 2), x=met(own, 0, 2), y=met(own, 1, 0), o=own)
-    near, total = call(functools.partial(pair_kernel, 2), (element, element), *[m[k] for k in ['xy', 'x', 'y', 'o']])
+    if lat > 2:
+        others, owns = [met(own, 1, 2)], [met(own, 0, 2), own]
+        others.append(met(own, 1, 0))
+        parts = [others[0], owns[0], others[1], owns[1]]
+    else:
+        parts = [met(own, 1, 0), own]
+    near, total = call(pair_kernel, (element, element), *parts)
     gap = near
     quarter = max(depth // 4, 2)
     reach = 2

time: 46.1 us -> 46.1 us (level)
  no operation moved by 1% of the time
where the time goes in v7:
time: 46.1 us; the launch traced here: 45.8 us
  waiting for transfers between devices  20 us (43%)
  starting transfers between devices  16.1 us (35%)
  Pallas kernels  4.65 us (10%)
  local copies, waits for them, and re-layouts  4.19 us (9%)
  between operations  0.8 us (2%)
    ppermute x2, waiting for transfers between devices, shifted(): lax.ppermute(value, 'depth', [(k, (k + step) % depth) for k in range(dept...  9.85 us
    ppermute x7, waiting for transfers between devices, swapped(): return lax.ppermute(value, ('depth', 'lat'), pairs)  7.96 us
    ppermute x2, starting transfers between devices, shifted(): lax.ppermute(value, 'depth', [(k, (k + step) % depth) for k in range(dept...  6.15 us
    ppermute x7, starting transfers between devices, swapped(): return lax.ppermute(value, ('depth', 'lat'), pairs)  5.79 us
    ppermute x3, starting transfers between devices, body(): parts.append((bits, lax.ppermute(total, ('depth', 'lat'), moves)))  4.19 us
    unnamed x20, local copies, waits for them, and re-layouts  4.19 us
    pallas_call x7, Pallas kernels, call(): pl.pallas_call(kernel, out_shape=outs, in_specs=[SMEM] * scalars + [VMEM]...  3.54 us
    ppermute x3, waiting for transfers between devices, body(): parts.append((bits, lax.ppermute(total, ('depth', 'lat'), moves)))  2.22 us
  transfers between devices with their start and end apart: 12, of which 10 were waited for; matrix products, arithmetic and copies ran while one was open for 0% of the time, Pallas kernels for 5%

profile of v7, /device:TPU:0, one launch (start us, length us, event | category | flops | bytes accessed | tf_op | source)
XLA Modules:
  0.0 45.8 jit_solution(16231879526180573888)
XLA Ops:
  0.0 3.0 %collective-permute-start.3 = (f32[128,1024]{1,0:T(8,128)}, f32[128,1024]{1,0:T(8,128)S(1)}, u32[]{:S(2)}, u32[]{:S(2)}) collective-permute-start(f32[128,1024]{1,0:T(8,128)} %bitcast.13), channel_id=1, source_target_pairs={{0,4},{4,8},{8,12},{12,16},{16,20},{20,24},{24,28},{28,0},{1,5},{5... | collective-permute-start | bytes 1572872 | tf_op jit(solution)/shard_map/ppermute | solution.py:247
  3.1 3.1 %collective-permute-start = (f32[128,1024]{1,0:T(8,128)}, f32[128,1024]{1,0:T(8,128)S(1)}, u32[]{:S(2)}, u32[]{:S(2)}) collective-permute-start(f32[128,1024]{1,0:T(8,128)} %bitcast.15), channel_id=1, source_target_pairs={{0,28},{4,0},{8,4},{12,8},{16,12},{20,16},{24,20},{28,24},{1,29},{... | collective-permute-start | bytes 1572872 | tf_op jit(solution)/shard_map/ppermute | solution.py:247
  6.2 1.0 %copy-done.3 = f32[2,64,1024]{2,1,0:T(8,128)S(1)} copy-done((f32[2,64,1024]{2,1,0:T(8,128)S(1)}, f32[2,64,1024]{2,1,0:T(8,128)}, u32[]{:S(2)}) %copy-start.3) | copy-done | bytes 524312
  7.2 1.0 %copy-done.4 = f32[2,64,1024]{2,1,0:T(8,128)S(1)} copy-done((f32[2,64,1024]{2,1,0:T(8,128)S(1)}, f32[2,64,1024]{2,1,0:T(8,128)}, u32[]{:S(2)}) %copy-start.4) | copy-done | bytes 524312
  8.2 1.0 %copy-done.5 = f32[1,2,64,1024]{3,2,1,0:T(8,128)S(1)} copy-done((f32[1,2,64,1024]{3,2,1,0:T(8,128)S(1)}, f32[1,2,64,1024]{3,2,1,0:T(8,128)}, u32[]{:S(2)}) %copy-start.5) | copy-done | bytes 524312
  9.3 1.0 %copy-done.6 = f32[1,2,64,1024]{3,2,1,0:T(8,128)S(1)} copy-done((f32[1,2,64,1024]{3,2,1,0:T(8,128)S(1)}, f32[1,2,64,1024]{3,2,1,0:T(8,128)}, u32[]{:S(2)}) %copy-start.6) | copy-done | bytes 524312
  10.3 0.7 %shard_map.109 = f32[128,128]{1,0:T(8,128)S(1)} custom-call(f32[128,1024]{1,0:T(8,128)S(1)} %bitcast.16, f32[128,1024]{1,0:T(8,128)S(1)} %bitcast.14, f32[128,1024]{1,0:T(8,128)S(1)} %bitcast.11, f32[128,1024]{1,0:T(8,128)S(1)} %bitcast.12), custom_call_target="tpu_custom_call" | custom-call | tf_op jit(solution)/shard_map/pallas_call | solution.py:212
  11.0 0.1 collective-permute-start.1
  11.1 1.2 %collective-permute-done.1 = f32[128,128]{1,0:T(8,128)S(1)} collective-permute-done((f32[128,128]{1,0:T(8,128)S(1)}, f32[128,128]{1,0:T(8,128)S(1)}, u32[]{:S(2)}, u32[]{:S(2)}) %collective-permute-start.1) | collective-permute-done | bytes 65568 | tf_op jit(solution)/shard_map/ppermute | solution.py:251
  12.4 1.7 %collective-permute-start.2 = (f32[128,128]{1,0:T(8,128)S(1)}, f32[128,128]{1,0:T(8,128)S(1)}, u32[]{:S(2)}, u32[]{:S(2)}) collective-permute-start(f32[128,128]{1,0:T(8,128)S(1)} %add.9), channel_id=1, source_target_pairs={{0,2},{1,3},{2,0},{3,1},{4,6},{5,7},{6,4},{7,5},{8,10},{9,11},{10,... | collective-permute-start | bytes 196616 | tf_op jit(solution)/shard_map/ppermute | solution.py:251
  14.7 2.0 %collective-permute-done.2 = f32[128,128]{1,0:T(8,128)S(1)} collective-permute-done((f32[128,128]{1,0:T(8,128)S(1)}, f32[128,128]{1,0:T(8,128)S(1)}, u32[]{:S(2)}, u32[]{:S(2)}) %collective-permute-start.2) | collective-permute-done | bytes 65568 | tf_op jit(solution)/shard_map/ppermute | solution.py:251
  16.8 0.7 %shard_map.110 = (f32[128,1024]{1,0:T(8,128)S(1)}, bf16[2,2,256,1024]{3,2,1,0:T(8,128)(2,1)S(1)}) custom-call(s32[1]{0:T(128)S(6)} %copy.12.count_ref, s32[1,64]{1,0:T(1,128)S(1)} %copy-done.7, f32[128,1024]{1,0:T(8,128)S(1)} %bitcast.8, f32[128,1024]{1,0:T(8,128)S(1)} %bitcast.9, f32[128,1024]{1,0:T(8,128)S(1)} %bitcast.10, f32[1,64]{1,0:T(1,128)S(1)} %copy-done.8, ...), custom_call_target="tpu_custom_call" | custom-call | tf_op jit(solution)/shard_map/pallas_call | solution.py:212
  17.5 8.3 %collective-permute-done.3.proj_ref = f32[128,1024]{1,0:T(8,128)S(1)} collective-permute-done((f32[128,1024]{1,0:T(8,128)}, f32[128,1024]{1,0:T(8,128)S(1)}, u32[]{:S(2)}, u32[]{:S(2)}) %collective-permute-start.3) | collective-permute-done | bytes 524320 | tf_op jit(solution)/shard_map/ppermute | solution.py:247
  25.8 0.5 %shard_map.111.first_ref = f32[128,128]{1,0:T(8,128)S(1)} custom-call(f32[128,1024]{1,0:T(8,128)S(1)} %collective-permute-done.3.proj_ref, bf16[2,2,256,1024]{3,2,1,0:T(8,128)(2,1)S(1)} %get-tuple-element.11.left_ref), custom_call_target="tpu_custom_call" | custom-call | tf_op jit(solution)/shard_map/pallas_call | solution.py:212
  26.3 1.5 %collective-permute-done.proj_ref = f32[128,1024]{1,0:T(8,128)S(1)} collective-permute-done((f32[128,1024]{1,0:T(8,128)}, f32[128,1024]{1,0:T(8,128)S(1)}, u32[]{:S(2)}, u32[]{:S(2)}) %collective-permute-start) | collective-permute-done | bytes 524320 | tf_op jit(solution)/shard_map/ppermute | solution.py:247
  27.9 0.5 %shard_map.112 = (f32[128,128]{1,0:T(8,128)S(1)}, f32[128,128]{1,0:T(8,128)S(1)}) custom-call(f32[128,1024]{1,0:T(8,128)S(1)} %collective-permute-done.proj_ref, bf16[2,2,256,1024]{3,2,1,0:T(8,128)(2,1)S(1)} %get-tuple-element.11.left_ref, f32[128,128]{1,0:T(8,128)S(1)} %shard_map.111.first_ref), custom_call_target="tpu_custom_call" | custom-call | tf_op jit(solution)/shard_map/pallas_call | solution.py:212
  28.5 1.2 %collective-permute-done.4 = f32[128,128]{1,0:T(8,128)S(1)} collective-permute-done((f32[128,128]{1,0:T(8,128)S(1)}, f32[128,128]{1,0:T(8,128)S(1)}, u32[]{:S(2)}, u32[]{:S(2)}) %collective-permute-start.4) | collective-permute-done | bytes 65568 | tf_op jit(solution)/shard_map/ppermute | solution.py:251
  29.8 1.8 %collective-permute-start.5 = (f32[128,128]{1,0:T(8,128)S(1)}, f32[128,128]{1,0:T(8,128)S(1)}, u32[]{:S(2)}, u32[]{:S(2)}) collective-permute-start(f32[128,128]{1,0:T(8,128)S(1)} %add.11.refs_3_), channel_id=1, source_target_pairs={{0,6},{1,7},{2,4},{3,5},{4,2},{5,3},{6,0},{7,1},{8,14},{9,15},{10,... | collective-permute-start | bytes 196616 | tf_op jit(solution)/shard_map/ppermute | solution.py:251
  31.6 1.4 %collective-permute-start.7 = (f32[128,128]{1,0:T(8,128)S(1)}, f32[128,128]{1,0:T(8,128)S(1)}, u32[]{:S(2)}, u32[]{:S(2)}) collective-permute-start(f32[128,128]{1,0:T(8,128)S(1)} %add.11.refs_3_), channel_id=1, source_target_pairs={{0,5},{1,4},{2,7},{3,6},{4,1},{5,0},{6,3},{7,2},{8,13},{9,12},{10,... | collective-permute-start | bytes 196616 | tf_op jit(solution)/shard_map/ppermute | solution.py:251
  33.0 2.0 %collective-permute-done.5.refs_0_ = f32[128,128]{1,0:T(8,128)S(1)} collective-permute-done((f32[128,128]{1,0:T(8,128)S(1)}, f32[128,128]{1,0:T(8,128)S(1)}, u32[]{:S(2)}, u32[]{:S(2)}) %collective-permute-start.5) | collective-permute-done | bytes 65568 | tf_op jit(solution)/shard_map/ppermute | solution.py:251
  35.0 0.9 %collective-permute-done.6.refs_1_ = f32[128,128]{1,0:T(8,128)S(1)} collective-permute-done((f32[128,128]{1,0:T(8,128)S(1)}, f32[128,128]{1,0:T(8,128)S(1)}, u32[]{:S(2)}, u32[]{:S(2)}) %collective-permute-start.6) | collective-permute-done | bytes 65568 | tf_op jit(solution)/shard_map/ppermute | solution.py:251
  36.0 0.2 shard_map.113
  36.2 1.3 %collective-permute-start.10 = (f32[128,128]{1,0:T(8,128)S(1)}, f32[128,128]{1,0:T(8,128)S(1)}, u32[]{:S(2)}, u32[]{:S(2)}) collective-permute-start(f32[128,128]{1,0:T(8,128)S(1)} %get-tuple-element.14), channel_id=1, source_target_pairs={{0,9},{1,0},{2,3},{3,10},{4,5},{5,12},{6,15},{7,6},{8,1},{9,8},{10... | collective-permute-start | bytes 196616 | tf_op jit(solution)/shard_map/ppermute | solution.py:322
  37.6 2.6 %collective-permute-start.8 = (f32[128,128]{1,0:T(8,128)S(1)}, f32[128,128]{1,0:T(8,128)S(1)}, u32[]{:S(2)}, u32[]{:S(2)}) collective-permute-start(f32[128,128]{1,0:T(8,128)S(1)} %get-tuple-element.14), channel_id=1, source_target_pairs={{0,17},{1,0},{2,3},{3,18},{4,5},{5,20},{6,23},{7,6},{8,9},{9,24},{... | collective-permute-start | bytes 196616 | tf_op jit(solution)/shard_map/ppermute | solution.py:322
  40.1 0.3 collective-permute-start.9
  40.4 1.6 %collective-permute-done.8.refs_0_ = f32[128,128]{1,0:T(8,128)S(1)} collective-permute-done((f32[128,128]{1,0:T(8,128)S(1)}, f32[128,128]{1,0:T(8,128)S(1)}, u32[]{:S(2)}, u32[]{:S(2)}) %collective-permute-start.8) | collective-permute-done | bytes 65568 | tf_op jit(solution)/shard_map/ppermute | solution.py:322
  42.0 0.6 %collective-permute-done.9.refs_1_ = f32[128,128]{1,0:T(8,128)S(1)} collective-permute-done((f32[128,128]{1,0:T(8,128)S(1)}, f32[128,128]{1,0:T(8,128)S(1)}, u32[]{:S(2)}, u32[]{:S(2)}) %collective-permute-start.9) | collective-permute-done | bytes 65568 | tf_op jit(solution)/shard_map/ppermute | solution.py:322
  42.7 0.5 %shard_map.114.rows_ref = f32[64,128]{1,0:T(8,128)S(1)} custom-call(f32[128,128]{1,0:T(8,128)S(1)} %collective-permute-done.8.refs_0_, f32[128,128]{1,0:T(8,128)S(1)} %collective-permute-done.9.refs_1_, f32[128,128]{1,0:T(8,128)S(1)} %collective-permute-done.10.refs_2_, f32[128,128]{1,0:T(8,128)S(1)} %get-tuple-element.15.refs_3_.refs_4_, ...), custom_call_target="tpu_custom_call" | custom-call | tf_op jit(solution)/shard_map/pallas_call | solution.py:212
  43.1 0.7 %collective-permute-start.11 = (f32[64,128]{1,0:T(8,128)S(1)}, f32[64,128]{1,0:T(8,128)S(1)}, u32[]{:S(2)}, u32[]{:S(2)}) collective-permute-start(f32[64,128]{1,0:T(8,128)S(1)} %shard_map.114.rows_ref), channel_id=1, source_target_pairs={{0,1},{1,0},{2,3},{3,2},{4,5},{5,4},{6,7},{7,6},{8,9},{9,8},{10,11... | collective-permute-start | bytes 98312 | tf_op jit(solution)/shard_map/ppermute | solution.py:251
  43.9 0.3 shard_map.115.sum_ref
  44.2 0.5 %collective-permute-done.11.rows_ref = f32[64,128]{1,0:T(8,128)S(1)} collective-permute-done((f32[64,128]{1,0:T(8,128)S(1)}, f32[64,128]{1,0:T(8,128)S(1)}, u32[]{:S(2)}, u32[]{:S(2)}) %collective-permute-start.11) | collective-permute-done | bytes 32800 | tf_op jit(solution)/shard_map/ppermute | solution.py:251
  44.7 1.1 %shard_map.116 = f32[128,1024]{1,0:T(8,128)} custom-call(f32[64,128]{1,0:T(8,128)S(1)} %collective-permute-done.11.rows_ref, bf16[2,2,256,1024]{3,2,1,0:T(8,128)(2,1)S(1)} %get-tuple-element.11.left_ref, f32[128,1024]{1,0:T(8,128)S(1)} %shard_map.115.sum_ref), custom_call_target="tpu_custom_call" | custom-call | tf_op jit(solution)/shard_map/pallas_call | solution.py:327
  (23 shorter events, 0.2 us)
Async XLA Ops:
  0.0 16.7 %copy-start = (f32[1,2,64,1024]{3,2,1,0:T(8,128)S(1)}, f32[1,2,64,1024]{3,2,1,0:T(8,128)}, u32[]{:S(2)}) copy-start(f32[1,2,64,1024]{3,2,1,0:T(8,128)} %param.11) | copy-start | bytes 1572868
  0.0 16.7 %copy-start.1 = (f32[1,2,64,1024]{3,2,1,0:T(8,128)S(1)}, f32[1,2,64,1024]{3,2,1,0:T(8,128)}, u32[]{:S(2)}) copy-start(f32[1,2,64,1024]{3,2,1,0:T(8,128)} %param.12) | copy-start | bytes 1572868
  0.0 16.7 %copy-start.2 = (f32[1,2,64,1024]{3,2,1,0:T(8,128)S(1)}, f32[1,2,64,1024]{3,2,1,0:T(8,128)}, u32[]{:S(2)}) copy-start(f32[1,2,64,1024]{3,2,1,0:T(8,128)} %param.14) | copy-start | bytes 1572868
  0.0 25.8 %collective-permute-start.3 = (f32[128,1024]{1,0:T(8,128)}, f32[128,1024]{1,0:T(8,128)S(1)}, u32[]{:S(2)}, u32[]{:S(2)}) collective-permute-start(f32[128,1024]{1,0:T(8,128)} %bitcast.13), channel_id=1, source_target_pairs={{0,4},{4,8},{8,12},{12,16},{16,20},{20,24},{24,28},{28,0},{1,5},{5... | collective-permute-start | bytes 1572872 | tf_op jit(solution)/shard_map/ppermute | solution.py:247
  3.1 24.8 %collective-permute-start = (f32[128,1024]{1,0:T(8,128)}, f32[128,1024]{1,0:T(8,128)S(1)}, u32[]{:S(2)}, u32[]{:S(2)}) collective-permute-start(f32[128,1024]{1,0:T(8,128)} %bitcast.15), channel_id=1, source_target_pairs={{0,28},{4,0},{8,4},{12,8},{16,12},{20,16},{24,20},{28,24},{1,29},{... | collective-permute-start | bytes 1572872 | tf_op jit(solution)/shard_map/ppermute | solution.py:247
  6.2 1.0 %copy-start.3 = (f32[2,64,1024]{2,1,0:T(8,128)S(1)}, f32[2,64,1024]{2,1,0:T(8,128)}, u32[]{:S(2)}) copy-start(f32[2,64,1024]{2,1,0:T(8,128)} %param.20) | copy-start | bytes 1572868
  7.2 1.0 %copy-start.4 = (f32[2,64,1024]{2,1,0:T(8,128)S(1)}, f32[2,64,1024]{2,1,0:T(8,128)}, u32[]{:S(2)}) copy-start(f32[2,64,1024]{2,1,0:T(8,128)} %param.21) | copy-start | bytes 1572868
  8.2 1.0 %copy-start.5 = (f32[1,2,64,1024]{3,2,1,0:T(8,128)S(1)}, f32[1,2,64,1024]{3,2,1,0:T(8,128)}, u32[]{:S(2)}) copy-start(f32[1,2,64,1024]{3,2,1,0:T(8,128)} %param.15) | copy-start | bytes 1572868
  9.3 1.0 %copy-start.6 = (f32[1,2,64,1024]{3,2,1,0:T(8,128)S(1)}, f32[1,2,64,1024]{3,2,1,0:T(8,128)}, u32[]{:S(2)}) copy-start(f32[1,2,64,1024]{3,2,1,0:T(8,128)} %param.13) | copy-start | bytes 1572868
  10.3 6.4 %copy-start.7 = (s32[1,64]{1,0:T(1,128)S(1)}, s32[1,64]{1,0:T(1,128)}, u32[]{:S(2)}) copy-start(s32[1,64]{1,0:T(1,128)} %list_ref.1) | copy-start | bytes 772
  10.3 6.4 %copy-start.8 = (f32[1,64]{1,0:T(1,128)S(1)}, f32[1,64]{1,0:T(1,128)}, u32[]{:S(2)}) copy-start(f32[1,64]{1,0:T(1,128)} %dd_ref.1) | copy-start | bytes 772
  10.3 6.4 %copy-start.9 = (f32[1,64]{1,0:T(1,128)S(1)}, f32[1,64]{1,0:T(1,128)}, u32[]{:S(2)}) copy-start(f32[1,64]{1,0:T(1,128)} %ud_ref.1) | copy-start | bytes 772
  11.0 1.3 %collective-permute-start.1 = (f32[128,128]{1,0:T(8,128)S(1)}, f32[128,128]{1,0:T(8,128)S(1)}, u32[]{:S(2)}, u32[]{:S(2)}) collective-permute-start(f32[128,128]{1,0:T(8,128)S(1)} %shard_map.109), channel_id=1, source_target_pairs={{0,1},{1,0},{2,3},{3,2},{4,5},{5,4},{6,7},{7,6},{8,9},{9,8},{10,11... | collective-permute-start | bytes 196616 | tf_op jit(solution)/shard_map/ppermute | solution.py:251
  12.4 4.3 %collective-permute-start.2 = (f32[128,128]{1,0:T(8,128)S(1)}, f32[128,128]{1,0:T(8,128)S(1)}, u32[]{:S(2)}, u32[]{:S(2)}) collective-permute-start(f32[128,128]{1,0:T(8,128)S(1)} %add.9), channel_id=1, source_target_pairs={{0,2},{1,3},{2,0},{3,1},{4,6},{5,7},{6,4},{7,5},{8,10},{9,11},{10,... | collective-permute-start | bytes 196616 | tf_op jit(solution)/shard_map/ppermute | solution.py:251
  28.4 1.3 %collective-permute-start.4 = (f32[128,128]{1,0:T(8,128)S(1)}, f32[128,128]{1,0:T(8,128)S(1)}, u32[]{:S(2)}, u32[]{:S(2)}) collective-permute-start(f32[128,128]{1,0:T(8,128)S(1)} %get-tuple-element.13), channel_id=1, source_target_pairs={{0,1},{1,0},{2,3},{3,2},{4,5},{5,4},{6,7},{7,6},{8,9},{9,8},{10,11... | collective-permute-start | bytes 196616 | tf_op jit(solution)/shard_map/ppermute | solution.py:251
  29.8 5.3 %collective-permute-start.5 = (f32[128,128]{1,0:T(8,128)S(1)}, f32[128,128]{1,0:T(8,128)S(1)}, u32[]{:S(2)}, u32[]{:S(2)}) collective-permute-start(f32[128,128]{1,0:T(8,128)S(1)} %add.11.refs_3_), channel_id=1, source_target_pairs={{0,6},{1,7},{2,4},{3,5},{4,2},{5,3},{6,0},{7,1},{8,14},{9,15},{10,... | collective-permute-start | bytes 196616 | tf_op jit(solution)/shard_map/ppermute | solution.py:251
  31.6 4.3 %collective-permute-start.6 = (f32[128,128]{1,0:T(8,128)S(1)}, f32[128,128]{1,0:T(8,128)S(1)}, u32[]{:S(2)}, u32[]{:S(2)}) collective-permute-start(f32[128,128]{1,0:T(8,128)S(1)} %add.11.refs_3_), channel_id=1, source_target_pairs={{0,3},{1,2},{2,1},{3,0},{4,7},{5,6},{6,5},{7,4},{8,11},{9,10},{10,... | collective-permute-start | bytes 196616 | tf_op jit(solution)/shard_map/ppermute | solution.py:251
  31.6 4.4 %collective-permute-start.7 = (f32[128,128]{1,0:T(8,128)S(1)}, f32[128,128]{1,0:T(8,128)S(1)}, u32[]{:S(2)}, u32[]{:S(2)}) collective-permute-start(f32[128,128]{1,0:T(8,128)S(1)} %add.11.refs_3_), channel_id=1, source_target_pairs={{0,5},{1,4},{2,7},{3,6},{4,1},{5,0},{6,3},{7,2},{8,13},{9,12},{10,... | collective-permute-start | bytes 196616 | tf_op jit(solution)/shard_map/ppermute | solution.py:251
  36.2 4.2 %collective-permute-start.10 = (f32[128,128]{1,0:T(8,128)S(1)}, f32[128,128]{1,0:T(8,128)S(1)}, u32[]{:S(2)}, u32[]{:S(2)}) collective-permute-start(f32[128,128]{1,0:T(8,128)S(1)} %get-tuple-element.14), channel_id=1, source_target_pairs={{0,9},{1,0},{2,3},{3,10},{4,5},{5,12},{6,15},{7,6},{8,1},{9,8},{10... | collective-permute-start | bytes 196616 | tf_op jit(solution)/shard_map/ppermute | solution.py:322
  37.6 4.5 %collective-permute-start.8 = (f32[128,128]{1,0:T(8,128)S(1)}, f32[128,128]{1,0:T(8,128)S(1)}, u32[]{:S(2)}, u32[]{:S(2)}) collective-permute-start(f32[128,128]{1,0:T(8,128)S(1)} %get-tuple-element.14), channel_id=1, source_target_pairs={{0,17},{1,0},{2,3},{3,18},{4,5},{5,20},{6,23},{7,6},{8,9},{9,24},{... | collective-permute-start | bytes 196616 | tf_op jit(solution)/shard_map/ppermute | solution.py:322
  40.1 2.5 %collective-permute-start.9 = (f32[128,128]{1,0:T(8,128)S(1)}, f32[128,128]{1,0:T(8,128)S(1)}, u32[]{:S(2)}, u32[]{:S(2)}) collective-permute-start(f32[128,128]{1,0:T(8,128)S(1)} %get-tuple-element.14), channel_id=1, source_target_pairs={{0,24},{1,0},{2,3},{3,27},{4,5},{5,29},{6,30},{7,6},{8,9},{9,17},{... | collective-permute-start | bytes 196616 | tf_op jit(solution)/shard_map/ppermute | solution.py:322
  43.1 1.6 %collective-permute-start.11 = (f32[64,128]{1,0:T(8,128)S(1)}, f32[64,128]{1,0:T(8,128)S(1)}, u32[]{:S(2)}, u32[]{:S(2)}) collective-permute-start(f32[64,128]{1,0:T(8,128)S(1)} %shard_map.114.rows_ref), channel_id=1, source_target_pairs={{0,1},{1,0},{2,3},{3,2},{4,5},{5,4},{6,7},{7,6},{8,9},{9,8},{10,11... | collective-permute-start | bytes 98312 | tf_op jit(solution)/shard_map/ppermute | solution.py:251
